TPU v7x, 32 devices: a whole 2x2x4 slice. The times are simulated.
32 devices in a mesh: blk: 8 (over z, x), dp: 4 (over y, core).
Axes of the slice: x: 2, y: 2, z: 4, core: 2. Of those that a mesh axis runs over, the one named last changes fastest.
Arguments:
- x_rows: bfloat16 [8192, 2048], P('blk'), may hold values from -6 to 6
- grad_rows: bfloat16 [8192, 2048], P('blk'), may hold values from -3 to 3
- w_gate_up: bfloat16 [8, 2, 768, 2048], P('blk', None, 'dp'), may hold values from -0.125 to 0.125
- w_down: bfloat16 [8, 768, 2048], P('blk', 'dp'), may hold values from -0.21875 to 0.21875
- counts: int32 [8, 5], replicated, may hold values from 1 to 384, as said below
Outputs:
- grad_gate_up: float32 [8, 2, 768, 2048], P('blk', None, 'dp')
- grad_down: float32 [8, 768, 2048], P('blk', 'dp')
- grad_x: bfloat16 [8192, 2048], P('blk', 'dp')
Inputs may be any that keep to these rules, and one draw needn't show every extreme that they name: `counts`: on every device the 5 offsets take 3, 2, 1, 1 and 1 blocks of 128 rows, in an order drawn for each device, so the blocks fill all 1024 rows; an offset with k blocks has more than 128 * (k - 1) live rows; in every draw some device has an offset with exactly 384 live rows.
All inputs are finite; a program needn't handle non-finite values.
Results may differ from a plain program's by a relative error of at most 0.0095.
Values may be sent and summed in bfloat16 or wider, within the bound.
No kernel may reach another device: no remote copies, remote signals or barrier semaphores. Data moves between devices by JAX's collectives and lax.ppermute only.
A program may use at most 192 MiB of HBM per device.

v0:
```python
import functools

import jax
import jax.numpy as jnp
from jax import lax
from jax.experimental import pallas as pl
from jax.experimental.pallas import tpu as pltpu
from jax.sharding import PartitionSpec as P


HOPS = 4
SPAN = HOPS + 1
BLOCK = 128
MOST = 3
PARTS = 4
BF16 = jnp.bfloat16
F32 = jnp.float32


def size_of(axis):
    return lax.axis_size(axis)


def ahead(array, by, parity=None):
    size = size_of("blk")
    moves = lambda i: parity is None or i % 2 == parity
    return lax.ppermute(array, "blk", [((i + by) % size if moves(i) else i, i) for i in range(size)])


def swap_pair(array):
    return lax.ppermute(array, "blk", [(i, i ^ 1) for i in range(size_of("blk"))])


def swap_dp(array, bit):
    return lax.ppermute(array, "dp", [(i, i ^ bit) for i in range(size_of("dp"))])


def contract_last(lhs, rhs):
    return lax.dot_general(lhs, rhs, (((1,), (1,)), ((), ())), preferred_element_type=F32)


def matmul(lhs, rhs):
    return lax.dot_general(lhs, rhs, (((1,), (0,)), ((), ())), preferred_element_type=F32)


def whole(shape, **more):
    zeros = (0,) * len(shape)
    return pl.BlockSpec(tuple(shape), lambda i, s: zeros, **more)


OWN, ODD, WIN, START, LIM = 0, 1, 2, 2 + 2 * SPAN, 2 + 3 * SPAN
TABLE = LIM + SPAN * MOST


def table_kernel(n_dev, nblk, s_ref, out_ref):
    me, own = s_ref[0], s_ref[1]
    out_ref[OWN] = own
    out_ref[ODD] = lax.rem(me, 2)

    def count(device, o):
        return s_ref[2 + device * SPAN + o]

    def start(device, o):
        total = jnp.int32(0)
        for p in range(o):
            total += lax.div(count(device, p) + (BLOCK - 1), BLOCK)
        return total

    there = lax.rem(me + 2, n_dev)
    for o in range(SPAN):
        out_ref[START + o] = start(me, o)
        out_ref[WIN + o] = jnp.minimum(start(me, o), nblk - MOST)
        out_ref[WIN + SPAN + o] = jnp.minimum(start(there, o), nblk - MOST)
        device = lax.rem(me + o, n_dev)
        first = start(device, o)
        window = jnp.minimum(first, nblk - MOST)
        for t in range(MOST):
            block = window + t - first
            out_ref[LIM + o * MOST + t] = jnp.where(block >= 0, count(device, o) - block * BLOCK, 0)


def make_table(counts, n_dev, nblk):
    place = jnp.stack([lax.axis_index("blk"), lax.axis_index("dp")]).astype(jnp.int32)
    return pl.pallas_call(
        functools.partial(table_kernel, n_dev, nblk),
        out_shape=jax.ShapeDtypeStruct((TABLE,), jnp.int32),
        in_specs=[pl.BlockSpec(memory_space=pltpu.SMEM)],
        out_specs=pl.BlockSpec(memory_space=pltpu.SMEM),
    )(jnp.concatenate([place, counts.reshape(-1)]))


def cut(array, index):
    return lax.dynamic_slice_in_dim(array, index, MOST, 0)


def column(k, own):
    return (((k % 2) * 2) | (1 - k // 2)) ^ own


def expert_kernel(offsets, home, last, s_ref, *refs):
    refs = list(refs)
    take = lambda n: [refs.pop(0) for _ in range(n)]
    n_away = len(offsets) - home
    home_refs = take(2 * home)
    pieces = [take(2) for _ in range(n_away)]
    shares = take(4)
    add_in, add_out = take(2) if last else (None, None)
    if last:
        own_in, own_out, far_in, far_out = take(4)
    else:
        sum_in, sum_out = take(2)
    give, keep, w_ref, v_ref, sems, x_s, c_s, proj_s, hg_s, gu_s, gut_s, ht_s = refs
    step = pl.program_id(0)
    own = s_ref[OWN]
    core = own % 2
    half = BLOCK // 2
    quarter = BLOCK // PARTS
    depth = w_ref.shape[1]
    width = depth // PARTS
    units = v_ref.shape[0]
    fw = units // 2

    @pl.when(step == 0)
    def _():
        copies = []
        for k in range(2):
            w_share, v_share = shares[2 * k : 2 * k + 2]
            for g in range(2):
                copies.append((w_share.at[g], w_ref.at[pl.ds(g * units + k * fw, fw)]))
            copies.append((v_share, v_ref.at[pl.ds(k * fw, fw)]))
        copies = [pltpu.make_async_copy(a, b, sems.at[n]) for n, (a, b) in enumerate(copies)]
        for copy in copies:
            copy.start()

        def put(slot, t, at, size, x, c):
            rows = pl.ds(pl.multiple_of(slot * MOST * half + t * half + at, quarter), size)
            ids = lax.broadcasted_iota(jnp.int32, (size, 1), 0) + (own // 2) * half + at
            live = ids < s_ref[LIM + offsets[slot] * MOST + t]
            x_s[rows, :] = x
            c_s[rows, :] = jnp.where(live, c, jnp.zeros((), BF16))

        for slot in range(len(offsets)):
            for t in range(MOST):
                if slot < home:
                    put(slot, t, 0, half, home_refs[0][t, 0], home_refs[1][t, 0])
                else:
                    near, other = pieces[slot - home]
                    put(slot, t, core * quarter, quarter, near[t, 0], near[t, 1])
                    put(slot, t, (1 - core) * quarter, quarter, other[t, 0], other[t, 1])

        for copy in copies:
            copy.wait()

        def project(k, _):
            cols = pl.ds(pl.multiple_of(k * width, width), width)
            proj = contract_last(x_s[:, cols], w_ref[:, cols])
            hg = contract_last(c_s[:, cols], v_ref[:, cols])

            @pl.when(k == 0)
            def _():
                proj_s[...] = proj
                hg_s[...] = hg

            @pl.when(k > 0)
            def _():
                proj_s[...] += proj
                hg_s[...] += hg

            return 0

        lax.fori_loop(0, PARTS, project, 0)
        gate_pre = proj_s[:, :units]
        up_pre = proj_s[:, units:]
        hidden_grad = hg_s[...]
        sig = jax.nn.sigmoid(gate_pre)
        active = gate_pre * sig
        hidden = (active * up_pre).astype(BF16)
        gate_rows = (hidden_grad * up_pre * sig * (1.0 + gate_pre * (1.0 - sig))).astype(BF16)
        up_rows = (hidden_grad * active).astype(BF16)
        gu_s[:, :units] = gate_rows
        gu_s[:, units:] = up_rows
        gut_s[:units, :] = gate_rows.T
        gut_s[units:, :] = up_rows.T
        ht_s[...] = hidden.T

    cols = pl.ds(pl.multiple_of(column(step, own) * width, width), width)
    new_in = matmul(gut_s[...], x_s[:, cols])
    new_out = matmul(ht_s[...], c_s[:, cols])
    if last:
        new_in += add_in[...]
        new_out += add_out[...]
        own_in[0] = new_in[:fw]
        own_in[1] = new_in[units : units + fw]
        own_out[...] = new_out[:fw]
        far_in[0] = new_in[fw:units].astype(BF16)
        far_in[1] = new_in[units + fw :].astype(BF16)
        far_out[...] = new_out[fw:].astype(BF16)
    else:
        sum_in[...] = new_in
        sum_out[...] = new_out
    row_grad = matmul(gu_s[...], w_ref[:, cols]).astype(BF16)

    @pl.when(step < 2)
    def _():
        give[0] = row_grad

    @pl.when(step >= 2)
    def _():
        keep[0] = row_grad


def expert(table, offsets, home, pieces, shares, sums):
    last = sums is not None
    fw, depth = shares[1].shape
    units = 2 * fw
    width = depth // PARTS
    half = BLOCK // 2
    rows = len(offsets) * MOST * half
    once = pl.Buffered(1)
    arrays, specs = [], []
    for a in home:
        arrays.append(a)
        specs.append(whole(a.shape, pipeline_mode=once))
    for pair in pieces:
        for a in pair:
            arrays.append(a)
            specs.append(whole(a.shape, pipeline_mode=once))
    for a in shares:
        arrays.append(a)
        specs.append(pl.BlockSpec(memory_space=pl.ANY))
    chunk_in = pl.BlockSpec((2 * units, width), lambda i, s: (0, column(i, s[OWN])))
    chunk_out = pl.BlockSpec((units, width), lambda i, s: (0, column(i, s[OWN])))
    own_in = pl.BlockSpec((2, fw, width), lambda i, s: (0, 0, column(i, s[OWN])))
    own_out = pl.BlockSpec((fw, width), lambda i, s: (0, column(i, s[OWN])))
    if last:
        arrays += list(sums)
        specs += [chunk_in, chunk_out]
        shapes = [((2, fw, depth), F32), ((fw, depth), F32), ((2, fw, depth), BF16), ((fw, depth), BF16)]
        outs = [own_in, own_out, own_in, own_out]
    else:
        shapes = [((2 * units, depth), F32), ((units, depth), F32)]
        outs = [chunk_in, chunk_out]
    shapes += [((2, rows, width), BF16)] * 2
    outs += [
        pl.BlockSpec((1, rows, width), lambda i, s: (jnp.minimum(i, 1), 0, 0)),
        pl.BlockSpec((1, rows, width), lambda i, s: (jnp.maximum(i - 2, 0), 0, 0)),
    ]
    return pl.pallas_call(
        functools.partial(expert_kernel, tuple(offsets), len(home) // 2, last),
        out_shape=[jax.ShapeDtypeStruct(*s) for s in shapes],
        grid_spec=pltpu.PrefetchScalarGridSpec(
            num_scalar_prefetch=1,
            grid=(PARTS,),
            in_specs=specs,
            out_specs=outs,
            scratch_shapes=[
                pltpu.VMEM((2 * units, depth), BF16),
                pltpu.VMEM((units, depth), BF16),
                pltpu.SemaphoreType.DMA((6,)),
                pltpu.VMEM((rows, depth), BF16),
                pltpu.VMEM((rows, depth), BF16),
                pltpu.VMEM((rows, 2 * units), F32),
                pltpu.VMEM((rows, units), F32),
                pltpu.VMEM((rows, 2 * units), BF16),
                pltpu.VMEM((2 * units, rows), BF16),
                pltpu.VMEM((units, rows), BF16),
            ],
        ),
        compiler_params=pltpu.CompilerParams(vmem_limit_bytes=28 * 2**20),
        cost_estimate=pl.CostEstimate(
            flops=16 * rows * units * depth,
            bytes_accessed=rows * depth * 6 + units * depth * (6 + (24 if last else 12)),
            transcendentals=rows * units,
        ),
    )(table, *arrays)


def add_cores(give, keep, n):
    got = swap_dp(give, 1)
    shape = (n, MOST, BLOCK // 2, keep.shape[-1])
    return [(keep[k].astype(F32) + got[k].astype(F32)).astype(BF16).reshape(shape) for k in range(2)]


def add_rows(here, other):
    return [jnp.stack([here[k], other[k]]) for k in range(other.shape[0])]


def merge_kernel(s_ref, *refs):
    *sources, out = refs
    half = BLOCK // 2
    y = s_ref[OWN] // 2
    for b in range(out.shape[0]):
        for o, source in enumerate(sources):
            begin = s_ref[START + o]
            end = s_ref[START + o + 1] if o + 1 < SPAN else out.shape[0]

            @pl.when((b >= begin) & (b < end))
            def _():
                at = jnp.clip(b - s_ref[WIN + o], 0, MOST - 1)
                out[b, pl.ds(pl.multiple_of(y * half, half), half), :] = source[0, at]
                out[b, pl.ds(pl.multiple_of((1 - y) * half, half), half), :] = source[1, at]


def merge(table, sources, nblk):
    shape = (nblk, BLOCK, sources[0].shape[-1])
    return pl.pallas_call(
        merge_kernel,
        out_shape=jax.ShapeDtypeStruct(shape, BF16),
        grid_spec=pltpu.PrefetchScalarGridSpec(
            num_scalar_prefetch=1,
            grid=(1,),
            in_specs=[whole(s.shape) for s in sources],
            out_specs=whole(shape),
        ),
    )(table, *sources)


def on_device(x_rows, grad_rows, w_gate_up, w_down, counts):
    w_in, w_out = w_gate_up[0], w_down[0]
    _, depth = w_out.shape
    total = x_rows.shape[0]
    nblk = total // BLOCK
    n_dev = size_of("blk")
    assert size_of("dp") == PARTS and n_dev % 2 == 0 and n_dev > HOPS
    part = BLOCK // PARTS
    own = lax.axis_index("dp")

    def pick(array, first, end):
        array = array.reshape(nblk, PARTS, part, depth)
        return lax.dynamic_slice(array, (first, own, 0, 0), (end - first, 1, part, depth))

    def quarter(first, end):
        return jnp.concatenate([pick(x_rows, first, end), pick(grad_rows, first, end)], axis=1)

    mine = quarter(1, nblk)
    there = ahead(mine, 2)
    mine, counts, x_rows, grad_rows = lax.optimization_barrier((mine, counts, x_rows, grad_rows))
    table = make_table(counts, n_dev, nblk)
    o_in, o_out = swap_dp(w_in, 2), swap_dp(w_out, 2)
    home = lambda a: lax.dynamic_slice(
        a[: MOST * BLOCK].reshape(MOST, 2, BLOCK // 2, depth), (0, own // 2, 0, 0), (MOST, 1, BLOCK // 2, depth)
    )

    fourth = ahead(there[nblk - 1 - MOST :], 2)
    third = swap_pair(cut(there, table[WIN + SPAN + 3] - 1))
    third = ahead(third, 2, parity=1)
    first = jnp.where(table[ODD] == 1, cut(mine, table[WIN + 1] - 1), cut(there, table[WIN + SPAN + 1] - 1))
    first = swap_pair(first)
    second = cut(there, table[WIN + SPAN + 2] - 1)
    shares = (w_in, w_out, o_in, o_out)
    pair = lambda a: (a, swap_dp(a, 1))
    sum_in, sum_out, give, keep = expert(
        table, (0, 2, 4), (home(x_rows), home(grad_rows)), [pair(second), pair(fourth)], shares, None
    )
    here, there = add_cores(give, keep, 3)
    sum_in, there = lax.optimization_barrier((sum_in, there))
    there = swap_dp(there, 2)
    r0, r2, r4 = add_rows(here, there)
    pieces = [pair(first), pair(third)]
    own_in, own_out, far_in, far_out, give, keep = expert(table, (1, 3), (), pieces, shares, (sum_in, sum_out))
    here, there = add_cores(give, keep, 2)
    there = swap_dp(there, 2)
    there, far_in, far_out = lax.optimization_barrier((there, far_in, far_out))
    r1, r3 = add_rows(here, there)
    far_in, far_out = swap_dp(far_in, 2), swap_dp(far_out, 2)
    results = [r0] + [ahead(r, -o) for o, r in ((1, r1), (2, r2), (3, r3), (4, r4))]
    done = merge(table, results, nblk)
    return (own_in + far_in)[None], (own_out + far_out)[None], done.reshape(total, -1)


def solution(mesh):
    return jax.shard_map(
        on_device,
        mesh=mesh,
        in_specs=(
            P("blk", None),
            P("blk", None),
            P("blk", None, "dp", None),
            P("blk", "dp", None),
            P(),
        ),
        out_specs=(P("blk", None, "dp", None), P("blk", "dp", None), P("blk", "dp")),
        check_vma=False,
    )
```

profile of v0, /device:TPU:0, one launch (start us, length us, event | category | flops | bytes accessed | tf_op | source)
XLA Modules:
  0.0 202.3 jit_solution(9556337079240691741)
XLA Ops:
  0.6 1.6 constant_dynamic-slice_fusion.4
  3.6 5.1 %collective-permute-start = (bf16[7,2,32,2048]{3,2,1,0:T(8,128)(2,1)}, bf16[7,2,32,2048]{3,2,1,0:T(8,128)(2,1)}, u32[]{:S(2)}, u32[]{:S(2)}) collective-permute-start(bf16[7,2,32,2048]{3,2,1,0:T(8,128)(2,1)} %pad_maximum_fusion), channel_id=1, source_target_pairs={{8,0},{12,4},{16,8},{20,12},{24,16},{28,20},{0,24},{4,28},{9,1},{1... | collective-permute-start | bytes 5505032 | tf_op jit(solution)/shard_map/ppermute | solution.py:27
  8.7 1.5 collective-permute-start.6
  19.3 29.0 %collective-permute-done = bf16[7,2,32,2048]{3,2,1,0:T(8,128)(2,1)} collective-permute-done((bf16[7,2,32,2048]{3,2,1,0:T(8,128)(2,1)}, bf16[7,2,32,2048]{3,2,1,0:T(8,128)(2,1)}, u32[]{:S(2)}, u32[]{:S(2)}) %collective-permute-start) | collective-permute-done | bytes 1835040 | tf_op jit(solution)/shard_map/ppermute | solution.py:27
  48.3 3.5 %fusion = (bf16[3,2,32,2048]{3,2,1,0:T(8,128)(2,1)S(1)}, bf16[3,2,32,2048]{3,2,1,0:T(8,128)(2,1)S(1)}, bf16[3,2,32,2048]{3,2,1,0:T(8,128)(2,1)}, bf16[3,2,32,2048]{3,2,1,0:T(8,128)(2,1)}) fusion(bf16[7,2,32,2048]{3,2,1,0:T(8,128)(2,1)} %collective-permute-done, s32[]{:T(128)S(6)} %select_n.42, s32[]{:T(128)S(6)} %select_n.39, s32[]{:T(128)S(6)} %select_n.37, ...), kind=kLoop, calls=%fused_computation.20 | loop fusion | flops 393216 | bytes 7077905 | tf_op jit(solution)/shard_map/slice | solution.py:344
  51.8 4.4 %collective-permute-start.9 = (bf16[3,2,32,2048]{3,2,1,0:T(8,128)(2,1)S(1)}, bf16[3,2,32,2048]{3,2,1,0:T(8,128)(2,1)}, u32[]{:S(2)}, u32[]{:S(2)}) collective-permute-start(bf16[3,2,32,2048]{3,2,1,0:T(8,128)(2,1)S(1)} %get-tuple-element.43), channel_id=1, source_target_pairs={{8,0},{12,4},{16,8},{20,12},{24,16},{28,20},{0,24},{4,28},{9,1},{1... | collective-permute-start | bytes 2359304 | tf_op jit(solution)/shard_map/ppermute | solution.py:27
  59.1 13.1 %collective-permute-done.9.refs_4_ = bf16[3,2,32,2048]{3,2,1,0:T(8,128)(2,1)} collective-permute-done((bf16[3,2,32,2048]{3,2,1,0:T(8,128)(2,1)S(1)}, bf16[3,2,32,2048]{3,2,1,0:T(8,128)(2,1)}, u32[]{:S(2)}, u32[]{:S(2)}) %collective-permute-start.9) | collective-permute-done | bytes 786464 | tf_op jit(solution)/shard_map/ppermute | solution.py:27
  72.2 2.7 %slice.102 = bf16[384,2048]{1,0:T(8,128)(2,1)} slice(bf16[1024,2048]{1,0:T(8,128)(2,1)} %param.5), slice={[0:384], [0:2048]} | slice | bytes 3145728 | tf_op jit(solution)/shard_map/slice | solution.py:341
  74.9 2.7 %slice.103 = bf16[384,2048]{1,0:T(8,128)(2,1)} slice(bf16[1024,2048]{1,0:T(8,128)(2,1)} %param.6), slice={[0:384], [0:2048]} | slice | bytes 3145728 | tf_op jit(solution)/shard_map/slice | solution.py:341
  80.9 1.8 collective-permute-start.4
  82.7 17.0 %shard_map.77 = (f32[768,2048]{1,0:T(8,128)S(1)}, f32[384,2048]{1,0:T(8,128)S(1)}, bf16[2,576,512]{2,1,0:T(8,128)(2,1)S(1)}, bf16[2,576,512]{2,1,0:T(8,128)(2,1)S(1)}) custom-call(s32[32]{0:T(128)S(1)} %copy-done.1, bf16[3,1,64,2048]{3,2,1,0:T(8,128)(2,1)S(1)} %constant_dynamic-slice_fusion.2.refs_0_, ...), custom_call_target="tpu_custom_call" | custom-call | flops 7247757312 | bytes 21233664 | tf_op jit(solution)/shard_map/pallas_call | solution.py:248
  100.5 2.1 %collective-permute-done.11 = bf16[2,576,512]{2,1,0:T(8,128)(2,1)S(1)} collective-permute-done((bf16[2,576,512]{2,1,0:T(8,128)(2,1)S(1)}, bf16[2,576,512]{2,1,0:T(8,128)(2,1)S(1)}, u32[]{:S(2)}, u32[]{:S(2)}) %collective-permute-start.11) | collective-permute-done | bytes 1179680 | tf_op jit(solution)/shard_map/ppermute | solution.py:35
  104.8 13.1 %shard_map.78 = (f32[2,192,2048]{2,1,0:T(8,128)S(1)}, f32[192,2048]{1,0:T(8,128)S(1)}, bf16[2,192,2048]{2,1,0:T(8,128)(2,1)}, bf16[192,2048]{1,0:T(8,128)(2,1)},...) custom-call(s32[32]{0:T(128)S(1)} %copy-done.1, ...), custom_call_target="tpu_custom_call" | custom-call | flops 4831838208 | bytes 28311552 | tf_op jit(solution)/shard_map/pallas_call | solution.py:248
  118.3 1.5 collective-permute-start.16
  120.5 1.6 collective-permute-start.13
  122.1 12.3 %collective-permute-done.16 = bf16[3,3,64,512]{3,2,1,0:T(8,128)(2,1)S(1)} collective-permute-done((bf16[3,3,64,512]{3,2,1,0:T(8,128)(2,1)S(1)}, bf16[3,3,64,512]{3,2,1,0:T(8,128)(2,1)S(1)}, u32[]{:S(2)}, u32[]{:S(2)}) %collective-permute-start.16) | collective-permute-done | bytes 589856 | tf_op jit(solution)/shard_map/ppermute | solution.py:35
  134.7 5.0 %collective-permute-start.20 = (bf16[2,3,64,512]{3,2,1,0:T(8,128)(2,1)S(1)}, bf16[2,3,64,512]{3,2,1,0:T(8,128)(2,1)}, u32[]{:S(2)}, u32[]{:S(2)}) collective-permute-start(bf16[2,3,64,512]{3,2,1,0:T(8,128)(2,1)S(1)} %pad_maximum_fusion.5), channel_id=1, source_target_pairs={{16,0},{20,4},{24,8},{28,12},{0,16},{4,20},{8,24},{12,28},{17,1},{... | collective-permute-start | bytes 1179656 | tf_op jit(solution)/shard_map/ppermute | solution.py:27
  139.7 2.5 %collective-permute-done.13 = bf16[2,3,64,512]{3,2,1,0:T(8,128)(2,1)S(1)} collective-permute-done((bf16[2,3,64,512]{3,2,1,0:T(8,128)(2,1)S(1)}, bf16[2,3,64,512]{3,2,1,0:T(8,128)(2,1)S(1)}, u32[]{:S(2)}, u32[]{:S(2)}) %collective-permute-start.13) | collective-permute-done | bytes 393248 | tf_op jit(solution)/shard_map/ppermute | solution.py:35
  144.4 5.2 %collective-permute-start.17 = (bf16[2,3,64,512]{3,2,1,0:T(8,128)(2,1)S(1)}, bf16[2,3,64,512]{3,2,1,0:T(8,128)(2,1)}, u32[]{:S(2)}, u32[]{:S(2)}) collective-permute-start(bf16[2,3,64,512]{3,2,1,0:T(8,128)(2,1)S(1)} %pad_maximum_fusion.2), channel_id=1, source_target_pairs={{28,0},{0,4},{4,8},{8,12},{12,16},{16,20},{20,24},{24,28},{29,1},{... | collective-permute-start | bytes 1179656 | tf_op jit(solution)/shard_map/ppermute | solution.py:27
  151.9 20.5 %collective-permute-done.20.refs_4_ = bf16[2,3,64,512]{3,2,1,0:T(8,128)(2,1)} collective-permute-done((bf16[2,3,64,512]{3,2,1,0:T(8,128)(2,1)S(1)}, bf16[2,3,64,512]{3,2,1,0:T(8,128)(2,1)}, u32[]{:S(2)}, u32[]{:S(2)}) %collective-permute-start.20) | collective-permute-done | bytes 393248 | tf_op jit(solution)/shard_map/ppermute | solution.py:27
  172.4 19.9 %collective-permute-done.19.refs_3_ = bf16[2,3,64,512]{3,2,1,0:T(8,128)(2,1)} collective-permute-done((bf16[2,3,64,512]{3,2,1,0:T(8,128)(2,1)S(1)}, bf16[2,3,64,512]{3,2,1,0:T(8,128)(2,1)}, u32[]{:S(2)}, u32[]{:S(2)}) %collective-permute-start.19) | collective-permute-done | bytes 393248 | tf_op jit(solution)/shard_map/ppermute | solution.py:27
  192.3 3.5 %shard_map.79 = bf16[8,128,512]{2,1,0:T(8,128)(2,1)} custom-call(s32[32]{0:T(128)} %shard_map.76.s_ref, bf16[2,3,64,512]{3,2,1,0:T(8,128)(2,1)} %pad_maximum_fusion.1.refs_0_, bf16[2,3,64,512]{3,2,1,0:T(8,128)(2,1)} %collective-permute-done.17.refs_1_, bf16[2,3,64,512]{3,2,1,0:T(8,128)(2,1)} %copy-done.8, ...), custom_call_target="tpu_custom_call" | custom-call | tf_op jit(solution)/shard_map/pallas_call | solution.py:306
  195.8 3.0 %add_bitcast_fusion.1 = f32[1,192,2048]{2,1,0:T(8,128)} fusion(f32[192,2048]{1,0:T(8,128)} %copy-done, bf16[192,2048]{1,0:T(8,128)(2,1)} %collective-permute-done.15), kind=kLoop, calls=%fused_computation.2 | loop fusion | flops 786432 | bytes 3932160 | tf_op jit(solution)/shard_map/broadcast_in_dim | solution.py:368
  198.8 3.5 %add_bitcast_fusion = f32[1,2,192,2048]{3,2,1,0:T(8,128)} fusion(f32[2,192,2048]{2,1,0:T(8,128)S(1)} %get-tuple-element.31, bf16[2,192,2048]{2,1,0:T(8,128)(2,1)} %collective-permute-done.14), kind=kLoop, calls=%fused_computation | loop fusion | flops 1572864 | bytes 7864320 | tf_op jit(solution)/shard_map/broadcast_in_dim | solution.py:368
  (65 shorter events, 19.7 us)
Async XLA Ops:
  2.2 8.0 %copy-start.9 = (s32[8,5]{1,0:T(8,128)S(1)}, s32[8,5]{1,0:T(8,128)}, u32[]{:S(2)}) copy-start(s32[8,5]{1,0:T(8,128)} %param.9) | copy-start | bytes 484
  3.6 44.7 %collective-permute-start = (bf16[7,2,32,2048]{3,2,1,0:T(8,128)(2,1)}, bf16[7,2,32,2048]{3,2,1,0:T(8,128)(2,1)}, u32[]{:S(2)}, u32[]{:S(2)}) collective-permute-start(bf16[7,2,32,2048]{3,2,1,0:T(8,128)(2,1)} %pad_maximum_fusion), channel_id=1, source_target_pairs={{8,0},{12,4},{16,8},{20,12},{24,16},{28,20},{0,24},{4,28},{9,1},{1... | collective-permute-start | bytes 5505032 | tf_op jit(solution)/shard_map/ppermute | solution.py:27
  8.7 73.9 %collective-permute-start.6 = (bf16[2,192,2048]{2,1,0:T(8,128)(2,1)S(1)}, bf16[2,192,2048]{2,1,0:T(8,128)(2,1)}, u32[]{:S(2)}, u32[]{:S(2)}) collective-permute-start(bf16[2,192,2048]{2,1,0:T(8,128)(2,1)S(1)} %bitcast.29), channel_id=1, source_target_pairs={{0,2},{1,3},{2,0},{3,1},{4,6},{5,7},{6,4},{7,5},{8,10},{9,11},{10,... | collective-permute-start | bytes 4718600 | tf_op jit(solution)/shard_map/ppermute | solution.py:35
  48.3 7.9 %copy-start.4 = (bf16[1,192,2048]{2,1,0:T(8,128)(2,1)S(1)}, bf16[1,192,2048]{2,1,0:T(8,128)(2,1)}, u32[]{:S(2)}) copy-start(bf16[1,192,2048]{2,1,0:T(8,128)(2,1)} %param.8) | copy-start | bytes 2359300
  51.8 20.4 %collective-permute-start.9 = (bf16[3,2,32,2048]{3,2,1,0:T(8,128)(2,1)S(1)}, bf16[3,2,32,2048]{3,2,1,0:T(8,128)(2,1)}, u32[]{:S(2)}, u32[]{:S(2)}) collective-permute-start(bf16[3,2,32,2048]{3,2,1,0:T(8,128)(2,1)S(1)} %get-tuple-element.43), channel_id=1, source_target_pairs={{8,0},{12,4},{16,8},{20,12},{24,16},{28,20},{0,24},{4,28},{9,1},{1... | collective-permute-start | bytes 2359304 | tf_op jit(solution)/shard_map/ppermute | solution.py:27
  56.3 23.1 %collective-permute-start.7 = (bf16[192,2048]{1,0:T(8,128)(2,1)S(1)}, bf16[192,2048]{1,0:T(8,128)(2,1)}, u32[]{:S(2)}, u32[]{:S(2)}) collective-permute-start(bf16[192,2048]{1,0:T(8,128)(2,1)S(1)} %bitcast.32), channel_id=1, source_target_pairs={{0,2},{1,3},{2,0},{3,1},{4,6},{5,7},{6,4},{7,5},{8,10},{9,11},{10,... | collective-permute-start | bytes 2359304 | tf_op jit(solution)/shard_map/ppermute | solution.py:35
  57.8 23.1 %collective-permute-start.3 = (bf16[3,2,32,2048]{3,2,1,0:T(8,128)(2,1)}, bf16[3,2,32,2048]{3,2,1,0:T(8,128)(2,1)}, u32[]{:S(2)}, u32[]{:S(2)}) collective-permute-start(bf16[3,2,32,2048]{3,2,1,0:T(8,128)(2,1)} %get-tuple-element.45), channel_id=1, source_target_pairs={{0,4},{4,0},{8,12},{12,8},{16,20},{20,16},{24,28},{28,24},{1,5},{5... | collective-permute-start | bytes 2359304 | tf_op jit(solution)/shard_map/ppermute | solution.py:31
  59.1 23.5 %collective-permute-start.8 = (bf16[3,2,32,2048]{3,2,1,0:T(8,128)(2,1)S(1)}, bf16[3,2,32,2048]{3,2,1,0:T(8,128)(2,1)}, u32[]{:S(2)}, u32[]{:S(2)}) collective-permute-start(bf16[3,2,32,2048]{3,2,1,0:T(8,128)(2,1)S(1)} %get-tuple-element.44.refs_2_), channel_id=1, source_target_pairs={{0,1},{1,0},{2,3},{3,2},{4,5},{5,4},{6,7},{7,6},{8,9},{9,8},{10,11... | collective-permute-start | bytes 2359304 | tf_op jit(solution)/shard_map/ppermute | solution.py:35
  72.2 10.5 %collective-permute-start.10 = (bf16[3,2,32,2048]{3,2,1,0:T(8,128)(2,1)}, bf16[3,2,32,2048]{3,2,1,0:T(8,128)(2,1)}, u32[]{:S(2)}, u32[]{:S(2)}) collective-permute-start(bf16[3,2,32,2048]{3,2,1,0:T(8,128)(2,1)} %collective-permute-done.9.refs_4_), channel_id=1, source_target_pairs={{0,1},{1,0},{2,3},{3,2},{4,5},{5,4},{6,7},{7,6},{8,9},{9,8},{10,11... | collective-permute-start | bytes 2359304 | tf_op jit(solution)/shard_map/ppermute | solution.py:35
  79.5 20.5 %collective-permute-start.1 = (bf16[3,2,32,2048]{3,2,1,0:T(8,128)(2,1)S(1)}, bf16[3,2,32,2048]{3,2,1,0:T(8,128)(2,1)S(1)}, u32[]{:S(2)}, u32[]{:S(2)}) collective-permute-start(bf16[3,2,32,2048]{3,2,1,0:T(8,128)(2,1)S(1)} %copy-done.7), channel_id=1, source_target_pairs={{0,4},{4,0},{8,12},{12,8},{16,20},{20,16},{24,28},{28,24},{1,5},{5... | collective-permute-start | bytes 2359304 | tf_op jit(solution)/shard_map/ppermute | solution.py:31
  80.9 19.4 %collective-permute-start.4 = (bf16[3,2,32,2048]{3,2,1,0:T(8,128)(2,1)}, bf16[3,2,32,2048]{3,2,1,0:T(8,128)(2,1)S(1)}, u32[]{:S(2)}, u32[]{:S(2)}) collective-permute-start(bf16[3,2,32,2048]{3,2,1,0:T(8,128)(2,1)} %collective-permute-done.3), channel_id=1, source_target_pairs={{0,0},{12,4},{8,8},{20,12},{16,16},{28,20},{24,24},{4,28},{1,1},{1... | collective-permute-start | bytes 2359304 | tf_op jit(solution)/shard_map/ppermute | solution.py:27
  99.6 2.9 %collective-permute-start.11 = (bf16[2,576,512]{2,1,0:T(8,128)(2,1)S(1)}, bf16[2,576,512]{2,1,0:T(8,128)(2,1)S(1)}, u32[]{:S(2)}, u32[]{:S(2)}) collective-permute-start(bf16[2,576,512]{2,1,0:T(8,128)(2,1)S(1)} %get-tuple-element.28), channel_id=1, source_target_pairs={{0,1},{1,0},{2,3},{3,2},{4,5},{5,4},{6,7},{7,6},{8,9},{9,8},{10,11... | collective-permute-start | bytes 3538952 | tf_op jit(solution)/shard_map/ppermute | solution.py:35
  99.9 3.7 %collective-permute-start.2 = (bf16[3,2,32,2048]{3,2,1,0:T(8,128)(2,1)S(1)}, bf16[3,2,32,2048]{3,2,1,0:T(8,128)(2,1)S(1)}, u32[]{:S(2)}, u32[]{:S(2)}) collective-permute-start(bf16[3,2,32,2048]{3,2,1,0:T(8,128)(2,1)S(1)} %collective-permute-done.1.refs_0_), channel_id=1, source_target_pairs={{0,1},{1,0},{2,3},{3,2},{4,5},{5,4},{6,7},{7,6},{8,9},{9,8},{10,11... | collective-permute-start | bytes 2359304 | tf_op jit(solution)/shard_map/ppermute | solution.py:35
  100.2 4.6 %collective-permute-start.5 = (bf16[3,2,32,2048]{3,2,1,0:T(8,128)(2,1)S(1)}, bf16[3,2,32,2048]{3,2,1,0:T(8,128)(2,1)S(1)}, u32[]{:S(2)}, u32[]{:S(2)}) collective-permute-start(bf16[3,2,32,2048]{3,2,1,0:T(8,128)(2,1)S(1)} %collective-permute-done.4.refs_2_), channel_id=1, source_target_pairs={{0,1},{1,0},{2,3},{3,2},{4,5},{5,4},{6,7},{7,6},{8,9},{9,8},{10,11... | collective-permute-start | bytes 2359304 | tf_op jit(solution)/shard_map/ppermute | solution.py:35
  118.0 2.4 %collective-permute-start.12 = (bf16[2,384,512]{2,1,0:T(8,128)(2,1)S(1)}, bf16[2,384,512]{2,1,0:T(8,128)(2,1)S(1)}, u32[]{:S(2)}, u32[]{:S(2)}) collective-permute-start(bf16[2,384,512]{2,1,0:T(8,128)(2,1)S(1)} %get-tuple-element.33), channel_id=1, source_target_pairs={{0,1},{1,0},{2,3},{3,2},{4,5},{5,4},{6,7},{7,6},{8,9},{9,8},{10,11... | collective-permute-start | bytes 2359304 | tf_op jit(solution)/shard_map/ppermute | solution.py:35
  118.3 16.2 %collective-permute-start.16 = (bf16[3,3,64,512]{3,2,1,0:T(8,128)(2,1)S(1)}, bf16[3,3,64,512]{3,2,1,0:T(8,128)(2,1)S(1)}, u32[]{:S(2)}, u32[]{:S(2)}) collective-permute-start(bf16[3,3,64,512]{3,2,1,0:T(8,128)(2,1)S(1)} %bitcast.45), channel_id=1, source_target_pairs={{0,2},{1,3},{2,0},{3,1},{4,6},{5,7},{6,4},{7,5},{8,10},{9,11},{10,... | collective-permute-start | bytes 1769480 | tf_op jit(solution)/shard_map/ppermute | solution.py:35
  120.5 21.6 %collective-permute-start.13 = (bf16[2,3,64,512]{3,2,1,0:T(8,128)(2,1)S(1)}, bf16[2,3,64,512]{3,2,1,0:T(8,128)(2,1)S(1)}, u32[]{:S(2)}, u32[]{:S(2)}) collective-permute-start(bf16[2,3,64,512]{3,2,1,0:T(8,128)(2,1)S(1)} %bitcast.46), channel_id=1, source_target_pairs={{0,2},{1,3},{2,0},{3,1},{4,6},{5,7},{6,4},{7,5},{8,10},{9,11},{10,... | collective-permute-start | bytes 1179656 | tf_op jit(solution)/shard_map/ppermute | solution.py:35
  134.6 15.1 %collective-permute-start.18 = (bf16[2,3,64,512]{3,2,1,0:T(8,128)(2,1)S(1)}, bf16[2,3,64,512]{3,2,1,0:T(8,128)(2,1)S(1)}, u32[]{:S(2)}, u32[]{:S(2)}) collective-permute-start(bf16[2,3,64,512]{3,2,1,0:T(8,128)(2,1)S(1)} %pad_maximum_fusion.3), channel_id=1, source_target_pairs={{24,0},{28,4},{0,8},{4,12},{8,16},{12,20},{16,24},{20,28},{25,1},{... | collective-permute-start | bytes 1179656 | tf_op jit(solution)/shard_map/ppermute | solution.py:27
  134.7 37.8 %collective-permute-start.20 = (bf16[2,3,64,512]{3,2,1,0:T(8,128)(2,1)S(1)}, bf16[2,3,64,512]{3,2,1,0:T(8,128)(2,1)}, u32[]{:S(2)}, u32[]{:S(2)}) collective-permute-start(bf16[2,3,64,512]{3,2,1,0:T(8,128)(2,1)S(1)} %pad_maximum_fusion.5), channel_id=1, source_target_pairs={{16,0},{20,4},{24,8},{28,12},{0,16},{4,20},{8,24},{12,28},{17,1},{... | collective-permute-start | bytes 1179656 | tf_op jit(solution)/shard_map/ppermute | solution.py:27
  142.2 56.6 %collective-permute-start.14 = (bf16[2,192,2048]{2,1,0:T(8,128)(2,1)}, bf16[2,192,2048]{2,1,0:T(8,128)(2,1)}, u32[]{:S(2)}, u32[]{:S(2)}) collective-permute-start(bf16[2,192,2048]{2,1,0:T(8,128)(2,1)} %get-tuple-element.36), channel_id=1, source_target_pairs={{0,2},{1,3},{2,0},{3,1},{4,6},{5,7},{6,4},{7,5},{8,10},{9,11},{10,... | collective-permute-start | bytes 4718600 | tf_op jit(solution)/shard_map/ppermute | solution.py:35
  143.7 52.1 %collective-permute-start.15 = (bf16[192,2048]{1,0:T(8,128)(2,1)}, bf16[192,2048]{1,0:T(8,128)(2,1)}, u32[]{:S(2)}, u32[]{:S(2)}) collective-permute-start(bf16[192,2048]{1,0:T(8,128)(2,1)} %get-tuple-element.38), channel_id=1, source_target_pairs={{0,2},{1,3},{2,0},{3,1},{4,6},{5,7},{6,4},{7,5},{8,10},{9,11},{10,... | collective-permute-start | bytes 2359304 | tf_op jit(solution)/shard_map/ppermute | solution.py:35
  144.4 28.0 %collective-permute-start.17 = (bf16[2,3,64,512]{3,2,1,0:T(8,128)(2,1)S(1)}, bf16[2,3,64,512]{3,2,1,0:T(8,128)(2,1)}, u32[]{:S(2)}, u32[]{:S(2)}) collective-permute-start(bf16[2,3,64,512]{3,2,1,0:T(8,128)(2,1)S(1)} %pad_maximum_fusion.2), channel_id=1, source_target_pairs={{28,0},{0,4},{4,8},{8,12},{12,16},{16,20},{20,24},{24,28},{29,1},{... | collective-permute-start | bytes 1179656 | tf_op jit(solution)/shard_map/ppermute | solution.py:27
  149.7 42.7 %copy-start.8 = (bf16[2,3,64,512]{3,2,1,0:T(8,128)(2,1)}, bf16[2,3,64,512]{3,2,1,0:T(8,128)(2,1)S(1)}, u32[]{:S(2)}) copy-start(bf16[2,3,64,512]{3,2,1,0:T(8,128)(2,1)S(1)} %collective-permute-done.18.refs_2_) | copy-start | bytes 1179652
  149.7 42.6 %collective-permute-start.19 = (bf16[2,3,64,512]{3,2,1,0:T(8,128)(2,1)S(1)}, bf16[2,3,64,512]{3,2,1,0:T(8,128)(2,1)}, u32[]{:S(2)}, u32[]{:S(2)}) collective-permute-start(bf16[2,3,64,512]{3,2,1,0:T(8,128)(2,1)S(1)} %pad_maximum_fusion.4), channel_id=1, source_target_pairs={{20,0},{24,4},{28,8},{0,12},{4,16},{8,20},{12,24},{16,28},{21,1},{... | collective-permute-start | bytes 1179656 | tf_op jit(solution)/shard_map/ppermute | solution.py:27
  (7 other events, 22.1 us)
where the time goes:
time: 204 us; the launch traced here: 202 us
  waiting for transfers between devices  102 us (50%)
  starting transfers between devices  35.1 us (17%)
  Pallas kernels  34.9 us (17%)
  other arithmetic  13.5 us (7%)
  local copies, waits for them, and re-layouts  10.6 us (5%)
  between operations  6.42 us (3%)
    ppermute x7, waiting for transfers between devices, ahead(): lax.ppermute(array, 'blk', [((i + by) % size if moves(i) else i, i) for i...  82.5 us
    pallas_call x2, Pallas kernels, expert(): pl.pallas_call(functools.partial(expert_kernel, tuple(offsets), len(home)...  30.1 us
    ppermute x7, starting transfers between devices, ahead(): lax.ppermute(array, 'blk', [((i + by) % size if moves(i) else i, i) for i...  23 us
    ppermute x12, waiting for transfers between devices, swap_dp(): lax.ppermute(array, 'dp', [(i, i ^ bit) for i in range(size_of('dp'))])  19.3 us
    ppermute x12, starting transfers between devices, swap_dp(): lax.ppermute(array, 'dp', [(i, i ^ bit) for i in range(size_of('dp'))])  9.39 us
    slice x2, local copies, waits for them, and re-layouts, on_device(): a[:MOST * BLOCK].reshape(MOST, 2, BLOCK // 2, depth)  5.45 us
  transfers between devices with their start and end apart: 21, of which 10 were waited for; matrix products, arithmetic and copies ran while one was open for 8% of the time, Pallas kernels for 11%

commit v1 on v0

--- a/solution.py
+++ b/solution.py
@@ -122,53 +122,40 @@
 
     @pl.when(step == 0)
     def _():
-        copies = []
+        moves = []
         for k in range(2):
             w_share, v_share = shares[2 * k : 2 * k + 2]
             for g in range(2):
-                copies.append((w_share.at[g], w_ref.at[pl.ds(g * units + k * fw, fw)]))
-            copies.append((v_share, v_ref.at[pl.ds(k * fw, fw)]))
-        copies = [pltpu.make_async_copy(a, b, sems.at[n]) for n, (a, b) in enumerate(copies)]
+                moves.append((w_share.at[g], w_ref.at[pl.ds(g * units + k * fw, fw)]))
+            moves.append((v_share, v_ref.at[pl.ds(k * fw, fw)]))
+        for slot in range(len(offsets)):
+            for t in range(MOST):
+                base = (slot * MOST + t) * half
+                if slot < home:
+                    for ref, rows in zip(home_refs, (x_s, c_s)):
+                        moves.append((ref.at[t, 0], rows.at[pl.ds(base, half)]))
+                else:
+                    for ref, at in zip(pieces[slot - home], (core, 1 - core)):
+                        place = pl.ds(pl.multiple_of(base + at * quarter, quarter), quarter)
+                        for g, rows in enumerate((x_s, c_s)):
+                            moves.append((ref.at[t, g], rows.at[place]))
+        copies = [pltpu.make_async_copy(a, b, sems.at[n]) for n, (a, b) in enumerate(moves)]
         for copy in copies:
             copy.start()
-
-        def put(slot, t, at, size, x, c):
-            rows = pl.ds(pl.multiple_of(slot * MOST * half + t * half + at, quarter), size)
-            ids = lax.broadcasted_iota(jnp.int32, (size, 1), 0) + (own // 2) * half + at
-            live = ids < s_ref[LIM + offsets[slot] * MOST + t]
-            x_s[rows, :] = x
-            c_s[rows, :] = jnp.where(live, c, jnp.zeros((), BF16))
-
+        for copy in copies:
+            copy.wait()
         for slot in range(len(offsets)):
             for t in range(MOST):
-                if slot < home:
-                    put(slot, t, 0, half, home_refs[0][t, 0], home_refs[1][t, 0])
-                else:
-                    near, other = pieces[slot - home]
-                    put(slot, t, core * quarter, quarter, near[t, 0], near[t, 1])
-                    put(slot, t, (1 - core) * quarter, quarter, other[t, 0], other[t, 1])
-
-        for copy in copies:
-            copy.wait()
-
-        def project(k, _):
-            cols = pl.ds(pl.multiple_of(k * width, width), width)
-            proj = contract_last(x_s[:, cols], w_ref[:, cols])
-            hg = contract_last(c_s[:, cols], v_ref[:, cols])
-
-            @pl.when(k == 0)
-            def _():
-                proj_s[...] = proj
-                hg_s[...] = hg
-
-            @pl.when(k > 0)
-            def _():
-                proj_s[...] += proj
-                hg_s[...] += hg
-
-            return 0
-
-        lax.fori_loop(0, PARTS, project, 0)
+                limit = s_ref[LIM + offsets[slot] * MOST + t]
+                rows = pl.ds((slot * MOST + t) * half, half)
+
+                @pl.when(limit < BLOCK)
+                def _():
+                    ids = lax.broadcasted_iota(jnp.int32, (half, 1), 0) + (own // 2) * half
+                    c_s[rows, :] = jnp.where(ids < limit, c_s[rows, :], jnp.zeros((), BF16))
+
+        proj_s[...] = contract_last(x_s[...], w_ref[...])
+        hg_s[...] = contract_last(c_s[...], v_ref[...])
         gate_pre = proj_s[:, :units]
         up_pre = proj_s[:, units:]
         hidden_grad = hg_s[...]
@@ -216,15 +203,14 @@
     width = depth // PARTS
     half = BLOCK // 2
     rows = len(offsets) * MOST * half
-    once = pl.Buffered(1)
     arrays, specs = [], []
     for a in home:
         arrays.append(a)
-        specs.append(whole(a.shape, pipeline_mode=once))
+        specs.append(pl.BlockSpec(memory_space=pl.ANY))
     for pair in pieces:
         for a in pair:
             arrays.append(a)
-            specs.append(whole(a.shape, pipeline_mode=once))
+            specs.append(pl.BlockSpec(memory_space=pl.ANY))
     for a in shares:
         arrays.append(a)
         specs.append(pl.BlockSpec(memory_space=pl.ANY))
@@ -256,7 +242,7 @@
             scratch_shapes=[
                 pltpu.VMEM((2 * units, depth), BF16),
                 pltpu.VMEM((units, depth), BF16),
-                pltpu.SemaphoreType.DMA((6,)),
+                pltpu.SemaphoreType.DMA((6 + MOST * (len(home) + 4 * len(pieces)),)),
                 pltpu.VMEM((rows, depth), BF16),
                 pltpu.VMEM((rows, depth), BF16),
                 pltpu.VMEM((rows, 2 * units), F32),
@@ -266,7 +252,7 @@
                 pltpu.VMEM((units, rows), BF16),
             ],
         ),
-        compiler_params=pltpu.CompilerParams(vmem_limit_bytes=28 * 2**20),
+        compiler_params=pltpu.CompilerParams(vmem_limit_bytes=25 * 2**20),
         cost_estimate=pl.CostEstimate(
             flops=16 * rows * units * depth,
             bytes_accessed=rows * depth * 6 + units * depth * (6 + (24 if last else 12)),
@@ -336,36 +322,43 @@
     there = ahead(mine, 2)
     mine, counts, x_rows, grad_rows = lax.optimization_barrier((mine, counts, x_rows, grad_rows))
     table = make_table(counts, n_dev, nblk)
+    home = [
+        lax.dynamic_slice(a.reshape(nblk, 2, -1, depth), (0, own // 2, 0, 0), (MOST, 1, BLOCK // 2, depth))
+        for a in (x_rows, grad_rows)
+    ]
     o_in, o_out = swap_dp(w_in, 2), swap_dp(w_out, 2)
-    home = lambda a: lax.dynamic_slice(
-        a[: MOST * BLOCK].reshape(MOST, 2, BLOCK // 2, depth), (0, own // 2, 0, 0), (MOST, 1, BLOCK // 2, depth)
-    )
-
-    fourth = ahead(there[nblk - 1 - MOST :], 2)
-    third = swap_pair(cut(there, table[WIN + SPAN + 3] - 1))
-    third = ahead(third, 2, parity=1)
+
+    third = cut(there, table[WIN + SPAN + 3] - 1)
     first = jnp.where(table[ODD] == 1, cut(mine, table[WIN + 1] - 1), cut(there, table[WIN + SPAN + 1] - 1))
+    second = cut(there, table[WIN + SPAN + 2] - 1)
+    fourth = there[nblk - 1 - MOST :]
+    third = ahead(third, 1)
     first = swap_pair(first)
-    second = cut(there, table[WIN + SPAN + 2] - 1)
+    fourth = ahead(fourth, 2)
+
+    def pair(a):
+        return a, swap_dp(a, 1)
+
     shares = (w_in, w_out, o_in, o_out)
-    pair = lambda a: (a, swap_dp(a, 1))
-    sum_in, sum_out, give, keep = expert(
-        table, (0, 2, 4), (home(x_rows), home(grad_rows)), [pair(second), pair(fourth)], shares, None
-    )
+    pieces = [pair(second), pair(third)]
+    sum_in, sum_out, give, keep = expert(table, (0, 2, 3), home, pieces, shares, None)
     here, there = add_cores(give, keep, 3)
     sum_in, there = lax.optimization_barrier((sum_in, there))
     there = swap_dp(there, 2)
-    r0, r2, r4 = add_rows(here, there)
-    pieces = [pair(first), pair(third)]
-    own_in, own_out, far_in, far_out, give, keep = expert(table, (1, 3), (), pieces, shares, (sum_in, sum_out))
+    r0, r2, r3 = add_rows(here, there)
+    pieces = [pair(first), pair(fourth)]
+    own_in, own_out, far_in, far_out, give, keep = expert(table, (1, 4), (), pieces, shares, (sum_in, sum_out))
     here, there = add_cores(give, keep, 2)
     there = swap_dp(there, 2)
     there, far_in, far_out = lax.optimization_barrier((there, far_in, far_out))
-    r1, r3 = add_rows(here, there)
+    r1, r4 = add_rows(here, there)
     far_in, far_out = swap_dp(far_in, 2), swap_dp(far_out, 2)
+    total_in = own_in + far_in
     results = [r0] + [ahead(r, -o) for o, r in ((1, r1), (2, r2), (3, r3), (4, r4))]
+    results[1], total_in = lax.optimization_barrier((results[1], total_in))
     done = merge(table, results, nblk)
-    return (own_in + far_in)[None], (own_out + far_out)[None], done.reshape(total, -1)
+    done, far_out = lax.optimization_barrier((done, far_out))
+    return total_in[None], (own_out + far_out)[None], done.reshape(total, -1)
 
 
 def solution(mesh):

time: 204 us -> 202 us (level)
  waiting for transfers between devices: 102 us -> 114 us
  starting transfers between devices: 35.1 us -> 28.1 us
  local copies, waits for them, and re-layouts: 10.6 us -> 5.87 us
  other arithmetic: 13.5 us -> 10.6 us
    ppermute x12, waiting for transfers between devices: 19.3 us -> 53.3 us  [swap_dp(): lax.ppermute(array, 'dp', [(i, i ^ bit) for i in range(size_of('dp'))])]
    ppermute x7, waiting for transfers between devices: 82.5 us -> 57.9 us  [ahead(): lax.ppermute(array, 'blk', [((i + by) % size if moves(i) else i, i) for i...]
    ppermute x7, starting transfers between devices: 23 us -> 14.9 us  [ahead(): lax.ppermute(array, 'blk', [((i + by) % size if moves(i) else i, i) for i...]
    slice x3 -> x1, local copies, waits for them, and re-layouts: 6.94 us -> 1.5 us  [on_device(): third = cut(there, table[WIN + SPAN + 3] - 1)]
    broadcast_in_dim x2 -> x1, other arithmetic: 6.45 us -> 1.31 us  [on_device(): return (total_in[None], (own_out + far_out)[None], done.reshape(total, -1))]
    slice x1 -> x0, other arithmetic: 3.54 us -> none  [on_device(): fourth = ahead(there[nblk - 1 - MOST:], 2)]
    dynamic_slice x0 -> x1, other arithmetic: none -> 3.52 us  [cut(): return lax.dynamic_slice_in_dim(array, index, MOST, 0)]
    ppermute x2 -> x1, waiting for transfers between devices: 0.01 us -> 2.41 us  [swap_pair(): lax.ppermute(array, 'blk', [(i, i ^ 1) for i in range(size_of('blk'))])]
  transfers between devices with their start and end apart: 21 -> 20, of which waited for: 10 -> 11; matrix products, arithmetic and copies ran while one was open for 8% -> 6% of each run, Pallas kernels for 11% -> 10%
where the time goes in v1:
time: 202 us; the launch traced here: 200 us
  waiting for transfers between devices  114 us (56%)
  Pallas kernels  35 us (17%)
  starting transfers between devices  28.1 us (14%)
  other arithmetic  10.6 us (5%)
  between operations  6.62 us (3%)
  local copies, waits for them, and re-layouts  5.87 us (3%)
    ppermute x7, waiting for transfers between devices, ahead(): lax.ppermute(array, 'blk', [((i + by) % size if moves(i) else i, i) for i...  57.9 us
    ppermute x12, waiting for transfers between devices, swap_dp(): lax.ppermute(array, 'dp', [(i, i ^ bit) for i in range(size_of('dp'))])  53.3 us
    pallas_call x2, Pallas kernels, expert(): pl.pallas_call(functools.partial(expert_kernel, tuple(offsets), len(home)...  30.2 us
    ppermute x7, starting transfers between devices, ahead(): lax.ppermute(array, 'blk', [((i + by) % size if moves(i) else i, i) for i...  14.9 us
    ppermute x12, starting transfers between devices, swap_dp(): lax.ppermute(array, 'dp', [(i, i ^ bit) for i in range(size_of('dp'))])  9.03 us
    ppermute x1, starting transfers between devices, swap_pair(): lax.ppermute(array, 'blk', [(i, i ^ 1) for i in range(size_of('blk'))])  4.19 us
  transfers between devices with their start and end apart: 20, of which 11 were waited for; matrix products, arithmetic and copies ran while one was open for 6% of the time, Pallas kernels for 10%

profile of v1, /device:TPU:0, one launch (start us, length us, event | category | flops | bytes accessed | tf_op | source)
XLA Modules:
  0.0 199.7 jit_solution(17293845664163934168)
XLA Ops:
  0.6 1.6 constant_dynamic-slice_fusion.4
  3.6 5.1 %collective-permute-start = (bf16[7,2,32,2048]{3,2,1,0:T(8,128)(2,1)}, bf16[7,2,32,2048]{3,2,1,0:T(8,128)(2,1)}, u32[]{:S(2)}, u32[]{:S(2)}) collective-permute-start(bf16[7,2,32,2048]{3,2,1,0:T(8,128)(2,1)} %pad_maximum_fusion), channel_id=1, source_target_pairs={{8,0},{12,4},{16,8},{20,12},{24,16},{28,20},{0,24},{4,28},{9,1},{1... | collective-permute-start | bytes 5505032 | tf_op jit(solution)/shard_map/ppermute | solution.py:27
  8.7 1.5 collective-permute-start.5
  19.5 28.8 %collective-permute-done = bf16[7,2,32,2048]{3,2,1,0:T(8,128)(2,1)} collective-permute-done((bf16[7,2,32,2048]{3,2,1,0:T(8,128)(2,1)}, bf16[7,2,32,2048]{3,2,1,0:T(8,128)(2,1)}, u32[]{:S(2)}, u32[]{:S(2)}) %collective-permute-start) | collective-permute-done | bytes 1835040 | tf_op jit(solution)/shard_map/ppermute | solution.py:27
  48.3 3.5 %constant_dynamic-slice_fusion = (bf16[3,2,32,2048]{3,2,1,0:T(8,128)(2,1)S(1)}, bf16[3,2,32,2048]{3,2,1,0:T(8,128)(2,1)S(1)}, bf16[3,2,32,2048]{3,2,1,0:T(8,128)(2,1)}, bf16[3,2,32,2048]{3,2,1,0:T(8,128)(2,1)}) fusion(bf16[7,2,32,2048]{3,2,1,0:T(8,128)(2,1)} %collective-permute-done, s32[]{:T(128)S(6)} %select_n.42, s32[]{:T(128)S(6)} %select_n.41, ...), kind=kLoop, calls=%fused_computation.13 | loop fusion | flops 393216 | bytes 7077905 | tf_op jit(solution)/shard_map/dynamic_slice | solution.py:93
  51.8 5.2 %collective-permute-start.8 = (bf16[3,2,32,2048]{3,2,1,0:T(8,128)(2,1)S(1)}, bf16[3,2,32,2048]{3,2,1,0:T(8,128)(2,1)}, u32[]{:S(2)}, u32[]{:S(2)}) collective-permute-start(bf16[3,2,32,2048]{3,2,1,0:T(8,128)(2,1)S(1)} %get-tuple-element.51), channel_id=1, source_target_pairs={{4,0},{8,4},{12,8},{16,12},{20,16},{24,20},{28,24},{0,28},{5,1},{9... | collective-permute-start | bytes 2359304 | tf_op jit(solution)/shard_map/ppermute | solution.py:27
  58.6 14.4 %collective-permute-done.8.refs_4_ = bf16[3,2,32,2048]{3,2,1,0:T(8,128)(2,1)} collective-permute-done((bf16[3,2,32,2048]{3,2,1,0:T(8,128)(2,1)S(1)}, bf16[3,2,32,2048]{3,2,1,0:T(8,128)(2,1)}, u32[]{:S(2)}, u32[]{:S(2)}) %collective-permute-start.8) | collective-permute-done | bytes 786464 | tf_op jit(solution)/shard_map/ppermute | solution.py:27
  75.6 1.7 collective-permute-start.3
  77.3 4.2 %collective-permute-start.1 = (bf16[3,2,32,2048]{3,2,1,0:T(8,128)(2,1)S(1)}, bf16[3,2,32,2048]{3,2,1,0:T(8,128)(2,1)S(1)}, u32[]{:S(2)}, u32[]{:S(2)}) collective-permute-start(bf16[3,2,32,2048]{3,2,1,0:T(8,128)(2,1)S(1)} %copy-done.4), channel_id=1, source_target_pairs={{0,4},{4,0},{8,12},{12,8},{16,20},{20,16},{24,28},{28,24},{1,5},{5... | collective-permute-start | bytes 2359304 | tf_op jit(solution)/shard_map/ppermute | solution.py:31
  81.5 14.9 %shard_map.77 = (f32[768,2048]{1,0:T(8,128)S(1)}, f32[384,2048]{1,0:T(8,128)S(1)}, bf16[2,576,512]{2,1,0:T(8,128)(2,1)S(1)}, bf16[2,576,512]{2,1,0:T(8,128)(2,1)S(1)}) custom-call(s32[32]{0:T(128)S(1)} %copy-done, bf16[3,1,64,2048]{3,2,1,0:T(8,128)(2,1)S(1)} %constant_dynamic-slice_fusion.3.refs_0_, ...), custom_call_target="tpu_custom_call" | custom-call | flops 7247757312 | bytes 21233664 | tf_op jit(solution)/shard_map/pallas_call | solution.py:234
  97.0 2.4 %collective-permute-done.1.refs_0_ = bf16[3,2,32,2048]{3,2,1,0:T(8,128)(2,1)S(1)} collective-permute-done((bf16[3,2,32,2048]{3,2,1,0:T(8,128)(2,1)S(1)}, bf16[3,2,32,2048]{3,2,1,0:T(8,128)(2,1)S(1)}, u32[]{:S(2)}, u32[]{:S(2)}) %collective-permute-start.1) | collective-permute-done | bytes 786464 | tf_op jit(solution)/shard_map/ppermute | solution.py:31
  101.7 15.3 %shard_map.78 = (f32[2,192,2048]{2,1,0:T(8,128)S(1)}, f32[192,2048]{1,0:T(8,128)S(1)}, bf16[2,192,2048]{2,1,0:T(8,128)(2,1)S(1)}, bf16[192,2048]{1,0:T(8,128)(2,...) custom-call(s32[32]{0:T(128)S(1)} %copy-done, ...), custom_call_target="tpu_custom_call" | custom-call | flops 4831838208 | bytes 28311552 | tf_op jit(solution)/shard_map/pallas_call | solution.py:234
  117.2 2.1 %collective-permute-done.11 = bf16[2,384,512]{2,1,0:T(8,128)(2,1)S(1)} collective-permute-done((bf16[2,384,512]{2,1,0:T(8,128)(2,1)S(1)}, bf16[2,384,512]{2,1,0:T(8,128)(2,1)S(1)}, u32[]{:S(2)}, u32[]{:S(2)}) %collective-permute-start.11) | collective-permute-done | bytes 786464 | tf_op jit(solution)/shard_map/ppermute | solution.py:35
  119.5 1.6 collective-permute-start.12
  121.6 10.0 %collective-permute-done.12 = bf16[2,3,64,512]{3,2,1,0:T(8,128)(2,1)S(1)} collective-permute-done((bf16[2,3,64,512]{3,2,1,0:T(8,128)(2,1)S(1)}, bf16[2,3,64,512]{3,2,1,0:T(8,128)(2,1)S(1)}, u32[]{:S(2)}, u32[]{:S(2)}) %collective-permute-start.12) | collective-permute-done | bytes 393248 | tf_op jit(solution)/shard_map/ppermute | solution.py:35
  131.6 1.5 collective-permute-start.14
  133.1 11.1 %collective-permute-done.15 = bf16[3,3,64,512]{3,2,1,0:T(8,128)(2,1)S(1)} collective-permute-done((bf16[3,3,64,512]{3,2,1,0:T(8,128)(2,1)S(1)}, bf16[3,3,64,512]{3,2,1,0:T(8,128)(2,1)S(1)}, u32[]{:S(2)}, u32[]{:S(2)}) %collective-permute-start.15) | collective-permute-done | bytes 589856 | tf_op jit(solution)/shard_map/ppermute | solution.py:35
  144.4 1.9 collective-permute-start.17
  147.2 1.6 collective-permute-start.19
  149.7 28.2 %collective-permute-done.14 = bf16[2,192,2048]{2,1,0:T(8,128)(2,1)S(1)} collective-permute-done((bf16[2,192,2048]{2,1,0:T(8,128)(2,1)S(1)}, bf16[2,192,2048]{2,1,0:T(8,128)(2,1)S(1)}, u32[]{:S(2)}, u32[]{:S(2)}) %collective-permute-start.14) | collective-permute-done | bytes 1572896 | tf_op jit(solution)/shard_map/ppermute | solution.py:35
  177.9 2.3 %convert_add_fusion = f32[2,192,2048]{2,1,0:T(8,128)} fusion(f32[2,192,2048]{2,1,0:T(8,128)S(1)} %get-tuple-element.40, bf16[2,192,2048]{2,1,0:T(8,128)(2,1)S(1)} %collective-permute-done.14), kind=kLoop, calls=%fused_computation | loop fusion | flops 1572864 | bytes 7864320 | tf_op jit(solution)/shard_map/add | solution.py:356
  180.2 10.4 %collective-permute-done.17.refs_3_ = bf16[2,3,64,512]{3,2,1,0:T(8,128)(2,1)S(1)} collective-permute-done((bf16[2,3,64,512]{3,2,1,0:T(8,128)(2,1)S(1)}, bf16[2,3,64,512]{3,2,1,0:T(8,128)(2,1)S(1)}, u32[]{:S(2)}, u32[]{:S(2)}) %collective-permute-start.17) | collective-permute-done | bytes 393248 | tf_op jit(solution)/shard_map/ppermute | solution.py:27
  190.6 4.3 %collective-permute-done.18.refs_4_ = bf16[2,3,64,512]{3,2,1,0:T(8,128)(2,1)} collective-permute-done((bf16[2,3,64,512]{3,2,1,0:T(8,128)(2,1)S(1)}, bf16[2,3,64,512]{3,2,1,0:T(8,128)(2,1)}, u32[]{:S(2)}, u32[]{:S(2)}) %collective-permute-start.18) | collective-permute-done | bytes 393248 | tf_op jit(solution)/shard_map/ppermute | solution.py:27
  194.9 3.5 %shard_map.79 = bf16[8,128,512]{2,1,0:T(8,128)(2,1)} custom-call(s32[32]{0:T(128)} %shard_map.76.s_ref, bf16[2,3,64,512]{3,2,1,0:T(8,128)(2,1)} %pad_maximum_fusion.2.refs_0_, bf16[2,3,64,512]{3,2,1,0:T(8,128)(2,1)} %copy-done.8, bf16[2,3,64,512]{3,2,1,0:T(8,128)(2,1)} %copy-done.6, bf16[2,3,64,512]{3,2,1,0:T(8,128)(2,1)} %copy-done.7, ...), custom_call_target="tpu_custom_call" | custom-call | tf_op jit(solution)/shard_map/pallas_call | solution.py:292
  (61 shorter events, 16.1 us)
Async XLA Ops:
  3.6 44.7 %collective-permute-start = (bf16[7,2,32,2048]{3,2,1,0:T(8,128)(2,1)}, bf16[7,2,32,2048]{3,2,1,0:T(8,128)(2,1)}, u32[]{:S(2)}, u32[]{:S(2)}) collective-permute-start(bf16[7,2,32,2048]{3,2,1,0:T(8,128)(2,1)} %pad_maximum_fusion), channel_id=1, source_target_pairs={{8,0},{12,4},{16,8},{20,12},{24,16},{28,20},{0,24},{4,28},{9,1},{1... | collective-permute-start | bytes 5505032 | tf_op jit(solution)/shard_map/ppermute | solution.py:27
  8.7 72.7 %collective-permute-start.5 = (bf16[2,192,2048]{2,1,0:T(8,128)(2,1)S(1)}, bf16[2,192,2048]{2,1,0:T(8,128)(2,1)}, u32[]{:S(2)}, u32[]{:S(2)}) collective-permute-start(bf16[2,192,2048]{2,1,0:T(8,128)(2,1)S(1)} %bitcast.28), channel_id=1, source_target_pairs={{0,2},{1,3},{2,0},{3,1},{4,6},{5,7},{6,4},{7,5},{8,10},{9,11},{10,... | collective-permute-start | bytes 4718600 | tf_op jit(solution)/shard_map/ppermute | solution.py:35
  48.3 8.7 %copy-start.2 = (bf16[1,192,2048]{2,1,0:T(8,128)(2,1)S(1)}, bf16[1,192,2048]{2,1,0:T(8,128)(2,1)}, u32[]{:S(2)}) copy-start(bf16[1,192,2048]{2,1,0:T(8,128)(2,1)} %param.8) | copy-start | bytes 2359300
  51.8 21.2 %collective-permute-start.8 = (bf16[3,2,32,2048]{3,2,1,0:T(8,128)(2,1)S(1)}, bf16[3,2,32,2048]{3,2,1,0:T(8,128)(2,1)}, u32[]{:S(2)}, u32[]{:S(2)}) collective-permute-start(bf16[3,2,32,2048]{3,2,1,0:T(8,128)(2,1)S(1)} %get-tuple-element.51), channel_id=1, source_target_pairs={{4,0},{8,4},{12,8},{16,12},{20,16},{24,20},{28,24},{0,28},{5,1},{9... | collective-permute-start | bytes 2359304 | tf_op jit(solution)/shard_map/ppermute | solution.py:27
  57.0 20.2 %collective-permute-start.6 = (bf16[192,2048]{1,0:T(8,128)(2,1)S(1)}, bf16[192,2048]{1,0:T(8,128)(2,1)}, u32[]{:S(2)}, u32[]{:S(2)}) collective-permute-start(bf16[192,2048]{1,0:T(8,128)(2,1)S(1)} %bitcast.31), channel_id=1, source_target_pairs={{0,2},{1,3},{2,0},{3,1},{4,6},{5,7},{6,4},{7,5},{8,10},{9,11},{10,... | collective-permute-start | bytes 2359304 | tf_op jit(solution)/shard_map/ppermute | solution.py:35
  58.6 22.9 %collective-permute-start.7 = (bf16[3,2,32,2048]{3,2,1,0:T(8,128)(2,1)S(1)}, bf16[3,2,32,2048]{3,2,1,0:T(8,128)(2,1)}, u32[]{:S(2)}, u32[]{:S(2)}) collective-permute-start(bf16[3,2,32,2048]{3,2,1,0:T(8,128)(2,1)S(1)} %get-tuple-element.52.refs_2_), channel_id=1, source_target_pairs={{0,1},{1,0},{2,3},{3,2},{4,5},{5,4},{6,7},{7,6},{8,9},{9,8},{10,11... | collective-permute-start | bytes 2359304 | tf_op jit(solution)/shard_map/ppermute | solution.py:35
  73.0 8.5 %collective-permute-start.9 = (bf16[3,2,32,2048]{3,2,1,0:T(8,128)(2,1)}, bf16[3,2,32,2048]{3,2,1,0:T(8,128)(2,1)}, u32[]{:S(2)}, u32[]{:S(2)}) collective-permute-start(bf16[3,2,32,2048]{3,2,1,0:T(8,128)(2,1)} %collective-permute-done.8.refs_4_), channel_id=1, source_target_pairs={{0,1},{1,0},{2,3},{3,2},{4,5},{5,4},{6,7},{7,6},{8,9},{9,8},{10,11... | collective-permute-start | bytes 2359304 | tf_op jit(solution)/shard_map/ppermute | solution.py:35
  73.0 8.5 %copy-start = (s32[32]{0:T(128)S(1)}, s32[32]{0:T(128)}, u32[]{:S(2)}) copy-start(s32[32]{0:T(128)} %shard_map.76.s_ref) | copy-start | bytes 388
  75.6 20.9 %collective-permute-start.3 = (bf16[3,2,32,2048]{3,2,1,0:T(8,128)(2,1)S(1)}, bf16[3,2,32,2048]{3,2,1,0:T(8,128)(2,1)S(1)}, u32[]{:S(2)}, u32[]{:S(2)}) collective-permute-start(bf16[3,2,32,2048]{3,2,1,0:T(8,128)(2,1)S(1)} %copy-done.5), channel_id=1, source_target_pairs={{8,0},{12,4},{16,8},{20,12},{24,16},{28,20},{0,24},{4,28},{9,1},{1... | collective-permute-start | bytes 2359304 | tf_op jit(solution)/shard_map/ppermute | solution.py:27
  77.3 22.1 %collective-permute-start.1 = (bf16[3,2,32,2048]{3,2,1,0:T(8,128)(2,1)S(1)}, bf16[3,2,32,2048]{3,2,1,0:T(8,128)(2,1)S(1)}, u32[]{:S(2)}, u32[]{:S(2)}) collective-permute-start(bf16[3,2,32,2048]{3,2,1,0:T(8,128)(2,1)S(1)} %copy-done.4), channel_id=1, source_target_pairs={{0,4},{4,0},{8,12},{12,8},{16,20},{20,16},{24,28},{28,24},{1,5},{5... | collective-permute-start | bytes 2359304 | tf_op jit(solution)/shard_map/ppermute | solution.py:31
  96.4 3.0 %collective-permute-start.10 = (bf16[2,576,512]{2,1,0:T(8,128)(2,1)S(1)}, bf16[2,576,512]{2,1,0:T(8,128)(2,1)S(1)}, u32[]{:S(2)}, u32[]{:S(2)}) collective-permute-start(bf16[2,576,512]{2,1,0:T(8,128)(2,1)S(1)} %get-tuple-element.32), channel_id=1, source_target_pairs={{0,1},{1,0},{2,3},{3,2},{4,5},{5,4},{6,7},{7,6},{8,9},{9,8},{10,11... | collective-permute-start | bytes 3538952 | tf_op jit(solution)/shard_map/ppermute | solution.py:35
  96.5 3.9 %collective-permute-start.4 = (bf16[3,2,32,2048]{3,2,1,0:T(8,128)(2,1)S(1)}, bf16[3,2,32,2048]{3,2,1,0:T(8,128)(2,1)S(1)}, u32[]{:S(2)}, u32[]{:S(2)}) collective-permute-start(bf16[3,2,32,2048]{3,2,1,0:T(8,128)(2,1)S(1)} %collective-permute-done.3.refs_2_), channel_id=1, source_target_pairs={{0,1},{1,0},{2,3},{3,2},{4,5},{5,4},{6,7},{7,6},{8,9},{9,8},{10,11... | collective-permute-start | bytes 2359304 | tf_op jit(solution)/shard_map/ppermute | solution.py:35
  99.4 2.3 %collective-permute-start.2 = (bf16[3,2,32,2048]{3,2,1,0:T(8,128)(2,1)S(1)}, bf16[3,2,32,2048]{3,2,1,0:T(8,128)(2,1)S(1)}, u32[]{:S(2)}, u32[]{:S(2)}) collective-permute-start(bf16[3,2,32,2048]{3,2,1,0:T(8,128)(2,1)S(1)} %collective-permute-done.1.refs_0_), channel_id=1, source_target_pairs={{0,1},{1,0},{2,3},{3,2},{4,5},{5,4},{6,7},{7,6},{8,9},{9,8},{10,11... | collective-permute-start | bytes 2359304 | tf_op jit(solution)/shard_map/ppermute | solution.py:35
  116.9 2.4 %collective-permute-start.11 = (bf16[2,384,512]{2,1,0:T(8,128)(2,1)S(1)}, bf16[2,384,512]{2,1,0:T(8,128)(2,1)S(1)}, u32[]{:S(2)}, u32[]{:S(2)}) collective-permute-start(bf16[2,384,512]{2,1,0:T(8,128)(2,1)S(1)} %get-tuple-element.36), channel_id=1, source_target_pairs={{0,1},{1,0},{2,3},{3,2},{4,5},{5,4},{6,7},{7,6},{8,9},{9,8},{10,11... | collective-permute-start | bytes 2359304 | tf_op jit(solution)/shard_map/ppermute | solution.py:35
  119.5 12.1 %collective-permute-start.12 = (bf16[2,3,64,512]{3,2,1,0:T(8,128)(2,1)S(1)}, bf16[2,3,64,512]{3,2,1,0:T(8,128)(2,1)S(1)}, u32[]{:S(2)}, u32[]{:S(2)}) collective-permute-start(bf16[2,3,64,512]{3,2,1,0:T(8,128)(2,1)S(1)} %bitcast.46), channel_id=1, source_target_pairs={{0,2},{1,3},{2,0},{3,1},{4,6},{5,7},{6,4},{7,5},{8,10},{9,11},{10,... | collective-permute-start | bytes 1179656 | tf_op jit(solution)/shard_map/ppermute | solution.py:35
  121.1 23.1 %collective-permute-start.15 = (bf16[3,3,64,512]{3,2,1,0:T(8,128)(2,1)S(1)}, bf16[3,3,64,512]{3,2,1,0:T(8,128)(2,1)S(1)}, u32[]{:S(2)}, u32[]{:S(2)}) collective-permute-start(bf16[3,3,64,512]{3,2,1,0:T(8,128)(2,1)S(1)} %bitcast.45), channel_id=1, source_target_pairs={{0,2},{1,3},{2,0},{3,1},{4,6},{5,7},{6,4},{7,5},{8,10},{9,11},{10,... | collective-permute-start | bytes 1769480 | tf_op jit(solution)/shard_map/ppermute | solution.py:35
  131.6 46.3 %collective-permute-start.14 = (bf16[2,192,2048]{2,1,0:T(8,128)(2,1)S(1)}, bf16[2,192,2048]{2,1,0:T(8,128)(2,1)S(1)}, u32[]{:S(2)}, u32[]{:S(2)}) collective-permute-start(bf16[2,192,2048]{2,1,0:T(8,128)(2,1)S(1)} %get-tuple-element.41), channel_id=1, source_target_pairs={{0,2},{1,3},{2,0},{3,1},{4,6},{5,7},{6,4},{7,5},{8,10},{9,11},{10,... | collective-permute-start | bytes 4718600 | tf_op jit(solution)/shard_map/ppermute | solution.py:35
  144.3 35.9 %collective-permute-start.16 = (bf16[2,3,64,512]{3,2,1,0:T(8,128)(2,1)S(1)}, bf16[2,3,64,512]{3,2,1,0:T(8,128)(2,1)S(1)}, u32[]{:S(2)}, u32[]{:S(2)}) collective-permute-start(bf16[2,3,64,512]{3,2,1,0:T(8,128)(2,1)S(1)} %pad_maximum_fusion.3), channel_id=1, source_target_pairs={{24,0},{28,4},{0,8},{4,12},{8,16},{12,20},{16,24},{20,28},{25,1},{... | collective-permute-start | bytes 1179656 | tf_op jit(solution)/shard_map/ppermute | solution.py:27
  144.4 46.2 %collective-permute-start.17 = (bf16[2,3,64,512]{3,2,1,0:T(8,128)(2,1)S(1)}, bf16[2,3,64,512]{3,2,1,0:T(8,128)(2,1)S(1)}, u32[]{:S(2)}, u32[]{:S(2)}) collective-permute-start(bf16[2,3,64,512]{3,2,1,0:T(8,128)(2,1)S(1)} %pad_maximum_fusion.4), channel_id=1, source_target_pairs={{20,0},{24,4},{28,8},{0,12},{4,16},{8,20},{12,24},{16,28},{21,1},{... | collective-permute-start | bytes 1179656 | tf_op jit(solution)/shard_map/ppermute | solution.py:27
  147.2 51.2 %collective-permute-start.19 = (bf16[192,2048]{1,0:T(8,128)(2,1)}, bf16[192,2048]{1,0:T(8,128)(2,1)S(1)}, u32[]{:S(2)}, u32[]{:S(2)}) collective-permute-start(bf16[192,2048]{1,0:T(8,128)(2,1)} %get-tuple-element.46), channel_id=1, source_target_pairs={{0,2},{1,3},{2,0},{3,1},{4,6},{5,7},{6,4},{7,5},{8,10},{9,11},{10,... | collective-permute-start | bytes 2359304 | tf_op jit(solution)/shard_map/ppermute | solution.py:35
  148.8 31.4 %collective-permute-start.13 = (bf16[2,3,64,512]{3,2,1,0:T(8,128)(2,1)S(1)}, bf16[2,3,64,512]{3,2,1,0:T(8,128)(2,1)S(1)}, u32[]{:S(2)}, u32[]{:S(2)}) collective-permute-start(bf16[2,3,64,512]{3,2,1,0:T(8,128)(2,1)S(1)} %pad_maximum_fusion.1), channel_id=1, source_target_pairs={{28,0},{0,4},{4,8},{8,12},{12,16},{16,20},{20,24},{24,28},{29,1},{... | collective-permute-start | bytes 1179656 | tf_op jit(solution)/shard_map/ppermute | solution.py:27
  177.9 17.0 %collective-permute-start.18 = (bf16[2,3,64,512]{3,2,1,0:T(8,128)(2,1)S(1)}, bf16[2,3,64,512]{3,2,1,0:T(8,128)(2,1)}, u32[]{:S(2)}, u32[]{:S(2)}) collective-permute-start(bf16[2,3,64,512]{3,2,1,0:T(8,128)(2,1)S(1)} %pad_maximum_fusion.5), channel_id=1, source_target_pairs={{16,0},{20,4},{24,8},{28,12},{0,16},{4,20},{8,24},{12,28},{17,1},{... | collective-permute-start | bytes 1179656 | tf_op jit(solution)/shard_map/ppermute | solution.py:27
  180.2 14.7 %copy-start.8 = (bf16[2,3,64,512]{3,2,1,0:T(8,128)(2,1)}, bf16[2,3,64,512]{3,2,1,0:T(8,128)(2,1)S(1)}, u32[]{:S(2)}) copy-start(bf16[2,3,64,512]{3,2,1,0:T(8,128)(2,1)S(1)} %collective-permute-done.13.refs_1_) | copy-start | bytes 1179652
  180.2 14.7 %copy-start.6 = (bf16[2,3,64,512]{3,2,1,0:T(8,128)(2,1)}, bf16[2,3,64,512]{3,2,1,0:T(8,128)(2,1)S(1)}, u32[]{:S(2)}) copy-start(bf16[2,3,64,512]{3,2,1,0:T(8,128)(2,1)S(1)} %collective-permute-done.16.refs_2_) | copy-start | bytes 1179652
  (6 other events, 27.9 us)

commit v2 on v1

--- a/solution.py
+++ b/solution.py
@@ -318,23 +318,29 @@
     def quarter(first, end):
         return jnp.concatenate([pick(x_rows, first, end), pick(grad_rows, first, end)], axis=1)
 
-    mine = quarter(1, nblk)
-    there = ahead(mine, 2)
-    mine, counts, x_rows, grad_rows = lax.optimization_barrier((mine, counts, x_rows, grad_rows))
+    my_wide = quarter(MOST, nblk)
+    wide = ahead(my_wide, 2)
+    my_wide, counts, x_rows, grad_rows = lax.optimization_barrier((my_wide, counts, x_rows, grad_rows))
+    my_narrow = quarter(1, MOST)
+    narrow = ahead(my_narrow, 2)
     table = make_table(counts, n_dev, nblk)
     home = [
         lax.dynamic_slice(a.reshape(nblk, 2, -1, depth), (0, own // 2, 0, 0), (MOST, 1, BLOCK // 2, depth))
         for a in (x_rows, grad_rows)
     ]
-    o_in, o_out = swap_dp(w_in, 2), swap_dp(w_out, 2)
-
-    third = cut(there, table[WIN + SPAN + 3] - 1)
-    first = jnp.where(table[ODD] == 1, cut(mine, table[WIN + 1] - 1), cut(there, table[WIN + SPAN + 1] - 1))
+    mine = quarter(1, nblk)
+    mine = cut(mine, table[WIN + 1] - 1)
+    o_in = swap_dp(w_in, 2)
+    o_out = swap_dp(w_out, 2)
+
+    third = cut(wide, table[WIN + SPAN + 3] - MOST)
+    fourth = wide[nblk - 2 * MOST :]
+    third = ahead(third, 1)
+    fourth = ahead(fourth, 2)
+    there = jnp.concatenate([narrow, wide])
+    first = jnp.where(table[ODD] == 1, mine, cut(there, table[WIN + SPAN + 1] - 1))
     second = cut(there, table[WIN + SPAN + 2] - 1)
-    fourth = there[nblk - 1 - MOST :]
-    third = ahead(third, 1)
     first = swap_pair(first)
-    fourth = ahead(fourth, 2)
 
     def pair(a):
         return a, swap_dp(a, 1)
@@ -348,17 +354,16 @@
     r0, r2, r3 = add_rows(here, there)
     pieces = [pair(first), pair(fourth)]
     own_in, own_out, far_in, far_out, give, keep = expert(table, (1, 4), (), pieces, shares, (sum_in, sum_out))
+    far_out = swap_dp(far_out, 2)
     here, there = add_cores(give, keep, 2)
     there = swap_dp(there, 2)
-    there, far_in, far_out = lax.optimization_barrier((there, far_in, far_out))
     r1, r4 = add_rows(here, there)
-    far_in, far_out = swap_dp(far_in, 2), swap_dp(far_out, 2)
-    total_in = own_in + far_in
-    results = [r0] + [ahead(r, -o) for o, r in ((1, r1), (2, r2), (3, r3), (4, r4))]
-    results[1], total_in = lax.optimization_barrier((results[1], total_in))
-    done = merge(table, results, nblk)
-    done, far_out = lax.optimization_barrier((done, far_out))
-    return total_in[None], (own_out + far_out)[None], done.reshape(total, -1)
+    far_in = swap_dp(far_in, 2)
+    r2, r3 = ahead(r2, -2), ahead(r3, -3)
+    r1, r4 = ahead(r1, -1), ahead(r4, -4)
+    done = merge(table, [r0, r1, r2, r3, r4], nblk)
+    done, far_in = lax.optimization_barrier((done, far_in))
+    return (own_in + far_in)[None], (own_out + far_out)[None], done.reshape(total, -1)
 
 
 def solution(mesh):

time: 202 us -> 206 us (1.020)
  the two profiles are of different devices: /device:TPU:0 before, /device:TPU:6 now
where the time goes in v2:
time: 206 us; the launch traced here: 205 us
  waiting for transfers between devices  123 us (60%)
  Pallas kernels  34.9 us (17%)
  starting transfers between devices  17.3 us (8%)
  local copies, waits for them, and re-layouts  14.2 us (7%)
  other arithmetic  9.21 us (4%)
  between operations  6.59 us (3%)
    ppermute x8, waiting for transfers between devices, ahead(): lax.ppermute(array, 'blk', [((i + by) % size if moves(i) else i, i) for i...  62.1 us
    ppermute x12, waiting for transfers between devices, swap_dp(): lax.ppermute(array, 'dp', [(i, i ^ bit) for i in range(size_of('dp'))])  58.8 us
    pallas_call x2, Pallas kernels, expert(): pl.pallas_call(functools.partial(expert_kernel, tuple(offsets), len(home)...  30.1 us
    ppermute x8, starting transfers between devices, ahead(): lax.ppermute(array, 'blk', [((i + by) % size if moves(i) else i, i) for i...  11.6 us
    dynamic_slice x4, local copies, waits for them, and re-layouts, pick(): lax.dynamic_slice(array, (first, own, 0, 0), (end - first, 1, part, depth))  6.25 us
    ppermute x12, starting transfers between devices, swap_dp(): lax.ppermute(array, 'dp', [(i, i ^ bit) for i in range(size_of('dp'))])  5.68 us
  transfers between devices with their start and end apart: 21, of which 8 were waited for; matrix products, arithmetic and copies ran while one was open for 8% of the time, Pallas kernels for 17%

profile of v2, /device:TPU:6, one launch (start us, length us, event | category | flops | bytes accessed | tf_op | source)
XLA Modules:
  0.0 205.2 jit_solution(12411598683258091193)
XLA Ops:
  3.0 1.2 pad_maximum_fusion
  4.1 3.6 %collective-permute-start.1 = (bf16[5,2,32,2048]{3,2,1,0:T(8,128)(2,1)}, bf16[5,2,32,2048]{3,2,1,0:T(8,128)(2,1)}, u32[]{:S(2)}, u32[]{:S(2)}) collective-permute-start(bf16[5,2,32,2048]{3,2,1,0:T(8,128)(2,1)} %pad_maximum_fusion), channel_id=1, source_target_pairs={{8,0},{12,4},{16,8},{20,12},{24,16},{28,20},{0,24},{4,28},{9,1},{1... | collective-permute-start | bytes 3932168 | tf_op jit(solution)/shard_map/ppermute | solution.py:27
  9.9 1.5 collective-permute-start.6
  12.1 1.3 shard_map.76.s_ref
  13.4 1.5 fusion.6
  16.2 21.0 %collective-permute-done.1 = bf16[5,2,32,2048]{3,2,1,0:T(8,128)(2,1)} collective-permute-done((bf16[5,2,32,2048]{3,2,1,0:T(8,128)(2,1)}, bf16[5,2,32,2048]{3,2,1,0:T(8,128)(2,1)}, u32[]{:S(2)}, u32[]{:S(2)}) %collective-permute-start.1) | collective-permute-done | bytes 1310752 | tf_op jit(solution)/shard_map/ppermute | solution.py:27
  37.2 2.7 %constant_dynamic-slice_fusion = (bf16[3,2,32,2048]{3,2,1,0:T(8,128)(2,1)}, bf16[3,2,32,2048]{3,2,1,0:T(8,128)(2,1)}) fusion(bf16[5,2,32,2048]{3,2,1,0:T(8,128)(2,1)} %collective-permute-done.1, s32[]{:T(128)S(6)} %select_n.46), kind=kLoop, calls=%fused_computation.19 | loop fusion | bytes 3145732 | tf_op jit(solution)/shard_map/dynamic_slice | solution.py:93
  40.4 2.9 %constant_dynamic-slice_fusion.6 = (bf16[7,1,32,2048]{3,2,1,0:T(8,128)(2,1)}, bf16[7,1,32,2048]{3,2,1,0:T(8,128)(2,1)}) fusion(bf16[8,4,32,2048]{3,2,1,0:T(8,128)(2,1)} %bitcast.39, s32[]{:T(128)S(6)} %select_n.38, bf16[8,4,32,2048]{3,2,1,0:T(8,128)(2,1)} %bitcast.43), kind=kLoop, calls=%fused_computation.25 | loop fusion | bytes 3670020 | tf_op jit(solution)/shard_map/dynamic_slice | solution.py:316
  47.8 1.5 constant_dynamic-update-slice_fusion
  50.6 12.4 %collective-permute-done.9.refs_4_ = bf16[3,2,32,2048]{3,2,1,0:T(8,128)(2,1)} collective-permute-done((bf16[3,2,32,2048]{3,2,1,0:T(8,128)(2,1)}, bf16[3,2,32,2048]{3,2,1,0:T(8,128)(2,1)}, u32[]{:S(2)}, u32[]{:S(2)}) %collective-permute-start.9) | collective-permute-done | bytes 786464 | tf_op jit(solution)/shard_map/ppermute | solution.py:27
  63.0 1.7 constant_dynamic-slice_fusion.2
  64.7 5.5 %collective-permute-start.4 = (bf16[3,2,32,2048]{3,2,1,0:T(8,128)(2,1)S(1)}, bf16[3,2,32,2048]{3,2,1,0:T(8,128)(2,1)S(1)}, u32[]{:S(2)}, u32[]{:S(2)}) collective-permute-start(bf16[3,2,32,2048]{3,2,1,0:T(8,128)(2,1)S(1)} %copy-done.8), channel_id=1, source_target_pairs={{8,0},{12,4},{16,8},{20,12},{24,16},{28,20},{0,24},{4,28},{9,1},{1... | collective-permute-start | bytes 2359304 | tf_op jit(solution)/shard_map/ppermute | solution.py:27
  70.2 14.8 %shard_map.77 = (f32[768,2048]{1,0:T(8,128)S(1)}, f32[384,2048]{1,0:T(8,128)S(1)}, bf16[2,576,512]{2,1,0:T(8,128)(2,1)S(1)}, bf16[2,576,512]{2,1,0:T(8,128)(2,1)S(1)}) custom-call(s32[32]{0:T(128)S(1)} %copy-done, bf16[3,1,64,2048]{3,2,1,0:T(8,128)(2,1)S(1)} %get-tuple-element.65.refs_0_, bf16[3,1,64,2048]{3,2,1,0:T(8,128)(2,1)S(1)} %get-tuple-element.64.refs_1_, ...), custom_call_target="tpu_custom_call" | custom-call | flops 7247757312 | bytes 21233664 | tf_op jit(solution)/shard_map/pallas_call | solution.py:234
  85.3 2.3 %collective-permute-done.4.refs_2_ = bf16[3,2,32,2048]{3,2,1,0:T(8,128)(2,1)S(1)} collective-permute-done((bf16[3,2,32,2048]{3,2,1,0:T(8,128)(2,1)S(1)}, bf16[3,2,32,2048]{3,2,1,0:T(8,128)(2,1)S(1)}, u32[]{:S(2)}, u32[]{:S(2)}) %collective-permute-start.4) | collective-permute-done | bytes 786464 | tf_op jit(solution)/shard_map/ppermute | solution.py:27
  87.6 2.2 %collective-permute-done.2.refs_0_ = bf16[3,2,32,2048]{3,2,1,0:T(8,128)(2,1)S(1)} collective-permute-done((bf16[3,2,32,2048]{3,2,1,0:T(8,128)(2,1)S(1)}, bf16[3,2,32,2048]{3,2,1,0:T(8,128)(2,1)S(1)}, u32[]{:S(2)}, u32[]{:S(2)}) %collective-permute-start.2) | collective-permute-done | bytes 786464 | tf_op jit(solution)/shard_map/ppermute | solution.py:31
  90.8 1.3 collective-permute-done.3.refs_1_
  92.1 15.3 %shard_map.78 = (f32[2,192,2048]{2,1,0:T(8,128)S(1)}, f32[192,2048]{1,0:T(8,128)S(1)}, bf16[2,192,2048]{2,1,0:T(8,128)(2,1)}, bf16[192,2048]{1,0:T(8,128)(2,1)S(...) custom-call(s32[32]{0:T(128)S(1)} %copy-done, ...), custom_call_target="tpu_custom_call" | custom-call | flops 4831838208 | bytes 28311552 | tf_op jit(solution)/shard_map/pallas_call | solution.py:234
  108.1 1.5 collective-permute-start.19
  112.2 57.4 %collective-permute-done.14 = bf16[2,3,64,512]{3,2,1,0:T(8,128)(2,1)S(1)} collective-permute-done((bf16[2,3,64,512]{3,2,1,0:T(8,128)(2,1)S(1)}, bf16[2,3,64,512]{3,2,1,0:T(8,128)(2,1)S(1)}, u32[]{:S(2)}, u32[]{:S(2)}) %collective-permute-start.14) | collective-permute-done | bytes 393248 | tf_op jit(solution)/shard_map/ppermute | solution.py:35
  170.4 1.4 add_bitcast_fusion.1
  171.8 8.5 %collective-permute-done.15.refs_1_ = bf16[2,3,64,512]{3,2,1,0:T(8,128)(2,1)} collective-permute-done((bf16[2,3,64,512]{3,2,1,0:T(8,128)(2,1)S(1)}, bf16[2,3,64,512]{3,2,1,0:T(8,128)(2,1)}, u32[]{:S(2)}, u32[]{:S(2)}) %collective-permute-start.15) | collective-permute-done | bytes 393248 | tf_op jit(solution)/shard_map/ppermute | solution.py:27
  180.3 17.9 %collective-permute-done.18.refs_4_ = bf16[2,3,64,512]{3,2,1,0:T(8,128)(2,1)} collective-permute-done((bf16[2,3,64,512]{3,2,1,0:T(8,128)(2,1)S(1)}, bf16[2,3,64,512]{3,2,1,0:T(8,128)(2,1)}, u32[]{:S(2)}, u32[]{:S(2)}) %collective-permute-start.18) | collective-permute-done | bytes 393248 | tf_op jit(solution)/shard_map/ppermute | solution.py:27
  198.2 3.5 %shard_map.79 = bf16[8,128,512]{2,1,0:T(8,128)(2,1)} custom-call(s32[32]{0:T(128)} %shard_map.76.s_ref, bf16[2,3,64,512]{3,2,1,0:T(8,128)(2,1)} %pad_maximum_fusion.2.refs_0_, bf16[2,3,64,512]{3,2,1,0:T(8,128)(2,1)} %collective-permute-done.15.refs_1_, bf16[2,3,64,512]{3,2,1,0:T(8,128)(2,1)} %copy-done.9, ...), custom_call_target="tpu_custom_call" | custom-call | tf_op jit(solution)/shard_map/pallas_call | solution.py:292
  201.7 3.5 %add_bitcast_fusion = f32[1,2,192,2048]{3,2,1,0:T(8,128)} fusion(f32[2,192,2048]{2,1,0:T(8,128)S(1)} %get-tuple-element.28, bf16[2,192,2048]{2,1,0:T(8,128)(2,1)} %collective-permute-done.19), kind=kLoop, calls=%fused_computation | loop fusion | flops 1572864 | bytes 7864320 | tf_op jit(solution)/shard_map/broadcast_in_dim | solution.py:366
  (71 shorter events, 12.3 us)
Async XLA Ops:
  4.1 7.3 %copy-start.10 = (s32[8,5]{1,0:T(8,128)S(1)}, s32[8,5]{1,0:T(8,128)}, u32[]{:S(2)}) copy-start(s32[8,5]{1,0:T(8,128)} %param.9) | copy-start | bytes 484
  4.1 33.1 %collective-permute-start.1 = (bf16[5,2,32,2048]{3,2,1,0:T(8,128)(2,1)}, bf16[5,2,32,2048]{3,2,1,0:T(8,128)(2,1)}, u32[]{:S(2)}, u32[]{:S(2)}) collective-permute-start(bf16[5,2,32,2048]{3,2,1,0:T(8,128)(2,1)} %pad_maximum_fusion), channel_id=1, source_target_pairs={{8,0},{12,4},{16,8},{20,12},{24,16},{28,20},{0,24},{4,28},{9,1},{1... | collective-permute-start | bytes 3932168 | tf_op jit(solution)/shard_map/ppermute | solution.py:27
  8.9 38.8 %collective-permute-start = (bf16[2,2,32,2048]{3,2,1,0:T(8,128)(2,1)S(1)}, bf16[2,2,32,2048]{3,2,1,0:T(8,128)(2,1)S(1)}, u32[]{:S(2)}, u32[]{:S(2)}) collective-permute-start(bf16[2,2,32,2048]{3,2,1,0:T(8,128)(2,1)S(1)} %pad_maximum_fusion.1), channel_id=1, source_target_pairs={{8,0},{12,4},{16,8},{20,12},{24,16},{28,20},{0,24},{4,28},{9,1},{1... | collective-permute-start | bytes 1572872 | tf_op jit(solution)/shard_map/ppermute | solution.py:27
  9.4 60.8 %collective-permute-start.7 = (bf16[192,2048]{1,0:T(8,128)(2,1)S(1)}, bf16[192,2048]{1,0:T(8,128)(2,1)}, u32[]{:S(2)}, u32[]{:S(2)}) collective-permute-start(bf16[192,2048]{1,0:T(8,128)(2,1)S(1)} %bitcast.34), channel_id=1, source_target_pairs={{0,2},{1,3},{2,0},{3,1},{4,6},{5,7},{6,4},{7,5},{8,10},{9,11},{10,... | collective-permute-start | bytes 2359304 | tf_op jit(solution)/shard_map/ppermute | solution.py:35
  9.9 60.3 %collective-permute-start.6 = (bf16[2,192,2048]{2,1,0:T(8,128)(2,1)S(1)}, bf16[2,192,2048]{2,1,0:T(8,128)(2,1)}, u32[]{:S(2)}, u32[]{:S(2)}) collective-permute-start(bf16[2,192,2048]{2,1,0:T(8,128)(2,1)S(1)} %bitcast.31), channel_id=1, source_target_pairs={{0,2},{1,3},{2,0},{3,1},{4,6},{5,7},{6,4},{7,5},{8,10},{9,11},{10,... | collective-permute-start | bytes 4718600 | tf_op jit(solution)/shard_map/ppermute | solution.py:35
  39.9 23.1 %collective-permute-start.9 = (bf16[3,2,32,2048]{3,2,1,0:T(8,128)(2,1)}, bf16[3,2,32,2048]{3,2,1,0:T(8,128)(2,1)}, u32[]{:S(2)}, u32[]{:S(2)}) collective-permute-start(bf16[3,2,32,2048]{3,2,1,0:T(8,128)(2,1)} %get-tuple-element.43), channel_id=1, source_target_pairs={{4,0},{8,4},{12,8},{16,12},{20,16},{24,20},{28,24},{0,28},{5,1},{9... | collective-permute-start | bytes 2359304 | tf_op jit(solution)/shard_map/ppermute | solution.py:27
  50.6 19.6 %collective-permute-start.8 = (bf16[3,2,32,2048]{3,2,1,0:T(8,128)(2,1)S(1)}, bf16[3,2,32,2048]{3,2,1,0:T(8,128)(2,1)}, u32[]{:S(2)}, u32[]{:S(2)}) collective-permute-start(bf16[3,2,32,2048]{3,2,1,0:T(8,128)(2,1)S(1)} %get-tuple-element.39.refs_2_), channel_id=1, source_target_pairs={{0,1},{1,0},{2,3},{3,2},{4,5},{5,4},{6,7},{7,6},{8,9},{9,8},{10,11... | collective-permute-start | bytes 2359304 | tf_op jit(solution)/shard_map/ppermute | solution.py:35
  63.0 7.2 %collective-permute-start.10 = (bf16[3,2,32,2048]{3,2,1,0:T(8,128)(2,1)}, bf16[3,2,32,2048]{3,2,1,0:T(8,128)(2,1)}, u32[]{:S(2)}, u32[]{:S(2)}) collective-permute-start(bf16[3,2,32,2048]{3,2,1,0:T(8,128)(2,1)} %collective-permute-done.9.refs_4_), channel_id=1, source_target_pairs={{0,1},{1,0},{2,3},{3,2},{4,5},{5,4},{6,7},{7,6},{8,9},{9,8},{10,11... | collective-permute-start | bytes 2359304 | tf_op jit(solution)/shard_map/ppermute | solution.py:35
  63.0 7.2 %copy-start = (s32[32]{0:T(128)S(1)}, s32[32]{0:T(128)}, u32[]{:S(2)}) copy-start(s32[32]{0:T(128)} %shard_map.76.s_ref) | copy-start | bytes 388
  64.7 22.9 %collective-permute-start.4 = (bf16[3,2,32,2048]{3,2,1,0:T(8,128)(2,1)S(1)}, bf16[3,2,32,2048]{3,2,1,0:T(8,128)(2,1)S(1)}, u32[]{:S(2)}, u32[]{:S(2)}) collective-permute-start(bf16[3,2,32,2048]{3,2,1,0:T(8,128)(2,1)S(1)} %copy-done.8), channel_id=1, source_target_pairs={{8,0},{12,4},{16,8},{20,12},{24,16},{28,20},{0,24},{4,28},{9,1},{1... | collective-permute-start | bytes 2359304 | tf_op jit(solution)/shard_map/ppermute | solution.py:27
  70.2 19.7 %collective-permute-start.2 = (bf16[3,2,32,2048]{3,2,1,0:T(8,128)(2,1)S(1)}, bf16[3,2,32,2048]{3,2,1,0:T(8,128)(2,1)S(1)}, u32[]{:S(2)}, u32[]{:S(2)}) collective-permute-start(bf16[3,2,32,2048]{3,2,1,0:T(8,128)(2,1)S(1)} %copy-done.7), channel_id=1, source_target_pairs={{0,4},{4,0},{8,12},{12,8},{16,20},{20,16},{24,28},{28,24},{1,5},{5... | collective-permute-start | bytes 2359304 | tf_op jit(solution)/shard_map/ppermute | solution.py:31
  85.0 4.8 %collective-permute-start.11 = (bf16[2,576,512]{2,1,0:T(8,128)(2,1)S(1)}, bf16[2,576,512]{2,1,0:T(8,128)(2,1)S(1)}, u32[]{:S(2)}, u32[]{:S(2)}) collective-permute-start(bf16[2,576,512]{2,1,0:T(8,128)(2,1)S(1)} %get-tuple-element.25), channel_id=1, source_target_pairs={{0,1},{1,0},{2,3},{3,2},{4,5},{5,4},{6,7},{7,6},{8,9},{9,8},{10,11... | collective-permute-start | bytes 3538952 | tf_op jit(solution)/shard_map/ppermute | solution.py:35
  87.6 3.2 %collective-permute-start.5 = (bf16[3,2,32,2048]{3,2,1,0:T(8,128)(2,1)S(1)}, bf16[3,2,32,2048]{3,2,1,0:T(8,128)(2,1)S(1)}, u32[]{:S(2)}, u32[]{:S(2)}) collective-permute-start(bf16[3,2,32,2048]{3,2,1,0:T(8,128)(2,1)S(1)} %collective-permute-done.4.refs_2_), channel_id=1, source_target_pairs={{0,1},{1,0},{2,3},{3,2},{4,5},{5,4},{6,7},{7,6},{8,9},{9,8},{10,11... | collective-permute-start | bytes 2359304 | tf_op jit(solution)/shard_map/ppermute | solution.py:35
  89.8 2.3 %collective-permute-start.3 = (bf16[3,2,32,2048]{3,2,1,0:T(8,128)(2,1)S(1)}, bf16[3,2,32,2048]{3,2,1,0:T(8,128)(2,1)S(1)}, u32[]{:S(2)}, u32[]{:S(2)}) collective-permute-start(bf16[3,2,32,2048]{3,2,1,0:T(8,128)(2,1)S(1)} %collective-permute-done.2.refs_0_), channel_id=1, source_target_pairs={{0,1},{1,0},{2,3},{3,2},{4,5},{5,4},{6,7},{7,6},{8,9},{9,8},{10,11... | collective-permute-start | bytes 2359304 | tf_op jit(solution)/shard_map/ppermute | solution.py:35
  90.2 19.4 %collective-permute-start.12 = (bf16[3,3,64,512]{3,2,1,0:T(8,128)(2,1)S(1)}, bf16[3,3,64,512]{3,2,1,0:T(8,128)(2,1)S(1)}, u32[]{:S(2)}, u32[]{:S(2)}) collective-permute-start(bf16[3,3,64,512]{3,2,1,0:T(8,128)(2,1)S(1)} %bitcast.51), channel_id=1, source_target_pairs={{0,2},{1,3},{2,0},{3,1},{4,6},{5,7},{6,4},{7,5},{8,10},{9,11},{10,... | collective-permute-start | bytes 1769480 | tf_op jit(solution)/shard_map/ppermute | solution.py:35
  107.4 2.4 %collective-permute-start.13 = (bf16[2,384,512]{2,1,0:T(8,128)(2,1)S(1)}, bf16[2,384,512]{2,1,0:T(8,128)(2,1)S(1)}, u32[]{:S(2)}, u32[]{:S(2)}) collective-permute-start(bf16[2,384,512]{2,1,0:T(8,128)(2,1)S(1)} %get-tuple-element.31), channel_id=1, source_target_pairs={{0,1},{1,0},{2,3},{3,2},{4,5},{5,4},{6,7},{7,6},{8,9},{9,8},{10,11... | collective-permute-start | bytes 2359304 | tf_op jit(solution)/shard_map/ppermute | solution.py:35
  107.6 62.2 %collective-permute-start.20 = (bf16[192,2048]{1,0:T(8,128)(2,1)S(1)}, bf16[192,2048]{1,0:T(8,128)(2,1)S(1)}, u32[]{:S(2)}, u32[]{:S(2)}) collective-permute-start(bf16[192,2048]{1,0:T(8,128)(2,1)S(1)} %get-tuple-element.35), channel_id=1, source_target_pairs={{0,2},{1,3},{2,0},{3,1},{4,6},{5,7},{6,4},{7,5},{8,10},{9,11},{10,... | collective-permute-start | bytes 2359304 | tf_op jit(solution)/shard_map/ppermute | solution.py:35
  108.1 93.6 %collective-permute-start.19 = (bf16[2,192,2048]{2,1,0:T(8,128)(2,1)}, bf16[2,192,2048]{2,1,0:T(8,128)(2,1)}, u32[]{:S(2)}, u32[]{:S(2)}) collective-permute-start(bf16[2,192,2048]{2,1,0:T(8,128)(2,1)} %get-tuple-element.32), channel_id=1, source_target_pairs={{0,2},{1,3},{2,0},{3,1},{4,6},{5,7},{6,4},{7,5},{8,10},{9,11},{10,... | collective-permute-start | bytes 4718600 | tf_op jit(solution)/shard_map/ppermute | solution.py:35
  109.8 62.1 %collective-permute-start.16 = (bf16[2,3,64,512]{3,2,1,0:T(8,128)(2,1)S(1)}, bf16[2,3,64,512]{3,2,1,0:T(8,128)(2,1)S(1)}, u32[]{:S(2)}, u32[]{:S(2)}) collective-permute-start(bf16[2,3,64,512]{3,2,1,0:T(8,128)(2,1)S(1)} %pad_maximum_fusion.4), channel_id=1, source_target_pairs={{24,0},{28,4},{0,8},{4,12},{8,16},{12,20},{16,24},{20,28},{25,1},{... | collective-permute-start | bytes 1179656 | tf_op jit(solution)/shard_map/ppermute | solution.py:27
  110.1 59.5 %collective-permute-start.14 = (bf16[2,3,64,512]{3,2,1,0:T(8,128)(2,1)S(1)}, bf16[2,3,64,512]{3,2,1,0:T(8,128)(2,1)S(1)}, u32[]{:S(2)}, u32[]{:S(2)}) collective-permute-start(bf16[2,3,64,512]{3,2,1,0:T(8,128)(2,1)S(1)} %bitcast.52), channel_id=1, source_target_pairs={{0,2},{1,3},{2,0},{3,1},{4,6},{5,7},{6,4},{7,5},{8,10},{9,11},{10,... | collective-permute-start | bytes 1179656 | tf_op jit(solution)/shard_map/ppermute | solution.py:35
  110.7 61.1 %collective-permute-start.17 = (bf16[2,3,64,512]{3,2,1,0:T(8,128)(2,1)S(1)}, bf16[2,3,64,512]{3,2,1,0:T(8,128)(2,1)}, u32[]{:S(2)}, u32[]{:S(2)}) collective-permute-start(bf16[2,3,64,512]{3,2,1,0:T(8,128)(2,1)S(1)} %pad_maximum_fusion.5), channel_id=1, source_target_pairs={{20,0},{24,4},{28,8},{0,12},{4,16},{8,20},{12,24},{16,28},{21,1},{... | collective-permute-start | bytes 1179656 | tf_op jit(solution)/shard_map/ppermute | solution.py:27
  169.6 10.7 %collective-permute-start.15 = (bf16[2,3,64,512]{3,2,1,0:T(8,128)(2,1)S(1)}, bf16[2,3,64,512]{3,2,1,0:T(8,128)(2,1)}, u32[]{:S(2)}, u32[]{:S(2)}) collective-permute-start(bf16[2,3,64,512]{3,2,1,0:T(8,128)(2,1)S(1)} %pad_maximum_fusion.3), channel_id=1, source_target_pairs={{28,0},{0,4},{4,8},{8,12},{12,16},{16,20},{20,24},{24,28},{29,1},{... | collective-permute-start | bytes 1179656 | tf_op jit(solution)/shard_map/ppermute | solution.py:27
  169.8 28.5 %collective-permute-start.18 = (bf16[2,3,64,512]{3,2,1,0:T(8,128)(2,1)S(1)}, bf16[2,3,64,512]{3,2,1,0:T(8,128)(2,1)}, u32[]{:S(2)}, u32[]{:S(2)}) collective-permute-start(bf16[2,3,64,512]{3,2,1,0:T(8,128)(2,1)S(1)} %pad_maximum_fusion.6), channel_id=1, source_target_pairs={{16,0},{20,4},{24,8},{28,12},{0,16},{4,20},{8,24},{12,28},{17,1},{... | collective-permute-start | bytes 1179656 | tf_op jit(solution)/shard_map/ppermute | solution.py:27
  171.8 26.4 %copy-start.9 = (bf16[2,3,64,512]{3,2,1,0:T(8,128)(2,1)}, bf16[2,3,64,512]{3,2,1,0:T(8,128)(2,1)S(1)}, u32[]{:S(2)}) copy-start(bf16[2,3,64,512]{3,2,1,0:T(8,128)(2,1)S(1)} %collective-permute-done.16.refs_2_) | copy-start | bytes 1179652
  (8 other events, 29.0 us)

commit v3 on v2

--- a/solution.py
+++ b/solution.py
@@ -25,6 +25,11 @@
     size = size_of("blk")
     moves = lambda i: parity is None or i % 2 == parity
     return lax.ppermute(array, "blk", [((i + by) % size if moves(i) else i, i) for i in range(size)])
+
+
+def ahead_even(array, by):
+    size = size_of("blk")
+    return lax.ppermute(array, "blk", [((i + by) % size, i) for i in range(0, size, 2)])
 
 
 def swap_pair(array):
@@ -128,32 +133,28 @@
             for g in range(2):
                 moves.append((w_share.at[g], w_ref.at[pl.ds(g * units + k * fw, fw)]))
             moves.append((v_share, v_ref.at[pl.ds(k * fw, fw)]))
-        for slot in range(len(offsets)):
-            for t in range(MOST):
-                base = (slot * MOST + t) * half
-                if slot < home:
-                    for ref, rows in zip(home_refs, (x_s, c_s)):
-                        moves.append((ref.at[t, 0], rows.at[pl.ds(base, half)]))
-                else:
-                    for ref, at in zip(pieces[slot - home], (core, 1 - core)):
-                        place = pl.ds(pl.multiple_of(base + at * quarter, quarter), quarter)
-                        for g, rows in enumerate((x_s, c_s)):
-                            moves.append((ref.at[t, g], rows.at[place]))
         copies = [pltpu.make_async_copy(a, b, sems.at[n]) for n, (a, b) in enumerate(moves)]
         for copy in copies:
             copy.start()
+
+        def put(slot, t, at, x, c):
+            size = x.shape[0]
+            rows = pl.ds(pl.multiple_of((slot * MOST + t) * half + at, quarter), size)
+            ids = lax.broadcasted_iota(jnp.int32, (size, 1), 0) + (own // 2) * half + at
+            live = ids < s_ref[LIM + offsets[slot] * MOST + t]
+            x_s[rows, :] = x
+            c_s[rows, :] = jnp.where(live, c, jnp.zeros((), BF16))
+
+        for slot in range(len(offsets)):
+            for t in range(MOST):
+                if slot < home:
+                    put(slot, t, 0, home_refs[0][t, 0], home_refs[1][t, 0])
+                else:
+                    near, other = pieces[slot - home]
+                    put(slot, t, core * quarter, near[t, 0], near[t, 1])
+                    put(slot, t, (1 - core) * quarter, other[t, 0], other[t, 1])
         for copy in copies:
             copy.wait()
-        for slot in range(len(offsets)):
-            for t in range(MOST):
-                limit = s_ref[LIM + offsets[slot] * MOST + t]
-                rows = pl.ds((slot * MOST + t) * half, half)
-
-                @pl.when(limit < BLOCK)
-                def _():
-                    ids = lax.broadcasted_iota(jnp.int32, (half, 1), 0) + (own // 2) * half
-                    c_s[rows, :] = jnp.where(ids < limit, c_s[rows, :], jnp.zeros((), BF16))
-
         proj_s[...] = contract_last(x_s[...], w_ref[...])
         hg_s[...] = contract_last(c_s[...], v_ref[...])
         gate_pre = proj_s[:, :units]
@@ -204,13 +205,10 @@
     half = BLOCK // 2
     rows = len(offsets) * MOST * half
     arrays, specs = [], []
-    for a in home:
+    once = pl.Buffered(1)
+    for a in list(home) + [a for pair in pieces for a in pair]:
         arrays.append(a)
-        specs.append(pl.BlockSpec(memory_space=pl.ANY))
-    for pair in pieces:
-        for a in pair:
-            arrays.append(a)
-            specs.append(pl.BlockSpec(memory_space=pl.ANY))
+        specs.append(whole(a.shape, pipeline_mode=once))
     for a in shares:
         arrays.append(a)
         specs.append(pl.BlockSpec(memory_space=pl.ANY))
@@ -242,7 +240,7 @@
             scratch_shapes=[
                 pltpu.VMEM((2 * units, depth), BF16),
                 pltpu.VMEM((units, depth), BF16),
-                pltpu.SemaphoreType.DMA((6 + MOST * (len(home) + 4 * len(pieces)),)),
+                pltpu.SemaphoreType.DMA((6,)),
                 pltpu.VMEM((rows, depth), BF16),
                 pltpu.VMEM((rows, depth), BF16),
                 pltpu.VMEM((rows, 2 * units), F32),
@@ -252,7 +250,7 @@
                 pltpu.VMEM((units, rows), BF16),
             ],
         ),
-        compiler_params=pltpu.CompilerParams(vmem_limit_bytes=25 * 2**20),
+        compiler_params=pltpu.CompilerParams(vmem_limit_bytes=28 * 2**20),
         cost_estimate=pl.CostEstimate(
             flops=16 * rows * units * depth,
             bytes_accessed=rows * depth * 6 + units * depth * (6 + (24 if last else 12)),
@@ -321,8 +319,9 @@
     my_wide = quarter(MOST, nblk)
     wide = ahead(my_wide, 2)
     my_wide, counts, x_rows, grad_rows = lax.optimization_barrier((my_wide, counts, x_rows, grad_rows))
-    my_narrow = quarter(1, MOST)
-    narrow = ahead(my_narrow, 2)
+    my_two, my_one = quarter(2, MOST), quarter(1, 2)
+    two = ahead(my_two, 2)
+    one = ahead_even(my_one, 2)
     table = make_table(counts, n_dev, nblk)
     home = [
         lax.dynamic_slice(a.reshape(nblk, 2, -1, depth), (0, own // 2, 0, 0), (MOST, 1, BLOCK // 2, depth))
@@ -337,7 +336,7 @@
     fourth = wide[nblk - 2 * MOST :]
     third = ahead(third, 1)
     fourth = ahead(fourth, 2)
-    there = jnp.concatenate([narrow, wide])
+    there = jnp.concatenate([one, two, wide])
     first = jnp.where(table[ODD] == 1, mine, cut(there, table[WIN + SPAN + 1] - 1))
     second = cut(there, table[WIN + SPAN + 2] - 1)
     first = swap_pair(first)

time: 206 us -> 202 us (0.981)
  Pallas kernels: 34.9 us -> 31.6 us
    pallas_call x2, Pallas kernels: 30.1 us -> 26.8 us  [expert(): pl.pallas_call(functools.partial(expert_kernel, tuple(offsets), len(home)...]
  transfers between devices with their start and end apart: 21 -> 22, of which waited for: 8 -> 9; matrix products, arithmetic and copies ran while one was open for 8% -> 7% of each run, Pallas kernels for 17% -> 16%
where the time goes in v3:
time: 202 us
  waiting for transfers between devices  124 us (61%)
  Pallas kernels  31.6 us (16%)
  starting transfers between devices  18 us (9%)
  local copies, waits for them, and re-layouts  12.2 us (6%)
  other arithmetic  9.23 us (5%)
  between operations  6.6 us (3%)
    ppermute x8, waiting for transfers between devices, ahead(): lax.ppermute(array, 'blk', [((i + by) % size if moves(i) else i, i) for i...  63 us
    ppermute x12, waiting for transfers between devices, swap_dp(): lax.ppermute(array, 'dp', [(i, i ^ bit) for i in range(size_of('dp'))])  58.8 us
    pallas_call x2, Pallas kernels, expert(): pl.pallas_call(functools.partial(expert_kernel, tuple(offsets), len(home)...  26.8 us
    ppermute x8, starting transfers between devices, ahead(): lax.ppermute(array, 'blk', [((i + by) % size if moves(i) else i, i) for i...  11.6 us
    ppermute x12, starting transfers between devices, swap_dp(): lax.ppermute(array, 'dp', [(i, i ^ bit) for i in range(size_of('dp'))])  5.71 us
    dynamic_slice x4, local copies, waits for them, and re-layouts, pick(): lax.dynamic_slice(array, (first, own, 0, 0), (end - first, 1, part, depth))  5.01 us
  transfers between devices with their start and end apart: 22, of which 9 were waited for; matrix products, arithmetic and copies ran while one was open for 7% of the time, Pallas kernels for 16%

profile of v3, /device:TPU:6, one launch (start us, length us, event | category | flops | bytes accessed | tf_op | source)
XLA Modules:
  0.0 201.6 jit_solution(13828792552001299269)
XLA Ops:
  4.2 3.6 %collective-permute-start.2 = (bf16[5,2,32,2048]{3,2,1,0:T(8,128)(2,1)}, bf16[5,2,32,2048]{3,2,1,0:T(8,128)(2,1)}, u32[]{:S(2)}, u32[]{:S(2)}) collective-permute-start(bf16[5,2,32,2048]{3,2,1,0:T(8,128)(2,1)} %pad_maximum_fusion), channel_id=1, source_target_pairs={{8,0},{12,4},{16,8},{20,12},{24,16},{28,20},{0,24},{4,28},{9,1},{1... | collective-permute-start | bytes 3932168 | tf_op jit(solution)/shard_map/ppermute | solution.py:27
  10.7 1.5 collective-permute-start.7
  12.9 1.3 shard_map.76.s_ref
  14.3 1.5 fusion.6
  21.4 1.6 constant_dynamic-slice_fusion.8
  23.0 14.2 %collective-permute-done.2 = bf16[5,2,32,2048]{3,2,1,0:T(8,128)(2,1)} collective-permute-done((bf16[5,2,32,2048]{3,2,1,0:T(8,128)(2,1)}, bf16[5,2,32,2048]{3,2,1,0:T(8,128)(2,1)}, u32[]{:S(2)}, u32[]{:S(2)}) %collective-permute-start.2) | collective-permute-done | bytes 1310752 | tf_op jit(solution)/shard_map/ppermute | solution.py:27
  37.2 2.4 %constant_dynamic-slice_fusion = (bf16[3,2,32,2048]{3,2,1,0:T(8,128)(2,1)S(1)}, bf16[3,2,32,2048]{3,2,1,0:T(8,128)(2,1)}) fusion(bf16[5,2,32,2048]{3,2,1,0:T(8,128)(2,1)} %collective-permute-done.2, s32[]{:T(128)S(6)} %select_n.48), kind=kLoop, calls=%fused_computation.21 | loop fusion | bytes 3145732 | tf_op jit(solution)/shard_map/dynamic_slice | solution.py:98
  40.2 1.4 collective-permute-done.1
  41.6 1.4 constant_dynamic-update-slice_fusion
  44.1 19.0 %collective-permute-done.10.refs_4_ = bf16[3,2,32,2048]{3,2,1,0:T(8,128)(2,1)} collective-permute-done((bf16[3,2,32,2048]{3,2,1,0:T(8,128)(2,1)S(1)}, bf16[3,2,32,2048]{3,2,1,0:T(8,128)(2,1)}, u32[]{:S(2)}, u32[]{:S(2)}) %collective-permute-start.10) | collective-permute-done | bytes 786464 | tf_op jit(solution)/shard_map/ppermute | solution.py:27
  63.1 1.7 constant_dynamic-slice_fusion.2
  64.7 5.5 %collective-permute-start.5 = (bf16[3,2,32,2048]{3,2,1,0:T(8,128)(2,1)S(1)}, bf16[3,2,32,2048]{3,2,1,0:T(8,128)(2,1)S(1)}, u32[]{:S(2)}, u32[]{:S(2)}) collective-permute-start(bf16[3,2,32,2048]{3,2,1,0:T(8,128)(2,1)S(1)} %copy-done.6), channel_id=1, source_target_pairs={{8,0},{12,4},{16,8},{20,12},{24,16},{28,20},{0,24},{4,28},{9,1},{1... | collective-permute-start | bytes 2359304 | tf_op jit(solution)/shard_map/ppermute | solution.py:27
  70.2 15.1 %shard_map.77 = (f32[768,2048]{1,0:T(8,128)S(1)}, f32[384,2048]{1,0:T(8,128)S(1)}, bf16[2,576,512]{2,1,0:T(8,128)(2,1)S(1)}, bf16[2,576,512]{2,1,0:T(8,128)(2,1)S(1)}) custom-call(s32[32]{0:T(128)S(1)} %copy-done, bf16[3,1,64,2048]{3,2,1,0:T(8,128)(2,1)S(1)} %get-tuple-element.69.refs_0_, bf16[3,1,64,2048]{3,2,1,0:T(8,128)(2,1)S(1)} %get-tuple-element.68.refs_1_, ...), custom_call_target="tpu_custom_call" | custom-call | flops 7247757312 | bytes 21233664 | tf_op jit(solution)/shard_map/pallas_call | solution.py:232
  85.7 2.0 collective-permute-done.5.refs_2_
  87.7 2.2 %collective-permute-done.3.refs_0_ = bf16[3,2,32,2048]{3,2,1,0:T(8,128)(2,1)S(1)} collective-permute-done((bf16[3,2,32,2048]{3,2,1,0:T(8,128)(2,1)S(1)}, bf16[3,2,32,2048]{3,2,1,0:T(8,128)(2,1)S(1)}, u32[]{:S(2)}, u32[]{:S(2)}) %collective-permute-start.3) | collective-permute-done | bytes 786464 | tf_op jit(solution)/shard_map/ppermute | solution.py:36
  90.8 1.4 collective-permute-done.4.refs_1_
  92.2 11.7 %shard_map.78 = (f32[2,192,2048]{2,1,0:T(8,128)S(1)}, f32[192,2048]{1,0:T(8,128)S(1)}, bf16[2,192,2048]{2,1,0:T(8,128)(2,1)}, bf16[192,2048]{1,0:T(8,128)(2,1)S(...) custom-call(s32[32]{0:T(128)S(1)} %copy-done, ...), custom_call_target="tpu_custom_call" | custom-call | flops 4831838208 | bytes 28311552 | tf_op jit(solution)/shard_map/pallas_call | solution.py:232
  104.5 1.5 collective-permute-start.20
  108.6 57.4 %collective-permute-done.15 = bf16[2,3,64,512]{3,2,1,0:T(8,128)(2,1)S(1)} collective-permute-done((bf16[2,3,64,512]{3,2,1,0:T(8,128)(2,1)S(1)}, bf16[2,3,64,512]{3,2,1,0:T(8,128)(2,1)S(1)}, u32[]{:S(2)}, u32[]{:S(2)}) %collective-permute-start.15) | collective-permute-done | bytes 393248 | tf_op jit(solution)/shard_map/ppermute | solution.py:40
  166.9 1.4 add_bitcast_fusion.1
  168.3 8.5 %collective-permute-done.16.refs_1_ = bf16[2,3,64,512]{3,2,1,0:T(8,128)(2,1)} collective-permute-done((bf16[2,3,64,512]{3,2,1,0:T(8,128)(2,1)S(1)}, bf16[2,3,64,512]{3,2,1,0:T(8,128)(2,1)}, u32[]{:S(2)}, u32[]{:S(2)}) %collective-permute-start.16) | collective-permute-done | bytes 393248 | tf_op jit(solution)/shard_map/ppermute | solution.py:27
  176.8 17.9 %collective-permute-done.19.refs_4_ = bf16[2,3,64,512]{3,2,1,0:T(8,128)(2,1)} collective-permute-done((bf16[2,3,64,512]{3,2,1,0:T(8,128)(2,1)S(1)}, bf16[2,3,64,512]{3,2,1,0:T(8,128)(2,1)}, u32[]{:S(2)}, u32[]{:S(2)}) %collective-permute-start.19) | collective-permute-done | bytes 393248 | tf_op jit(solution)/shard_map/ppermute | solution.py:27
  194.6 3.5 %shard_map.79 = bf16[8,128,512]{2,1,0:T(8,128)(2,1)} custom-call(s32[32]{0:T(128)} %shard_map.76.s_ref, bf16[2,3,64,512]{3,2,1,0:T(8,128)(2,1)} %pad_maximum_fusion.1.refs_0_, bf16[2,3,64,512]{3,2,1,0:T(8,128)(2,1)} %collective-permute-done.16.refs_1_, bf16[2,3,64,512]{3,2,1,0:T(8,128)(2,1)} %copy-done.7, ...), custom_call_target="tpu_custom_call" | custom-call | tf_op jit(solution)/shard_map/pallas_call | solution.py:290
  198.1 3.5 %add_bitcast_fusion = f32[1,2,192,2048]{3,2,1,0:T(8,128)} fusion(f32[2,192,2048]{2,1,0:T(8,128)S(1)} %get-tuple-element.28, bf16[2,192,2048]{2,1,0:T(8,128)(2,1)} %collective-permute-done.20), kind=kLoop, calls=%fused_computation | loop fusion | flops 1572864 | bytes 7864320 | tf_op jit(solution)/shard_map/broadcast_in_dim | solution.py:365
  (71 shorter events, 14.0 us)
Async XLA Ops:
  4.2 33.1 %collective-permute-start.2 = (bf16[5,2,32,2048]{3,2,1,0:T(8,128)(2,1)}, bf16[5,2,32,2048]{3,2,1,0:T(8,128)(2,1)}, u32[]{:S(2)}, u32[]{:S(2)}) collective-permute-start(bf16[5,2,32,2048]{3,2,1,0:T(8,128)(2,1)} %pad_maximum_fusion), channel_id=1, source_target_pairs={{8,0},{12,4},{16,8},{20,12},{24,16},{28,20},{0,24},{4,28},{9,1},{1... | collective-permute-start | bytes 3932168 | tf_op jit(solution)/shard_map/ppermute | solution.py:27
  8.9 31.2 %collective-permute-start = (bf16[1,2,32,2048]{3,2,1,0:T(8,128)(2,1)S(1)}, bf16[1,2,32,2048]{3,2,1,0:T(8,128)(2,1)S(1)}, u32[]{:S(2)}, u32[]{:S(2)}) collective-permute-start(bf16[1,2,32,2048]{3,2,1,0:T(8,128)(2,1)S(1)} %pad_maximum_fusion.6), channel_id=1, source_target_pairs={{8,0},{16,8},{24,16},{0,24},{9,1},{17,9},{25,17},{1,25},{10,2},{18... | collective-permute-start | bytes 786440 | tf_op jit(solution)/shard_map/ppermute | solution.py:32
  9.6 32.0 %collective-permute-start.1 = (bf16[1,2,32,2048]{3,2,1,0:T(8,128)(2,1)S(1)}, bf16[1,2,32,2048]{3,2,1,0:T(8,128)(2,1)S(1)}, u32[]{:S(2)}, u32[]{:S(2)}) collective-permute-start(bf16[1,2,32,2048]{3,2,1,0:T(8,128)(2,1)S(1)} %pad_maximum_fusion.7), channel_id=1, source_target_pairs={{8,0},{12,4},{16,8},{20,12},{24,16},{28,20},{0,24},{4,28},{9,1},{1... | collective-permute-start | bytes 786440 | tf_op jit(solution)/shard_map/ppermute | solution.py:27
  10.1 60.0 %collective-permute-start.8 = (bf16[192,2048]{1,0:T(8,128)(2,1)S(1)}, bf16[192,2048]{1,0:T(8,128)(2,1)}, u32[]{:S(2)}, u32[]{:S(2)}) collective-permute-start(bf16[192,2048]{1,0:T(8,128)(2,1)S(1)} %bitcast.34), channel_id=1, source_target_pairs={{0,2},{1,3},{2,0},{3,1},{4,6},{5,7},{6,4},{7,5},{8,10},{9,11},{10,... | collective-permute-start | bytes 2359304 | tf_op jit(solution)/shard_map/ppermute | solution.py:40
  10.7 59.5 %collective-permute-start.7 = (bf16[2,192,2048]{2,1,0:T(8,128)(2,1)S(1)}, bf16[2,192,2048]{2,1,0:T(8,128)(2,1)}, u32[]{:S(2)}, u32[]{:S(2)}) collective-permute-start(bf16[2,192,2048]{2,1,0:T(8,128)(2,1)S(1)} %bitcast.31), channel_id=1, source_target_pairs={{0,2},{1,3},{2,0},{3,1},{4,6},{5,7},{6,4},{7,5},{8,10},{9,11},{10,... | collective-permute-start | bytes 4718600 | tf_op jit(solution)/shard_map/ppermute | solution.py:40
  39.6 23.4 %collective-permute-start.10 = (bf16[3,2,32,2048]{3,2,1,0:T(8,128)(2,1)S(1)}, bf16[3,2,32,2048]{3,2,1,0:T(8,128)(2,1)}, u32[]{:S(2)}, u32[]{:S(2)}) collective-permute-start(bf16[3,2,32,2048]{3,2,1,0:T(8,128)(2,1)S(1)} %get-tuple-element.47), channel_id=1, source_target_pairs={{4,0},{8,4},{12,8},{16,12},{20,16},{24,20},{28,24},{0,28},{5,1},{9... | collective-permute-start | bytes 2359304 | tf_op jit(solution)/shard_map/ppermute | solution.py:27
  44.1 26.2 %copy-start = (s32[32]{0:T(128)S(1)}, s32[32]{0:T(128)}, u32[]{:S(2)}) copy-start(s32[32]{0:T(128)} %shard_map.76.s_ref) | copy-start | bytes 388
  44.1 26.1 %collective-permute-start.9 = (bf16[3,2,32,2048]{3,2,1,0:T(8,128)(2,1)S(1)}, bf16[3,2,32,2048]{3,2,1,0:T(8,128)(2,1)}, u32[]{:S(2)}, u32[]{:S(2)}) collective-permute-start(bf16[3,2,32,2048]{3,2,1,0:T(8,128)(2,1)S(1)} %get-tuple-element.43.refs_2_), channel_id=1, source_target_pairs={{0,1},{1,0},{2,3},{3,2},{4,5},{5,4},{6,7},{7,6},{8,9},{9,8},{10,11... | collective-permute-start | bytes 2359304 | tf_op jit(solution)/shard_map/ppermute | solution.py:40
  63.0 7.2 %collective-permute-start.11 = (bf16[3,2,32,2048]{3,2,1,0:T(8,128)(2,1)}, bf16[3,2,32,2048]{3,2,1,0:T(8,128)(2,1)}, u32[]{:S(2)}, u32[]{:S(2)}) collective-permute-start(bf16[3,2,32,2048]{3,2,1,0:T(8,128)(2,1)} %collective-permute-done.10.refs_4_), channel_id=1, source_target_pairs={{0,1},{1,0},{2,3},{3,2},{4,5},{5,4},{6,7},{7,6},{8,9},{9,8},{10,11... | collective-permute-start | bytes 2359304 | tf_op jit(solution)/shard_map/ppermute | solution.py:40
  64.7 22.9 %collective-permute-start.5 = (bf16[3,2,32,2048]{3,2,1,0:T(8,128)(2,1)S(1)}, bf16[3,2,32,2048]{3,2,1,0:T(8,128)(2,1)S(1)}, u32[]{:S(2)}, u32[]{:S(2)}) collective-permute-start(bf16[3,2,32,2048]{3,2,1,0:T(8,128)(2,1)S(1)} %copy-done.6), channel_id=1, source_target_pairs={{8,0},{12,4},{16,8},{20,12},{24,16},{28,20},{0,24},{4,28},{9,1},{1... | collective-permute-start | bytes 2359304 | tf_op jit(solution)/shard_map/ppermute | solution.py:27
  70.2 19.7 %collective-permute-start.3 = (bf16[3,2,32,2048]{3,2,1,0:T(8,128)(2,1)S(1)}, bf16[3,2,32,2048]{3,2,1,0:T(8,128)(2,1)S(1)}, u32[]{:S(2)}, u32[]{:S(2)}) collective-permute-start(bf16[3,2,32,2048]{3,2,1,0:T(8,128)(2,1)S(1)} %copy-done.5), channel_id=1, source_target_pairs={{0,4},{4,0},{8,12},{12,8},{16,20},{20,16},{24,28},{28,24},{1,5},{5... | collective-permute-start | bytes 2359304 | tf_op jit(solution)/shard_map/ppermute | solution.py:36
  85.4 4.5 %collective-permute-start.12 = (bf16[2,576,512]{2,1,0:T(8,128)(2,1)S(1)}, bf16[2,576,512]{2,1,0:T(8,128)(2,1)S(1)}, u32[]{:S(2)}, u32[]{:S(2)}) collective-permute-start(bf16[2,576,512]{2,1,0:T(8,128)(2,1)S(1)} %get-tuple-element.25), channel_id=1, source_target_pairs={{0,1},{1,0},{2,3},{3,2},{4,5},{5,4},{6,7},{7,6},{8,9},{9,8},{10,11... | collective-permute-start | bytes 3538952 | tf_op jit(solution)/shard_map/ppermute | solution.py:40
  87.7 3.1 %collective-permute-start.6 = (bf16[3,2,32,2048]{3,2,1,0:T(8,128)(2,1)S(1)}, bf16[3,2,32,2048]{3,2,1,0:T(8,128)(2,1)S(1)}, u32[]{:S(2)}, u32[]{:S(2)}) collective-permute-start(bf16[3,2,32,2048]{3,2,1,0:T(8,128)(2,1)S(1)} %collective-permute-done.5.refs_2_), channel_id=1, source_target_pairs={{0,1},{1,0},{2,3},{3,2},{4,5},{5,4},{6,7},{7,6},{8,9},{9,8},{10,11... | collective-permute-start | bytes 2359304 | tf_op jit(solution)/shard_map/ppermute | solution.py:40
  89.9 2.3 %collective-permute-start.4 = (bf16[3,2,32,2048]{3,2,1,0:T(8,128)(2,1)S(1)}, bf16[3,2,32,2048]{3,2,1,0:T(8,128)(2,1)S(1)}, u32[]{:S(2)}, u32[]{:S(2)}) collective-permute-start(bf16[3,2,32,2048]{3,2,1,0:T(8,128)(2,1)S(1)} %collective-permute-done.3.refs_0_), channel_id=1, source_target_pairs={{0,1},{1,0},{2,3},{3,2},{4,5},{5,4},{6,7},{7,6},{8,9},{9,8},{10,11... | collective-permute-start | bytes 2359304 | tf_op jit(solution)/shard_map/ppermute | solution.py:40
  90.2 15.9 %collective-permute-start.13 = (bf16[3,3,64,512]{3,2,1,0:T(8,128)(2,1)S(1)}, bf16[3,3,64,512]{3,2,1,0:T(8,128)(2,1)S(1)}, u32[]{:S(2)}, u32[]{:S(2)}) collective-permute-start(bf16[3,3,64,512]{3,2,1,0:T(8,128)(2,1)S(1)} %bitcast.51), channel_id=1, source_target_pairs={{0,2},{1,3},{2,0},{3,1},{4,6},{5,7},{6,4},{7,5},{8,10},{9,11},{10,... | collective-permute-start | bytes 1769480 | tf_op jit(solution)/shard_map/ppermute | solution.py:40
  103.8 2.5 %collective-permute-start.14 = (bf16[2,384,512]{2,1,0:T(8,128)(2,1)S(1)}, bf16[2,384,512]{2,1,0:T(8,128)(2,1)S(1)}, u32[]{:S(2)}, u32[]{:S(2)}) collective-permute-start(bf16[2,384,512]{2,1,0:T(8,128)(2,1)S(1)} %get-tuple-element.31), channel_id=1, source_target_pairs={{0,1},{1,0},{2,3},{3,2},{4,5},{5,4},{6,7},{7,6},{8,9},{9,8},{10,11... | collective-permute-start | bytes 2359304 | tf_op jit(solution)/shard_map/ppermute | solution.py:40
  104.0 62.1 %collective-permute-start.21 = (bf16[192,2048]{1,0:T(8,128)(2,1)S(1)}, bf16[192,2048]{1,0:T(8,128)(2,1)S(1)}, u32[]{:S(2)}, u32[]{:S(2)}) collective-permute-start(bf16[192,2048]{1,0:T(8,128)(2,1)S(1)} %get-tuple-element.35), channel_id=1, source_target_pairs={{0,2},{1,3},{2,0},{3,1},{4,6},{5,7},{6,4},{7,5},{8,10},{9,11},{10,... | collective-permute-start | bytes 2359304 | tf_op jit(solution)/shard_map/ppermute | solution.py:40
  104.5 93.6 %collective-permute-start.20 = (bf16[2,192,2048]{2,1,0:T(8,128)(2,1)}, bf16[2,192,2048]{2,1,0:T(8,128)(2,1)}, u32[]{:S(2)}, u32[]{:S(2)}) collective-permute-start(bf16[2,192,2048]{2,1,0:T(8,128)(2,1)} %get-tuple-element.32), channel_id=1, source_target_pairs={{0,2},{1,3},{2,0},{3,1},{4,6},{5,7},{6,4},{7,5},{8,10},{9,11},{10,... | collective-permute-start | bytes 4718600 | tf_op jit(solution)/shard_map/ppermute | solution.py:40
  106.2 62.1 %collective-permute-start.17 = (bf16[2,3,64,512]{3,2,1,0:T(8,128)(2,1)S(1)}, bf16[2,3,64,512]{3,2,1,0:T(8,128)(2,1)S(1)}, u32[]{:S(2)}, u32[]{:S(2)}) collective-permute-start(bf16[2,3,64,512]{3,2,1,0:T(8,128)(2,1)S(1)} %pad_maximum_fusion.3), channel_id=1, source_target_pairs={{24,0},{28,4},{0,8},{4,12},{8,16},{12,20},{16,24},{20,28},{25,1},{... | collective-permute-start | bytes 1179656 | tf_op jit(solution)/shard_map/ppermute | solution.py:27
  106.5 59.5 %collective-permute-start.15 = (bf16[2,3,64,512]{3,2,1,0:T(8,128)(2,1)S(1)}, bf16[2,3,64,512]{3,2,1,0:T(8,128)(2,1)S(1)}, u32[]{:S(2)}, u32[]{:S(2)}) collective-permute-start(bf16[2,3,64,512]{3,2,1,0:T(8,128)(2,1)S(1)} %bitcast.52), channel_id=1, source_target_pairs={{0,2},{1,3},{2,0},{3,1},{4,6},{5,7},{6,4},{7,5},{8,10},{9,11},{10,... | collective-permute-start | bytes 1179656 | tf_op jit(solution)/shard_map/ppermute | solution.py:40
  107.1 61.2 %collective-permute-start.18 = (bf16[2,3,64,512]{3,2,1,0:T(8,128)(2,1)S(1)}, bf16[2,3,64,512]{3,2,1,0:T(8,128)(2,1)}, u32[]{:S(2)}, u32[]{:S(2)}) collective-permute-start(bf16[2,3,64,512]{3,2,1,0:T(8,128)(2,1)S(1)} %pad_maximum_fusion.4), channel_id=1, source_target_pairs={{20,0},{24,4},{28,8},{0,12},{4,16},{8,20},{12,24},{16,28},{21,1},{... | collective-permute-start | bytes 1179656 | tf_op jit(solution)/shard_map/ppermute | solution.py:27
  166.1 10.7 %collective-permute-start.16 = (bf16[2,3,64,512]{3,2,1,0:T(8,128)(2,1)S(1)}, bf16[2,3,64,512]{3,2,1,0:T(8,128)(2,1)}, u32[]{:S(2)}, u32[]{:S(2)}) collective-permute-start(bf16[2,3,64,512]{3,2,1,0:T(8,128)(2,1)S(1)} %pad_maximum_fusion.2), channel_id=1, source_target_pairs={{28,0},{0,4},{4,8},{8,12},{12,16},{16,20},{20,24},{24,28},{29,1},{... | collective-permute-start | bytes 1179656 | tf_op jit(solution)/shard_map/ppermute | solution.py:27
  166.2 28.5 %collective-permute-start.19 = (bf16[2,3,64,512]{3,2,1,0:T(8,128)(2,1)S(1)}, bf16[2,3,64,512]{3,2,1,0:T(8,128)(2,1)}, u32[]{:S(2)}, u32[]{:S(2)}) collective-permute-start(bf16[2,3,64,512]{3,2,1,0:T(8,128)(2,1)S(1)} %pad_maximum_fusion.5), channel_id=1, source_target_pairs={{16,0},{20,4},{24,8},{28,12},{0,16},{4,20},{8,24},{12,28},{17,1},{... | collective-permute-start | bytes 1179656 | tf_op jit(solution)/shard_map/ppermute | solution.py:27
  168.3 26.4 %copy-start.7 = (bf16[2,3,64,512]{3,2,1,0:T(8,128)(2,1)}, bf16[2,3,64,512]{3,2,1,0:T(8,128)(2,1)S(1)}, u32[]{:S(2)}) copy-start(bf16[2,3,64,512]{3,2,1,0:T(8,128)(2,1)S(1)} %collective-permute-done.17.refs_2_) | copy-start | bytes 1179652
  (7 other events, 46.5 us)

commit v4 on v3

--- a/solution.py
+++ b/solution.py
@@ -111,7 +111,7 @@
     shares = take(4)
     add_in, add_out = take(2) if last else (None, None)
     if last:
-        own_in, own_out, far_in, far_out = take(4)
+        own_in, own_out, far_gate, far_up, far_out = take(5)
     else:
         sum_in, sum_out = take(2)
     give, keep, w_ref, v_ref, sems, x_s, c_s, proj_s, hg_s, gu_s, gut_s, ht_s = refs
@@ -180,8 +180,8 @@
         own_in[0] = new_in[:fw]
         own_in[1] = new_in[units : units + fw]
         own_out[...] = new_out[:fw]
-        far_in[0] = new_in[fw:units].astype(BF16)
-        far_in[1] = new_in[units + fw :].astype(BF16)
+        far_gate[...] = new_in[fw:units].astype(BF16)
+        far_up[...] = new_in[units + fw :].astype(BF16)
         far_out[...] = new_out[fw:].astype(BF16)
     else:
         sum_in[...] = new_in
@@ -219,8 +219,8 @@
     if last:
         arrays += list(sums)
         specs += [chunk_in, chunk_out]
-        shapes = [((2, fw, depth), F32), ((fw, depth), F32), ((2, fw, depth), BF16), ((fw, depth), BF16)]
-        outs = [own_in, own_out, own_in, own_out]
+        shapes = [((2, fw, depth), F32), ((fw, depth), F32)] + [((fw, depth), BF16)] * 3
+        outs = [own_in] + [own_out] * 4
     else:
         shapes = [((2 * units, depth), F32), ((units, depth), F32)]
         outs = [chunk_in, chunk_out]
@@ -352,17 +352,19 @@
     there = swap_dp(there, 2)
     r0, r2, r3 = add_rows(here, there)
     pieces = [pair(first), pair(fourth)]
-    own_in, own_out, far_in, far_out, give, keep = expert(table, (1, 4), (), pieces, shares, (sum_in, sum_out))
-    far_out = swap_dp(far_out, 2)
+    own_in, own_out, far_gate, far_up, far_out, give, keep = expert(table, (1, 4), (), pieces, shares, (sum_in, sum_out))
+    far_gate = swap_dp(far_gate, 2)
     here, there = add_cores(give, keep, 2)
     there = swap_dp(there, 2)
     r1, r4 = add_rows(here, there)
-    far_in = swap_dp(far_in, 2)
+    far_up = swap_dp(far_up, 2)
+    far_out = swap_dp(far_out, 2)
     r2, r3 = ahead(r2, -2), ahead(r3, -3)
     r1, r4 = ahead(r1, -1), ahead(r4, -4)
     done = merge(table, [r0, r1, r2, r3, r4], nblk)
-    done, far_in = lax.optimization_barrier((done, far_in))
-    return (own_in + far_in)[None], (own_out + far_out)[None], done.reshape(total, -1)
+    total_in = own_in + jnp.stack([far_gate, far_up])
+    total_in, done, far_out = lax.optimization_barrier((total_in, done, far_out))
+    return total_in[None], (own_out + far_out)[None], done.reshape(total, -1)
 
 
 def solution(mesh):

time: 202 us -> 217 us (1.074)
  the two profiles are of different devices: /device:TPU:6 before, /device:TPU:2 now
where the time goes in v4:
time: 217 us; the launch traced here: 216 us
  waiting for transfers between devices  133 us (61%)
  Pallas kernels  31.7 us (15%)
  starting transfers between devices  24.5 us (11%)
  local copies, waits for them, and re-layouts  12.2 us (6%)
  other arithmetic  7.86 us (4%)
  between operations  6.59 us (3%)
    ppermute x8, waiting for transfers between devices, ahead(): lax.ppermute(array, 'blk', [((i + by) % size if moves(i) else i, i) for i...  73.9 us
    ppermute x13, waiting for transfers between devices, swap_dp(): lax.ppermute(array, 'dp', [(i, i ^ bit) for i in range(size_of('dp'))])  56.9 us
    pallas_call x2, Pallas kernels, expert(): pl.pallas_call(functools.partial(expert_kernel, tuple(offsets), len(home)...  26.8 us
    ppermute x8, starting transfers between devices, ahead(): lax.ppermute(array, 'blk', [((i + by) % size if moves(i) else i, i) for i...  15.7 us
    ppermute x13, starting transfers between devices, swap_dp(): lax.ppermute(array, 'dp', [(i, i ^ bit) for i in range(size_of('dp'))])  8.2 us
    dynamic_slice x4, local copies, waits for them, and re-layouts, pick(): lax.dynamic_slice(array, (first, own, 0, 0), (end - first, 1, part, depth))  5.01 us
  transfers between devices with their start and end apart: 23, of which 10 were waited for; matrix products, arithmetic and copies ran while one was open for 7% of the time, Pallas kernels for 15%

profile of v4, /device:TPU:2, one launch (start us, length us, event | category | flops | bytes accessed | tf_op | source)
XLA Modules:
  0.0 215.9 jit_solution(16982148272368638141)
XLA Ops:
  4.2 3.6 %collective-permute-start.2 = (bf16[5,2,32,2048]{3,2,1,0:T(8,128)(2,1)}, bf16[5,2,32,2048]{3,2,1,0:T(8,128)(2,1)}, u32[]{:S(2)}, u32[]{:S(2)}) collective-permute-start(bf16[5,2,32,2048]{3,2,1,0:T(8,128)(2,1)} %pad_maximum_fusion), channel_id=1, source_target_pairs={{8,0},{12,4},{16,8},{20,12},{24,16},{28,20},{0,24},{4,28},{9,1},{1... | collective-permute-start | bytes 3932168 | tf_op jit(solution)/shard_map/ppermute | solution.py:27
  10.1 1.5 collective-permute-start.8
  14.2 1.5 fusion.6
  21.3 1.6 constant_dynamic-slice_fusion.8
  22.9 14.3 %collective-permute-done.2 = bf16[5,2,32,2048]{3,2,1,0:T(8,128)(2,1)} collective-permute-done((bf16[5,2,32,2048]{3,2,1,0:T(8,128)(2,1)}, bf16[5,2,32,2048]{3,2,1,0:T(8,128)(2,1)}, u32[]{:S(2)}, u32[]{:S(2)}) %collective-permute-start.2) | collective-permute-done | bytes 1310752 | tf_op jit(solution)/shard_map/ppermute | solution.py:27
  37.2 2.4 %constant_dynamic-slice_fusion = (bf16[3,2,32,2048]{3,2,1,0:T(8,128)(2,1)S(1)}, bf16[3,2,32,2048]{3,2,1,0:T(8,128)(2,1)}) fusion(bf16[5,2,32,2048]{3,2,1,0:T(8,128)(2,1)} %collective-permute-done.2, s32[]{:T(128)S(6)} %select_n.48), kind=kLoop, calls=%fused_computation.21 | loop fusion | bytes 3145732 | tf_op jit(solution)/shard_map/dynamic_slice | solution.py:98
  44.1 18.8 %collective-permute-done.10.refs_4_ = bf16[3,2,32,2048]{3,2,1,0:T(8,128)(2,1)} collective-permute-done((bf16[3,2,32,2048]{3,2,1,0:T(8,128)(2,1)S(1)}, bf16[3,2,32,2048]{3,2,1,0:T(8,128)(2,1)}, u32[]{:S(2)}, u32[]{:S(2)}) %collective-permute-start.10) | collective-permute-done | bytes 786464 | tf_op jit(solution)/shard_map/ppermute | solution.py:27
  62.9 1.7 constant_dynamic-slice_fusion.2
  64.6 5.6 %collective-permute-start.5 = (bf16[3,2,32,2048]{3,2,1,0:T(8,128)(2,1)S(1)}, bf16[3,2,32,2048]{3,2,1,0:T(8,128)(2,1)S(1)}, u32[]{:S(2)}, u32[]{:S(2)}) collective-permute-start(bf16[3,2,32,2048]{3,2,1,0:T(8,128)(2,1)S(1)} %copy-done.5), channel_id=1, source_target_pairs={{8,0},{12,4},{16,8},{20,12},{24,16},{28,20},{0,24},{4,28},{9,1},{1... | collective-permute-start | bytes 2359304 | tf_op jit(solution)/shard_map/ppermute | solution.py:27
  70.2 15.1 %shard_map.77 = (f32[768,2048]{1,0:T(8,128)S(1)}, f32[384,2048]{1,0:T(8,128)S(1)}, bf16[2,576,512]{2,1,0:T(8,128)(2,1)S(1)}, bf16[2,576,512]{2,1,0:T(8,128)(2,1)S(1)}) custom-call(s32[32]{0:T(128)S(1)} %copy-done, bf16[3,1,64,2048]{3,2,1,0:T(8,128)(2,1)S(1)} %get-tuple-element.73.refs_0_, bf16[3,1,64,2048]{3,2,1,0:T(8,128)(2,1)S(1)} %get-tuple-element.72.refs_1_, ...), custom_call_target="tpu_custom_call" | custom-call | flops 7247757312 | bytes 21233664 | tf_op jit(solution)/shard_map/pallas_call | solution.py:232
  85.7 2.0 collective-permute-done.5.refs_2_
  87.7 2.2 %collective-permute-done.3.refs_0_ = bf16[3,2,32,2048]{3,2,1,0:T(8,128)(2,1)S(1)} collective-permute-done((bf16[3,2,32,2048]{3,2,1,0:T(8,128)(2,1)S(1)}, bf16[3,2,32,2048]{3,2,1,0:T(8,128)(2,1)S(1)}, u32[]{:S(2)}, u32[]{:S(2)}) %collective-permute-start.3) | collective-permute-done | bytes 786464 | tf_op jit(solution)/shard_map/ppermute | solution.py:36
  90.2 1.6 collective-permute-start.15
  92.2 11.7 %shard_map.78 = (f32[2,192,2048]{2,1,0:T(8,128)S(1)}, f32[192,2048]{1,0:T(8,128)S(1)}, bf16[192,2048]{1,0:T(8,128)(2,1)S(1)}, bf16[192,2048]{1,0:T(8,128)(2,1)S(...) custom-call(s32[32]{0:T(128)S(1)} %copy-done, ...), custom_call_target="tpu_custom_call" | custom-call | flops 4831838208 | bytes 28311552 | tf_op jit(solution)/shard_map/pallas_call | solution.py:232
  104.1 1.5 collective-permute-start.13
  106.1 1.5 collective-permute-start.22
  109.5 56.6 %collective-permute-done.17 = bf16[2,3,64,512]{3,2,1,0:T(8,128)(2,1)S(1)} collective-permute-done((bf16[2,3,64,512]{3,2,1,0:T(8,128)(2,1)S(1)}, bf16[2,3,64,512]{3,2,1,0:T(8,128)(2,1)S(1)}, u32[]{:S(2)}, u32[]{:S(2)}) %collective-permute-start.17) | collective-permute-done | bytes 393248 | tf_op jit(solution)/shard_map/ppermute | solution.py:40
  166.2 1.7 collective-permute-start.18
  167.9 3.6 %collective-permute-start.21 = (bf16[2,3,64,512]{3,2,1,0:T(8,128)(2,1)S(1)}, bf16[2,3,64,512]{3,2,1,0:T(8,128)(2,1)}, u32[]{:S(2)}, u32[]{:S(2)}) collective-permute-start(bf16[2,3,64,512]{3,2,1,0:T(8,128)(2,1)S(1)} %pad_maximum_fusion.5), channel_id=1, source_target_pairs={{16,0},{20,4},{24,8},{28,12},{0,16},{4,20},{8,24},{12,28},{17,1},{... | collective-permute-start | bytes 1179656 | tf_op jit(solution)/shard_map/ppermute | solution.py:27
  171.5 2.3 %convert_add_fusion = f32[2,192,2048]{2,1,0:T(8,128)} fusion(f32[2,192,2048]{2,1,0:T(8,128)S(1)} %get-tuple-element.30, bf16[1,192,2048]{2,1,0:T(8,128)(2,1)S(1)} %bitcast.54, bf16[1,192,2048]{2,1,0:T(8,128)(2,1)S(1)} %bitcast.53), kind=kLoop, calls=%fused_computation | loop fusion | flops 2359296 | bytes 7864320 | tf_op jit(solution)/shard_map/add | solution.py:365
  173.8 7.0 %collective-permute-done.20.refs_3_ = bf16[2,3,64,512]{3,2,1,0:T(8,128)(2,1)S(1)} collective-permute-done((bf16[2,3,64,512]{3,2,1,0:T(8,128)(2,1)S(1)}, bf16[2,3,64,512]{3,2,1,0:T(8,128)(2,1)S(1)}, u32[]{:S(2)}, u32[]{:S(2)}) %collective-permute-start.20) | collective-permute-done | bytes 393248 | tf_op jit(solution)/shard_map/ppermute | solution.py:27
  180.8 4.8 %collective-permute-done.18.refs_1_ = bf16[2,3,64,512]{3,2,1,0:T(8,128)(2,1)S(1)} collective-permute-done((bf16[2,3,64,512]{3,2,1,0:T(8,128)(2,1)S(1)}, bf16[2,3,64,512]{3,2,1,0:T(8,128)(2,1)S(1)}, u32[]{:S(2)}, u32[]{:S(2)}) %collective-permute-start.18) | collective-permute-done | bytes 393248 | tf_op jit(solution)/shard_map/ppermute | solution.py:27
  185.7 25.4 %collective-permute-done.21.refs_4_ = bf16[2,3,64,512]{3,2,1,0:T(8,128)(2,1)} collective-permute-done((bf16[2,3,64,512]{3,2,1,0:T(8,128)(2,1)S(1)}, bf16[2,3,64,512]{3,2,1,0:T(8,128)(2,1)}, u32[]{:S(2)}, u32[]{:S(2)}) %collective-permute-start.21) | collective-permute-done | bytes 393248 | tf_op jit(solution)/shard_map/ppermute | solution.py:27
  211.1 3.5 %shard_map.79 = bf16[8,128,512]{2,1,0:T(8,128)(2,1)} custom-call(s32[32]{0:T(128)} %shard_map.76.s_ref, bf16[2,3,64,512]{3,2,1,0:T(8,128)(2,1)} %pad_maximum_fusion.1.refs_0_, bf16[2,3,64,512]{3,2,1,0:T(8,128)(2,1)} %copy-done.8, bf16[2,3,64,512]{3,2,1,0:T(8,128)(2,1)} %copy-done.6, bf16[2,3,64,512]{3,2,1,0:T(8,128)(2,1)} %copy-done.7, ...), custom_call_target="tpu_custom_call" | custom-call | tf_op jit(solution)/shard_map/pallas_call | solution.py:290
  (75 shorter events, 17.7 us)
Async XLA Ops:
  4.2 33.1 %collective-permute-start.2 = (bf16[5,2,32,2048]{3,2,1,0:T(8,128)(2,1)}, bf16[5,2,32,2048]{3,2,1,0:T(8,128)(2,1)}, u32[]{:S(2)}, u32[]{:S(2)}) collective-permute-start(bf16[5,2,32,2048]{3,2,1,0:T(8,128)(2,1)} %pad_maximum_fusion), channel_id=1, source_target_pairs={{8,0},{12,4},{16,8},{20,12},{24,16},{28,20},{0,24},{4,28},{9,1},{1... | collective-permute-start | bytes 3932168 | tf_op jit(solution)/shard_map/ppermute | solution.py:27
  8.9 31.2 %collective-permute-start = (bf16[1,2,32,2048]{3,2,1,0:T(8,128)(2,1)S(1)}, bf16[1,2,32,2048]{3,2,1,0:T(8,128)(2,1)S(1)}, u32[]{:S(2)}, u32[]{:S(2)}) collective-permute-start(bf16[1,2,32,2048]{3,2,1,0:T(8,128)(2,1)S(1)} %pad_maximum_fusion.6), channel_id=1, source_target_pairs={{8,0},{16,8},{24,16},{0,24},{9,1},{17,9},{25,17},{1,25},{10,2},{18... | collective-permute-start | bytes 786440 | tf_op jit(solution)/shard_map/ppermute | solution.py:32
  9.6 32.0 %collective-permute-start.1 = (bf16[1,2,32,2048]{3,2,1,0:T(8,128)(2,1)S(1)}, bf16[1,2,32,2048]{3,2,1,0:T(8,128)(2,1)S(1)}, u32[]{:S(2)}, u32[]{:S(2)}) collective-permute-start(bf16[1,2,32,2048]{3,2,1,0:T(8,128)(2,1)S(1)} %pad_maximum_fusion.7), channel_id=1, source_target_pairs={{8,0},{12,4},{16,8},{20,12},{24,16},{28,20},{0,24},{4,28},{9,1},{1... | collective-permute-start | bytes 786440 | tf_op jit(solution)/shard_map/ppermute | solution.py:27
  10.1 60.0 %collective-permute-start.8 = (bf16[192,2048]{1,0:T(8,128)(2,1)S(1)}, bf16[192,2048]{1,0:T(8,128)(2,1)}, u32[]{:S(2)}, u32[]{:S(2)}) collective-permute-start(bf16[192,2048]{1,0:T(8,128)(2,1)S(1)} %bitcast.35), channel_id=1, source_target_pairs={{0,2},{1,3},{2,0},{3,1},{4,6},{5,7},{6,4},{7,5},{8,10},{9,11},{10,... | collective-permute-start | bytes 2359304 | tf_op jit(solution)/shard_map/ppermute | solution.py:40
  11.7 58.5 %collective-permute-start.7 = (bf16[2,192,2048]{2,1,0:T(8,128)(2,1)S(1)}, bf16[2,192,2048]{2,1,0:T(8,128)(2,1)}, u32[]{:S(2)}, u32[]{:S(2)}) collective-permute-start(bf16[2,192,2048]{2,1,0:T(8,128)(2,1)S(1)} %bitcast.32), channel_id=1, source_target_pairs={{0,2},{1,3},{2,0},{3,1},{4,6},{5,7},{6,4},{7,5},{8,10},{9,11},{10,... | collective-permute-start | bytes 4718600 | tf_op jit(solution)/shard_map/ppermute | solution.py:40
  39.6 23.3 %collective-permute-start.10 = (bf16[3,2,32,2048]{3,2,1,0:T(8,128)(2,1)S(1)}, bf16[3,2,32,2048]{3,2,1,0:T(8,128)(2,1)}, u32[]{:S(2)}, u32[]{:S(2)}) collective-permute-start(bf16[3,2,32,2048]{3,2,1,0:T(8,128)(2,1)S(1)} %get-tuple-element.51), channel_id=1, source_target_pairs={{4,0},{8,4},{12,8},{16,12},{20,16},{24,20},{28,24},{0,28},{5,1},{9... | collective-permute-start | bytes 2359304 | tf_op jit(solution)/shard_map/ppermute | solution.py:27
  44.1 26.1 %collective-permute-start.9 = (bf16[3,2,32,2048]{3,2,1,0:T(8,128)(2,1)S(1)}, bf16[3,2,32,2048]{3,2,1,0:T(8,128)(2,1)}, u32[]{:S(2)}, u32[]{:S(2)}) collective-permute-start(bf16[3,2,32,2048]{3,2,1,0:T(8,128)(2,1)S(1)} %get-tuple-element.47.refs_2_), channel_id=1, source_target_pairs={{0,1},{1,0},{2,3},{3,2},{4,5},{5,4},{6,7},{7,6},{8,9},{9,8},{10,11... | collective-permute-start | bytes 2359304 | tf_op jit(solution)/shard_map/ppermute | solution.py:40
  62.9 7.3 %collective-permute-start.11 = (bf16[3,2,32,2048]{3,2,1,0:T(8,128)(2,1)}, bf16[3,2,32,2048]{3,2,1,0:T(8,128)(2,1)}, u32[]{:S(2)}, u32[]{:S(2)}) collective-permute-start(bf16[3,2,32,2048]{3,2,1,0:T(8,128)(2,1)} %collective-permute-done.10.refs_4_), channel_id=1, source_target_pairs={{0,1},{1,0},{2,3},{3,2},{4,5},{5,4},{6,7},{7,6},{8,9},{9,8},{10,11... | collective-permute-start | bytes 2359304 | tf_op jit(solution)/shard_map/ppermute | solution.py:40
  64.6 23.1 %collective-permute-start.5 = (bf16[3,2,32,2048]{3,2,1,0:T(8,128)(2,1)S(1)}, bf16[3,2,32,2048]{3,2,1,0:T(8,128)(2,1)S(1)}, u32[]{:S(2)}, u32[]{:S(2)}) collective-permute-start(bf16[3,2,32,2048]{3,2,1,0:T(8,128)(2,1)S(1)} %copy-done.5), channel_id=1, source_target_pairs={{8,0},{12,4},{16,8},{20,12},{24,16},{28,20},{0,24},{4,28},{9,1},{1... | collective-permute-start | bytes 2359304 | tf_op jit(solution)/shard_map/ppermute | solution.py:27
  70.2 19.7 %collective-permute-start.3 = (bf16[3,2,32,2048]{3,2,1,0:T(8,128)(2,1)S(1)}, bf16[3,2,32,2048]{3,2,1,0:T(8,128)(2,1)S(1)}, u32[]{:S(2)}, u32[]{:S(2)}) collective-permute-start(bf16[3,2,32,2048]{3,2,1,0:T(8,128)(2,1)S(1)} %copy-done.4), channel_id=1, source_target_pairs={{0,4},{4,0},{8,12},{12,8},{16,20},{20,16},{24,28},{28,24},{1,5},{5... | collective-permute-start | bytes 2359304 | tf_op jit(solution)/shard_map/ppermute | solution.py:36
  85.4 4.5 %collective-permute-start.12 = (bf16[2,576,512]{2,1,0:T(8,128)(2,1)S(1)}, bf16[2,576,512]{2,1,0:T(8,128)(2,1)S(1)}, u32[]{:S(2)}, u32[]{:S(2)}) collective-permute-start(bf16[2,576,512]{2,1,0:T(8,128)(2,1)S(1)} %get-tuple-element.27), channel_id=1, source_target_pairs={{0,1},{1,0},{2,3},{3,2},{4,5},{5,4},{6,7},{7,6},{8,9},{9,8},{10,11... | collective-permute-start | bytes 3538952 | tf_op jit(solution)/shard_map/ppermute | solution.py:40
  87.7 4.1 %collective-permute-start.6 = (bf16[3,2,32,2048]{3,2,1,0:T(8,128)(2,1)S(1)}, bf16[3,2,32,2048]{3,2,1,0:T(8,128)(2,1)S(1)}, u32[]{:S(2)}, u32[]{:S(2)}) collective-permute-start(bf16[3,2,32,2048]{3,2,1,0:T(8,128)(2,1)S(1)} %collective-permute-done.5.refs_2_), channel_id=1, source_target_pairs={{0,1},{1,0},{2,3},{3,2},{4,5},{5,4},{6,7},{7,6},{8,9},{9,8},{10,11... | collective-permute-start | bytes 2359304 | tf_op jit(solution)/shard_map/ppermute | solution.py:40
  89.9 2.3 %collective-permute-start.4 = (bf16[3,2,32,2048]{3,2,1,0:T(8,128)(2,1)S(1)}, bf16[3,2,32,2048]{3,2,1,0:T(8,128)(2,1)S(1)}, u32[]{:S(2)}, u32[]{:S(2)}) collective-permute-start(bf16[3,2,32,2048]{3,2,1,0:T(8,128)(2,1)S(1)} %collective-permute-done.3.refs_0_), channel_id=1, source_target_pairs={{0,1},{1,0},{2,3},{3,2},{4,5},{5,4},{6,7},{7,6},{8,9},{9,8},{10,11... | collective-permute-start | bytes 2359304 | tf_op jit(solution)/shard_map/ppermute | solution.py:40
  90.2 17.5 %collective-permute-start.15 = (bf16[3,3,64,512]{3,2,1,0:T(8,128)(2,1)S(1)}, bf16[3,3,64,512]{3,2,1,0:T(8,128)(2,1)S(1)}, u32[]{:S(2)}, u32[]{:S(2)}) collective-permute-start(bf16[3,3,64,512]{3,2,1,0:T(8,128)(2,1)S(1)} %bitcast.55), channel_id=1, source_target_pairs={{0,2},{1,3},{2,0},{3,1},{4,6},{5,7},{6,4},{7,5},{8,10},{9,11},{10,... | collective-permute-start | bytes 1769480 | tf_op jit(solution)/shard_map/ppermute | solution.py:40
  103.9 3.9 %collective-permute-start.16 = (bf16[2,384,512]{2,1,0:T(8,128)(2,1)S(1)}, bf16[2,384,512]{2,1,0:T(8,128)(2,1)S(1)}, u32[]{:S(2)}, u32[]{:S(2)}) collective-permute-start(bf16[2,384,512]{2,1,0:T(8,128)(2,1)S(1)} %get-tuple-element.35), channel_id=1, source_target_pairs={{0,1},{1,0},{2,3},{3,2},{4,5},{5,4},{6,7},{7,6},{8,9},{9,8},{10,11... | collective-permute-start | bytes 2359304 | tf_op jit(solution)/shard_map/ppermute | solution.py:40
  104.1 62.1 %collective-permute-start.13 = (bf16[192,2048]{1,0:T(8,128)(2,1)S(1)}, bf16[192,2048]{1,0:T(8,128)(2,1)S(1)}, u32[]{:S(2)}, u32[]{:S(2)}) collective-permute-start(bf16[192,2048]{1,0:T(8,128)(2,1)S(1)} %get-tuple-element.31), channel_id=1, source_target_pairs={{0,2},{1,3},{2,0},{3,1},{4,6},{5,7},{6,4},{7,5},{8,10},{9,11},{10,... | collective-permute-start | bytes 2359304 | tf_op jit(solution)/shard_map/ppermute | solution.py:40
  105.6 62.3 %collective-permute-start.14 = (bf16[192,2048]{1,0:T(8,128)(2,1)S(1)}, bf16[192,2048]{1,0:T(8,128)(2,1)S(1)}, u32[]{:S(2)}, u32[]{:S(2)}) collective-permute-start(bf16[192,2048]{1,0:T(8,128)(2,1)S(1)} %get-tuple-element.32), channel_id=1, source_target_pairs={{0,2},{1,3},{2,0},{3,1},{4,6},{5,7},{6,4},{7,5},{8,10},{9,11},{10,... | collective-permute-start | bytes 2359304 | tf_op jit(solution)/shard_map/ppermute | solution.py:40
  106.1 108.5 %collective-permute-start.22 = (bf16[192,2048]{1,0:T(8,128)(2,1)}, bf16[192,2048]{1,0:T(8,128)(2,1)S(1)}, u32[]{:S(2)}, u32[]{:S(2)}) collective-permute-start(bf16[192,2048]{1,0:T(8,128)(2,1)} %get-tuple-element.36), channel_id=1, source_target_pairs={{0,2},{1,3},{2,0},{3,1},{4,6},{5,7},{6,4},{7,5},{8,10},{9,11},{10,... | collective-permute-start | bytes 2359304 | tf_op jit(solution)/shard_map/ppermute | solution.py:40
  107.8 66.0 %collective-permute-start.19 = (bf16[2,3,64,512]{3,2,1,0:T(8,128)(2,1)S(1)}, bf16[2,3,64,512]{3,2,1,0:T(8,128)(2,1)S(1)}, u32[]{:S(2)}, u32[]{:S(2)}) collective-permute-start(bf16[2,3,64,512]{3,2,1,0:T(8,128)(2,1)S(1)} %pad_maximum_fusion.3), channel_id=1, source_target_pairs={{24,0},{28,4},{0,8},{4,12},{8,16},{12,20},{16,24},{20,28},{25,1},{... | collective-permute-start | bytes 1179656 | tf_op jit(solution)/shard_map/ppermute | solution.py:27
  108.1 58.0 %collective-permute-start.17 = (bf16[2,3,64,512]{3,2,1,0:T(8,128)(2,1)S(1)}, bf16[2,3,64,512]{3,2,1,0:T(8,128)(2,1)S(1)}, u32[]{:S(2)}, u32[]{:S(2)}) collective-permute-start(bf16[2,3,64,512]{3,2,1,0:T(8,128)(2,1)S(1)} %bitcast.56), channel_id=1, source_target_pairs={{0,2},{1,3},{2,0},{3,1},{4,6},{5,7},{6,4},{7,5},{8,10},{9,11},{10,... | collective-permute-start | bytes 1179656 | tf_op jit(solution)/shard_map/ppermute | solution.py:40
  166.0 14.8 %collective-permute-start.20 = (bf16[2,3,64,512]{3,2,1,0:T(8,128)(2,1)S(1)}, bf16[2,3,64,512]{3,2,1,0:T(8,128)(2,1)S(1)}, u32[]{:S(2)}, u32[]{:S(2)}) collective-permute-start(bf16[2,3,64,512]{3,2,1,0:T(8,128)(2,1)S(1)} %pad_maximum_fusion.4), channel_id=1, source_target_pairs={{20,0},{24,4},{28,8},{0,12},{4,16},{8,20},{12,24},{16,28},{21,1},{... | collective-permute-start | bytes 1179656 | tf_op jit(solution)/shard_map/ppermute | solution.py:27
  166.2 19.5 %collective-permute-start.18 = (bf16[2,3,64,512]{3,2,1,0:T(8,128)(2,1)S(1)}, bf16[2,3,64,512]{3,2,1,0:T(8,128)(2,1)S(1)}, u32[]{:S(2)}, u32[]{:S(2)}) collective-permute-start(bf16[2,3,64,512]{3,2,1,0:T(8,128)(2,1)S(1)} %pad_maximum_fusion.2), channel_id=1, source_target_pairs={{28,0},{0,4},{4,8},{8,12},{12,16},{16,20},{20,24},{24,28},{29,1},{... | collective-permute-start | bytes 1179656 | tf_op jit(solution)/shard_map/ppermute | solution.py:27
  167.9 43.2 %collective-permute-start.21 = (bf16[2,3,64,512]{3,2,1,0:T(8,128)(2,1)S(1)}, bf16[2,3,64,512]{3,2,1,0:T(8,128)(2,1)}, u32[]{:S(2)}, u32[]{:S(2)}) collective-permute-start(bf16[2,3,64,512]{3,2,1,0:T(8,128)(2,1)S(1)} %pad_maximum_fusion.5), channel_id=1, source_target_pairs={{16,0},{20,4},{24,8},{28,12},{0,16},{4,20},{8,24},{12,28},{17,1},{... | collective-permute-start | bytes 1179656 | tf_op jit(solution)/shard_map/ppermute | solution.py:27
  173.8 37.3 %copy-start.6 = (bf16[2,3,64,512]{3,2,1,0:T(8,128)(2,1)}, bf16[2,3,64,512]{3,2,1,0:T(8,128)(2,1)S(1)}, u32[]{:S(2)}) copy-start(bf16[2,3,64,512]{3,2,1,0:T(8,128)(2,1)S(1)} %collective-permute-done.19.refs_2_) | copy-start | bytes 1179652
  (9 other events, 122.8 us)

commit v5 on v4

--- a/solution.py
+++ b/solution.py
@@ -102,7 +102,7 @@
     return (((k % 2) * 2) | (1 - k // 2)) ^ own
 
 
-def expert_kernel(offsets, home, last, s_ref, *refs):
+def expert_kernel(offsets, home, last, far_half, s_ref, *refs):
     refs = list(refs)
     take = lambda n: [refs.pop(0) for _ in range(n)]
     n_away = len(offsets) - home
@@ -112,7 +112,7 @@
     add_in, add_out = take(2) if last else (None, None)
     if last:
         own_in, own_out, far_gate, far_up, far_out = take(5)
-    else:
+    elif not far_half:
         sum_in, sum_out = take(2)
     give, keep, w_ref, v_ref, sems, x_s, c_s, proj_s, hg_s, gu_s, gut_s, ht_s = refs
     step = pl.program_id(0)
@@ -124,6 +124,7 @@
     width = depth // PARTS
     units = v_ref.shape[0]
     fw = units // 2
+    side = own // 2 ^ 1 if far_half else own // 2
 
     @pl.when(step == 0)
     def _():
@@ -140,7 +141,7 @@
         def put(slot, t, at, x, c):
             size = x.shape[0]
             rows = pl.ds(pl.multiple_of((slot * MOST + t) * half + at, quarter), size)
-            ids = lax.broadcasted_iota(jnp.int32, (size, 1), 0) + (own // 2) * half + at
+            ids = lax.broadcasted_iota(jnp.int32, (size, 1), 0) + side * half + at
             live = ids < s_ref[LIM + offsets[slot] * MOST + t]
             x_s[rows, :] = x
             c_s[rows, :] = jnp.where(live, c, jnp.zeros((), BF16))
@@ -167,13 +168,15 @@
         up_rows = (hidden_grad * active).astype(BF16)
         gu_s[:, :units] = gate_rows
         gu_s[:, units:] = up_rows
-        gut_s[:units, :] = gate_rows.T
-        gut_s[units:, :] = up_rows.T
-        ht_s[...] = hidden.T
+        if not far_half:
+            gut_s[:units, :] = gate_rows.T
+            gut_s[units:, :] = up_rows.T
+            ht_s[...] = hidden.T
 
     cols = pl.ds(pl.multiple_of(column(step, own) * width, width), width)
-    new_in = matmul(gut_s[...], x_s[:, cols])
-    new_out = matmul(ht_s[...], c_s[:, cols])
+    if not far_half:
+        new_in = matmul(gut_s[...], x_s[:, cols])
+        new_out = matmul(ht_s[...], c_s[:, cols])
     if last:
         new_in += add_in[...]
         new_out += add_out[...]
@@ -183,7 +186,7 @@
         far_gate[...] = new_in[fw:units].astype(BF16)
         far_up[...] = new_in[units + fw :].astype(BF16)
         far_out[...] = new_out[fw:].astype(BF16)
-    else:
+    elif not far_half:
         sum_in[...] = new_in
         sum_out[...] = new_out
     row_grad = matmul(gu_s[...], w_ref[:, cols]).astype(BF16)
@@ -197,7 +200,7 @@
         keep[0] = row_grad
 
 
-def expert(table, offsets, home, pieces, shares, sums):
+def expert(table, offsets, home, pieces, shares, sums=None, far_half=False):
     last = sums is not None
     fw, depth = shares[1].shape
     units = 2 * fw
@@ -221,6 +224,8 @@
         specs += [chunk_in, chunk_out]
         shapes = [((2, fw, depth), F32), ((fw, depth), F32)] + [((fw, depth), BF16)] * 3
         outs = [own_in] + [own_out] * 4
+    elif far_half:
+        shapes, outs = [], []
     else:
         shapes = [((2 * units, depth), F32), ((units, depth), F32)]
         outs = [chunk_in, chunk_out]
@@ -230,7 +235,7 @@
         pl.BlockSpec((1, rows, width), lambda i, s: (jnp.maximum(i - 2, 0), 0, 0)),
     ]
     return pl.pallas_call(
-        functools.partial(expert_kernel, tuple(offsets), len(home) // 2, last),
+        functools.partial(expert_kernel, tuple(offsets), len(home) // 2, last, far_half),
         out_shape=[jax.ShapeDtypeStruct(*s) for s in shapes],
         grid_spec=pltpu.PrefetchScalarGridSpec(
             num_scalar_prefetch=1,
@@ -250,7 +255,7 @@
                 pltpu.VMEM((units, rows), BF16),
             ],
         ),
-        compiler_params=pltpu.CompilerParams(vmem_limit_bytes=28 * 2**20),
+        compiler_params=pltpu.CompilerParams(vmem_limit_bytes=25 * 2**20),
         cost_estimate=pl.CostEstimate(
             flops=16 * rows * units * depth,
             bytes_accessed=rows * depth * 6 + units * depth * (6 + (24 if last else 12)),
@@ -324,8 +329,11 @@
     one = ahead_even(my_one, 2)
     table = make_table(counts, n_dev, nblk)
     home = [
-        lax.dynamic_slice(a.reshape(nblk, 2, -1, depth), (0, own // 2, 0, 0), (MOST, 1, BLOCK // 2, depth))
-        for a in (x_rows, grad_rows)
+        [
+            lax.dynamic_slice(a.reshape(nblk, 2, -1, depth), (0, side, 0, 0), (MOST, 1, BLOCK // 2, depth))
+            for a in (x_rows, grad_rows)
+        ]
+        for side in (own // 2, 1 - own // 2)
     ]
     mine = quarter(1, nblk)
     mine = cut(mine, table[WIN + 1] - 1)
@@ -346,11 +354,11 @@
 
     shares = (w_in, w_out, o_in, o_out)
     pieces = [pair(second), pair(third)]
-    sum_in, sum_out, give, keep = expert(table, (0, 2, 3), home, pieces, shares, None)
-    here, there = add_cores(give, keep, 3)
-    sum_in, there = lax.optimization_barrier((sum_in, there))
+    sum_in, sum_out, give, keep = expert(table, (0, 2, 3), home[0], pieces, shares)
+    here_early, there = add_cores(give, keep, 3)
+    sum_in, there = lax.optimization_barrier((sum_in, there[1:]))
     there = swap_dp(there, 2)
-    r0, r2, r3 = add_rows(here, there)
+    r2, r3 = add_rows(here_early[1:], there)
     pieces = [pair(first), pair(fourth)]
     own_in, own_out, far_gate, far_up, far_out, give, keep = expert(table, (1, 4), (), pieces, shares, (sum_in, sum_out))
     far_gate = swap_dp(far_gate, 2)
@@ -359,6 +367,10 @@
     r1, r4 = add_rows(here, there)
     far_up = swap_dp(far_up, 2)
     far_out = swap_dp(far_out, 2)
+    give, keep = expert(table, (0,), home[1], [], shares, far_half=True)
+    got = swap_dp(give[0], 1)
+    other = (keep[0].astype(F32) + got.astype(F32)).astype(BF16).reshape(here_early[0].shape)
+    r0 = jnp.stack([here_early[0], other])
     r2, r3 = ahead(r2, -2), ahead(r3, -3)
     r1, r4 = ahead(r1, -1), ahead(r4, -4)
     done = merge(table, [r0, r1, r2, r3, r4], nblk)

time: 217 us -> 219 us (level)
  the two profiles are of different devices: /device:TPU:2 before, /device:TPU:27 now
where the time goes in v5:
time: 219 us
  waiting for transfers between devices  133 us (61%)
  Pallas kernels  37.3 us (17%)
  starting transfers between devices  20.7 us (9%)
  local copies, waits for them, and re-layouts  13 us (6%)
  other arithmetic  7.85 us (4%)
  between operations  6.74 us (3%)
    ppermute x8, waiting for transfers between devices, ahead(): lax.ppermute(array, 'blk', [((i + by) % size if moves(i) else i, i) for i...  78.1 us
    ppermute x14, waiting for transfers between devices, swap_dp(): lax.ppermute(array, 'dp', [(i, i ^ bit) for i in range(size_of('dp'))])  55.1 us
    pallas_call x3, Pallas kernels, expert(): pl.pallas_call(functools.partial(expert_kernel, tuple(offsets), len(home)...  32.5 us
    ppermute x14, starting transfers between devices, swap_dp(): lax.ppermute(array, 'dp', [(i, i ^ bit) for i in range(size_of('dp'))])  11.2 us
    ppermute x8, starting transfers between devices, ahead(): lax.ppermute(array, 'blk', [((i + by) % size if moves(i) else i, i) for i...  8.71 us
    dynamic_slice x4, local copies, waits for them, and re-layouts, pick(): lax.dynamic_slice(array, (first, own, 0, 0), (end - first, 1, part, depth))  5.01 us
  transfers between devices with their start and end apart: 24, of which 9 were waited for; matrix products, arithmetic and copies ran while one was open for 7% of the time, Pallas kernels for 17%

profile of v5, /device:TPU:27, one launch (start us, length us, event | category | flops | bytes accessed | tf_op | source)
XLA Modules:
  0.0 218.7 jit_solution(8928393306701953575)
XLA Ops:
  8.6 1.3 shard_map.76.s_ref
  9.9 1.5 fusion.7
  17.1 1.6 constant_dynamic-slice_fusion.10
  18.7 17.2 %collective-permute-done.2 = bf16[5,2,32,2048]{3,2,1,0:T(8,128)(2,1)} collective-permute-done((bf16[5,2,32,2048]{3,2,1,0:T(8,128)(2,1)}, bf16[5,2,32,2048]{3,2,1,0:T(8,128)(2,1)}, u32[]{:S(2)}, u32[]{:S(2)}) %collective-permute-start.2) | collective-permute-done | bytes 1310752 | tf_op jit(solution)/shard_map/ppermute | solution.py:27
  35.9 2.4 %constant_dynamic-slice_fusion.2 = (bf16[3,2,32,2048]{3,2,1,0:T(8,128)(2,1)S(1)}, bf16[3,2,32,2048]{3,2,1,0:T(8,128)(2,1)}) fusion(bf16[5,2,32,2048]{3,2,1,0:T(8,128)(2,1)} %collective-permute-done.2, s32[]{:T(128)S(6)} %select_n.52), kind=kLoop, calls=%fused_computation.26 | loop fusion | bytes 3145732 | tf_op jit(solution)/shard_map/dynamic_slice | solution.py:98
  38.6 2.8 %collective-permute-done.1 = bf16[1,2,32,2048]{3,2,1,0:T(8,128)(2,1)S(1)} collective-permute-done((bf16[1,2,32,2048]{3,2,1,0:T(8,128)(2,1)S(1)}, bf16[1,2,32,2048]{3,2,1,0:T(8,128)(2,1)S(1)}, u32[]{:S(2)}, u32[]{:S(2)}) %collective-permute-start.1) | collective-permute-done | bytes 262176 | tf_op jit(solution)/shard_map/ppermute | solution.py:27
  41.5 1.4 constant_dynamic-update-slice_fusion
  43.9 1.5 collective-permute-start.9
  45.4 18.6 %collective-permute-done.10.refs_4_ = bf16[3,2,32,2048]{3,2,1,0:T(8,128)(2,1)} collective-permute-done((bf16[3,2,32,2048]{3,2,1,0:T(8,128)(2,1)S(1)}, bf16[3,2,32,2048]{3,2,1,0:T(8,128)(2,1)}, u32[]{:S(2)}, u32[]{:S(2)}) %collective-permute-start.10) | collective-permute-done | bytes 786464 | tf_op jit(solution)/shard_map/ppermute | solution.py:27
  64.0 1.5 collective-permute-start.11
  65.5 2.4 %constant_dynamic-slice_fusion = (bf16[3,1,64,2048]{3,2,1,0:T(8,128)(2,1)S(1)}, bf16[3,1,64,2048]{3,2,1,0:T(8,128)(2,1)S(1)}, bf16[3,1,64,2048]{3,2,1,0:T(8,128)(2,1)S(1)}, bf16[3,1,64,2048]{3,2,1,0:T(8,128)(2,1)S(1)}) fusion(bf16[8,2,64,2048]{3,2,1,0:T(8,128)(2,1)} %bitcast.50, s32[]{:T(128)S(6)} %select_n.53, s32[]{:T(128)S(6)} %select_n.50, ...), kind=kLoop, calls=%fused_computation.24 | loop fusion | bytes 6291464 | tf_op jit(solution)/shard_map/dynamic_slice | solution.py:333
  68.3 15.1 %shard_map.77 = (f32[768,2048]{1,0:T(8,128)S(1)}, f32[384,2048]{1,0:T(8,128)S(1)}, bf16[2,576,512]{2,1,0:T(8,128)(2,1)S(1)}, bf16[2,576,512]{2,1,0:T(8,128)(2,1)S(1)}) custom-call(s32[32]{0:T(128)S(1)} %copy-done, bf16[3,1,64,2048]{3,2,1,0:T(8,128)(2,1)S(1)} %get-tuple-element.77.refs_0_, bf16[3,1,64,2048]{3,2,1,0:T(8,128)(2,1)S(1)} %get-tuple-element.46.refs_1_, ...), custom_call_target="tpu_custom_call" | custom-call | flops 7247757312 | bytes 21233664 | tf_op jit(solution)/shard_map/pallas_call | solution.py:237
  83.5 5.6 %shard_map.79 = (bf16[2,192,512]{2,1,0:T(8,128)(2,1)S(1)}, bf16[2,192,512]{2,1,0:T(8,128)(2,1)S(1)}) custom-call(s32[32]{0:T(128)S(1)} %copy-done, bf16[3,1,64,2048]{3,2,1,0:T(8,128)(2,1)S(1)} %get-tuple-element.78.refs_0_, bf16[3,1,64,2048]{3,2,1,0:T(8,128)(2,1)S(1)} %get-tuple-element.45.refs_1_, bf16[2,192,2048]{2,1,0:T(8,128)(2,1)S(1)} %bitcast.40, ...), custom_call_target="tpu_custom_call" | custom-call | flops 2415919104 | bytes 16515072 | tf_op jit(solution)/shard_map/pallas_call | solution.py:237
  90.5 2.7 %collective-permute-done.15 = bf16[192,512]{1,0:T(8,128)(2,1)S(1)} collective-permute-done((bf16[192,512]{1,0:T(8,128)(2,1)S(1)}, bf16[192,512]{1,0:T(8,128)(2,1)S(1)}, u32[]{:S(2)}, u32[]{:S(2)}) %collective-permute-start.15) | collective-permute-done | bytes 196640 | tf_op jit(solution)/shard_map/ppermute | solution.py:40
  94.8 11.7 %shard_map.78 = (f32[2,192,2048]{2,1,0:T(8,128)S(1)}, f32[192,2048]{1,0:T(8,128)S(1)}, bf16[192,2048]{1,0:T(8,128)(2,1)S(1)}, bf16[192,2048]{1,0:T(8,128)(2,1)S(...) custom-call(s32[32]{0:T(128)S(1)} %copy-done, ...), custom_call_target="tpu_custom_call" | custom-call | flops 4831838208 | bytes 28311552 | tf_op jit(solution)/shard_map/pallas_call | solution.py:237
  112.1 3.0 %collective-permute-start.20 = (bf16[2,3,64,512]{3,2,1,0:T(8,128)(2,1)S(1)}, bf16[2,3,64,512]{3,2,1,0:T(8,128)(2,1)S(1)}, u32[]{:S(2)}, u32[]{:S(2)}) collective-permute-start(bf16[2,3,64,512]{3,2,1,0:T(8,128)(2,1)S(1)} %pad_maximum_fusion.3), channel_id=1, source_target_pairs={{24,0},{28,4},{0,8},{4,12},{8,16},{12,20},{16,24},{20,28},{25,1},{... | collective-permute-start | bytes 1179656 | tf_op jit(solution)/shard_map/ppermute | solution.py:27
  115.2 52.0 %collective-permute-done.17 = bf16[2,3,64,512]{3,2,1,0:T(8,128)(2,1)S(1)} collective-permute-done((bf16[2,3,64,512]{3,2,1,0:T(8,128)(2,1)S(1)}, bf16[2,3,64,512]{3,2,1,0:T(8,128)(2,1)S(1)}, u32[]{:S(2)}, u32[]{:S(2)}) %collective-permute-start.17) | collective-permute-done | bytes 393248 | tf_op jit(solution)/shard_map/ppermute | solution.py:40
  167.3 4.8 %collective-permute-start.18 = (bf16[2,3,64,512]{3,2,1,0:T(8,128)(2,1)S(1)}, bf16[2,3,64,512]{3,2,1,0:T(8,128)(2,1)S(1)}, u32[]{:S(2)}, u32[]{:S(2)}) collective-permute-start(bf16[2,3,64,512]{3,2,1,0:T(8,128)(2,1)S(1)} %pad_maximum_fusion.2), channel_id=1, source_target_pairs={{28,0},{0,4},{4,8},{8,12},{12,16},{16,20},{20,24},{24,28},{29,1},{... | collective-permute-start | bytes 1179656 | tf_op jit(solution)/shard_map/ppermute | solution.py:27
  172.2 2.2 %convert_add_fusion = f32[2,192,2048]{2,1,0:T(8,128)} fusion(f32[2,192,2048]{2,1,0:T(8,128)S(1)} %get-tuple-element.32, bf16[1,192,2048]{2,1,0:T(8,128)(2,1)S(1)} %bitcast.63, bf16[1,192,2048]{2,1,0:T(8,128)(2,1)S(1)} %bitcast.62), kind=kLoop, calls=%fused_computation | loop fusion | flops 2359296 | bytes 7864320 | tf_op jit(solution)/shard_map/add | solution.py:377
  174.4 4.4 %collective-permute-done.21.refs_3_ = bf16[2,3,64,512]{3,2,1,0:T(8,128)(2,1)S(1)} collective-permute-done((bf16[2,3,64,512]{3,2,1,0:T(8,128)(2,1)S(1)}, bf16[2,3,64,512]{3,2,1,0:T(8,128)(2,1)S(1)}, u32[]{:S(2)}, u32[]{:S(2)}) %collective-permute-start.21) | collective-permute-done | bytes 393248 | tf_op jit(solution)/shard_map/ppermute | solution.py:27
  178.9 8.7 %collective-permute-done.18.refs_1_ = bf16[2,3,64,512]{3,2,1,0:T(8,128)(2,1)S(1)} collective-permute-done((bf16[2,3,64,512]{3,2,1,0:T(8,128)(2,1)S(1)}, bf16[2,3,64,512]{3,2,1,0:T(8,128)(2,1)S(1)}, u32[]{:S(2)}, u32[]{:S(2)}) %collective-permute-start.18) | collective-permute-done | bytes 393248 | tf_op jit(solution)/shard_map/ppermute | solution.py:27
  187.6 26.3 %collective-permute-done.22.refs_4_ = bf16[2,3,64,512]{3,2,1,0:T(8,128)(2,1)} collective-permute-done((bf16[2,3,64,512]{3,2,1,0:T(8,128)(2,1)S(1)}, bf16[2,3,64,512]{3,2,1,0:T(8,128)(2,1)}, u32[]{:S(2)}, u32[]{:S(2)}) %collective-permute-start.22) | collective-permute-done | bytes 393248 | tf_op jit(solution)/shard_map/ppermute | solution.py:27
  213.9 3.5 %shard_map.80 = bf16[8,128,512]{2,1,0:T(8,128)(2,1)} custom-call(s32[32]{0:T(128)} %shard_map.76.s_ref, bf16[2,3,64,512]{3,2,1,0:T(8,128)(2,1)} %pad_maximum_fusion.1.refs_0_, bf16[2,3,64,512]{3,2,1,0:T(8,128)(2,1)} %copy-done.8, bf16[2,3,64,512]{3,2,1,0:T(8,128)(2,1)} %copy-done.6, bf16[2,3,64,512]{3,2,1,0:T(8,128)(2,1)} %copy-done.7, ...), custom_call_target="tpu_custom_call" | custom-call | tf_op jit(solution)/shard_map/pallas_call | solution.py:295
  217.4 1.3 add_bitcast_fusion
  (83 shorter events, 18.2 us)
Async XLA Ops:
  4.2 31.8 %collective-permute-start.2 = (bf16[5,2,32,2048]{3,2,1,0:T(8,128)(2,1)}, bf16[5,2,32,2048]{3,2,1,0:T(8,128)(2,1)}, u32[]{:S(2)}, u32[]{:S(2)}) collective-permute-start(bf16[5,2,32,2048]{3,2,1,0:T(8,128)(2,1)} %pad_maximum_fusion), channel_id=1, source_target_pairs={{8,0},{12,4},{16,8},{20,12},{24,16},{28,20},{0,24},{4,28},{9,1},{1... | collective-permute-start | bytes 3932168 | tf_op jit(solution)/shard_map/ppermute | solution.py:27
  5.5 33.1 %collective-permute-start = (bf16[1,2,32,2048]{3,2,1,0:T(8,128)(2,1)S(1)}, bf16[1,2,32,2048]{3,2,1,0:T(8,128)(2,1)S(1)}, u32[]{:S(2)}, u32[]{:S(2)}) collective-permute-start(bf16[1,2,32,2048]{3,2,1,0:T(8,128)(2,1)S(1)} %pad_maximum_fusion.6), channel_id=1, source_target_pairs={{8,0},{16,8},{24,16},{0,24},{9,1},{17,9},{25,17},{1,25},{10,2},{18... | collective-permute-start | bytes 786440 | tf_op jit(solution)/shard_map/ppermute | solution.py:32
  6.2 35.2 %collective-permute-start.1 = (bf16[1,2,32,2048]{3,2,1,0:T(8,128)(2,1)S(1)}, bf16[1,2,32,2048]{3,2,1,0:T(8,128)(2,1)S(1)}, u32[]{:S(2)}, u32[]{:S(2)}) collective-permute-start(bf16[1,2,32,2048]{3,2,1,0:T(8,128)(2,1)S(1)} %pad_maximum_fusion.7), channel_id=1, source_target_pairs={{8,0},{12,4},{16,8},{20,12},{24,16},{28,20},{0,24},{4,28},{9,1},{1... | collective-permute-start | bytes 786440 | tf_op jit(solution)/shard_map/ppermute | solution.py:27
  6.4 61.7 %collective-permute-start.8 = (bf16[192,2048]{1,0:T(8,128)(2,1)S(1)}, bf16[192,2048]{1,0:T(8,128)(2,1)}, u32[]{:S(2)}, u32[]{:S(2)}) collective-permute-start(bf16[192,2048]{1,0:T(8,128)(2,1)S(1)} %bitcast.42), channel_id=1, source_target_pairs={{0,2},{1,3},{2,0},{3,1},{4,6},{5,7},{6,4},{7,5},{8,10},{9,11},{10,... | collective-permute-start | bytes 2359304 | tf_op jit(solution)/shard_map/ppermute | solution.py:40
  7.7 60.6 %collective-permute-start.7 = (bf16[2,192,2048]{2,1,0:T(8,128)(2,1)S(1)}, bf16[2,192,2048]{2,1,0:T(8,128)(2,1)}, u32[]{:S(2)}, u32[]{:S(2)}) collective-permute-start(bf16[2,192,2048]{2,1,0:T(8,128)(2,1)S(1)} %bitcast.38), channel_id=1, source_target_pairs={{0,2},{1,3},{2,0},{3,1},{4,6},{5,7},{6,4},{7,5},{8,10},{9,11},{10,... | collective-permute-start | bytes 4718600 | tf_op jit(solution)/shard_map/ppermute | solution.py:40
  38.3 25.7 %collective-permute-start.10 = (bf16[3,2,32,2048]{3,2,1,0:T(8,128)(2,1)S(1)}, bf16[3,2,32,2048]{3,2,1,0:T(8,128)(2,1)}, u32[]{:S(2)}, u32[]{:S(2)}) collective-permute-start(bf16[3,2,32,2048]{3,2,1,0:T(8,128)(2,1)S(1)} %get-tuple-element.57), channel_id=1, source_target_pairs={{4,0},{8,4},{12,8},{16,12},{20,16},{24,20},{28,24},{0,28},{5,1},{9... | collective-permute-start | bytes 2359304 | tf_op jit(solution)/shard_map/ppermute | solution.py:27
  43.9 24.4 %collective-permute-start.9 = (bf16[3,2,32,2048]{3,2,1,0:T(8,128)(2,1)S(1)}, bf16[3,2,32,2048]{3,2,1,0:T(8,128)(2,1)}, u32[]{:S(2)}, u32[]{:S(2)}) collective-permute-start(bf16[3,2,32,2048]{3,2,1,0:T(8,128)(2,1)S(1)} %get-tuple-element.53.refs_2_), channel_id=1, source_target_pairs={{0,1},{1,0},{2,3},{3,2},{4,5},{5,4},{6,7},{7,6},{8,9},{9,8},{10,11... | collective-permute-start | bytes 2359304 | tf_op jit(solution)/shard_map/ppermute | solution.py:40
  64.0 4.3 %collective-permute-start.11 = (bf16[3,2,32,2048]{3,2,1,0:T(8,128)(2,1)}, bf16[3,2,32,2048]{3,2,1,0:T(8,128)(2,1)}, u32[]{:S(2)}, u32[]{:S(2)}) collective-permute-start(bf16[3,2,32,2048]{3,2,1,0:T(8,128)(2,1)} %collective-permute-done.10.refs_4_), channel_id=1, source_target_pairs={{0,1},{1,0},{2,3},{3,2},{4,5},{5,4},{6,7},{7,6},{8,9},{9,8},{10,11... | collective-permute-start | bytes 2359304 | tf_op jit(solution)/shard_map/ppermute | solution.py:40
  67.9 21.2 %collective-permute-start.5 = (bf16[3,2,32,2048]{3,2,1,0:T(8,128)(2,1)S(1)}, bf16[3,2,32,2048]{3,2,1,0:T(8,128)(2,1)S(1)}, u32[]{:S(2)}, u32[]{:S(2)}) collective-permute-start(bf16[3,2,32,2048]{3,2,1,0:T(8,128)(2,1)S(1)} %copy-done.5), channel_id=1, source_target_pairs={{8,0},{12,4},{16,8},{20,12},{24,16},{28,20},{0,24},{4,28},{9,1},{1... | collective-permute-start | bytes 2359304 | tf_op jit(solution)/shard_map/ppermute | solution.py:27
  68.2 21.7 %collective-permute-start.3 = (bf16[3,2,32,2048]{3,2,1,0:T(8,128)(2,1)S(1)}, bf16[3,2,32,2048]{3,2,1,0:T(8,128)(2,1)S(1)}, u32[]{:S(2)}, u32[]{:S(2)}) collective-permute-start(bf16[3,2,32,2048]{3,2,1,0:T(8,128)(2,1)S(1)} %copy-done.4), channel_id=1, source_target_pairs={{0,4},{4,0},{8,12},{12,8},{16,20},{20,16},{24,28},{28,24},{1,5},{5... | collective-permute-start | bytes 2359304 | tf_op jit(solution)/shard_map/ppermute | solution.py:36
  83.4 9.9 %collective-permute-start.12 = (bf16[2,576,512]{2,1,0:T(8,128)(2,1)S(1)}, bf16[2,576,512]{2,1,0:T(8,128)(2,1)S(1)}, u32[]{:S(2)}, u32[]{:S(2)}) collective-permute-start(bf16[2,576,512]{2,1,0:T(8,128)(2,1)S(1)} %get-tuple-element.29), channel_id=1, source_target_pairs={{0,1},{1,0},{2,3},{3,2},{4,5},{5,4},{6,7},{7,6},{8,9},{9,8},{10,11... | collective-permute-start | bytes 3538952 | tf_op jit(solution)/shard_map/ppermute | solution.py:40
  89.1 5.7 %collective-permute-start.6 = (bf16[3,2,32,2048]{3,2,1,0:T(8,128)(2,1)S(1)}, bf16[3,2,32,2048]{3,2,1,0:T(8,128)(2,1)S(1)}, u32[]{:S(2)}, u32[]{:S(2)}) collective-permute-start(bf16[3,2,32,2048]{3,2,1,0:T(8,128)(2,1)S(1)} %collective-permute-done.5.refs_2_), channel_id=1, source_target_pairs={{0,1},{1,0},{2,3},{3,2},{4,5},{5,4},{6,7},{7,6},{8,9},{9,8},{10,11... | collective-permute-start | bytes 2359304 | tf_op jit(solution)/shard_map/ppermute | solution.py:40
  89.9 4.9 %collective-permute-start.4 = (bf16[3,2,32,2048]{3,2,1,0:T(8,128)(2,1)S(1)}, bf16[3,2,32,2048]{3,2,1,0:T(8,128)(2,1)S(1)}, u32[]{:S(2)}, u32[]{:S(2)}) collective-permute-start(bf16[3,2,32,2048]{3,2,1,0:T(8,128)(2,1)S(1)} %collective-permute-done.3.refs_0_), channel_id=1, source_target_pairs={{0,1},{1,0},{2,3},{3,2},{4,5},{5,4},{6,7},{7,6},{8,9},{9,8},{10,11... | collective-permute-start | bytes 2359304 | tf_op jit(solution)/shard_map/ppermute | solution.py:40
  89.9 3.3 %collective-permute-start.15 = (bf16[192,512]{1,0:T(8,128)(2,1)S(1)}, bf16[192,512]{1,0:T(8,128)(2,1)S(1)}, u32[]{:S(2)}, u32[]{:S(2)}) collective-permute-start(bf16[192,512]{1,0:T(8,128)(2,1)S(1)} %slice_bitcast_fusion), channel_id=1, source_target_pairs={{0,1},{1,0},{2,3},{3,2},{4,5},{5,4},{6,7},{7,6},{8,9},{9,8},{10,11... | collective-permute-start | bytes 589832 | tf_op jit(solution)/shard_map/ppermute | solution.py:40
  93.5 17.3 %collective-permute-start.19 = (bf16[2,3,64,512]{3,2,1,0:T(8,128)(2,1)S(1)}, bf16[2,3,64,512]{3,2,1,0:T(8,128)(2,1)S(1)}, u32[]{:S(2)}, u32[]{:S(2)}) collective-permute-start(bf16[2,3,64,512]{3,2,1,0:T(8,128)(2,1)S(1)} %bitcast.65), channel_id=1, source_target_pairs={{0,2},{1,3},{2,0},{3,1},{4,6},{5,7},{6,4},{7,5},{8,10},{9,11},{10,... | collective-permute-start | bytes 1179656 | tf_op jit(solution)/shard_map/ppermute | solution.py:40
  106.5 60.8 %collective-permute-start.13 = (bf16[192,2048]{1,0:T(8,128)(2,1)S(1)}, bf16[192,2048]{1,0:T(8,128)(2,1)S(1)}, u32[]{:S(2)}, u32[]{:S(2)}) collective-permute-start(bf16[192,2048]{1,0:T(8,128)(2,1)S(1)} %get-tuple-element.33), channel_id=1, source_target_pairs={{0,2},{1,3},{2,0},{3,1},{4,6},{5,7},{6,4},{7,5},{8,10},{9,11},{10,... | collective-permute-start | bytes 2359304 | tf_op jit(solution)/shard_map/ppermute | solution.py:40
  107.4 64.8 %collective-permute-start.14 = (bf16[192,2048]{1,0:T(8,128)(2,1)S(1)}, bf16[192,2048]{1,0:T(8,128)(2,1)S(1)}, u32[]{:S(2)}, u32[]{:S(2)}) collective-permute-start(bf16[192,2048]{1,0:T(8,128)(2,1)S(1)} %get-tuple-element.34), channel_id=1, source_target_pairs={{0,2},{1,3},{2,0},{3,1},{4,6},{5,7},{6,4},{7,5},{8,10},{9,11},{10,... | collective-permute-start | bytes 2359304 | tf_op jit(solution)/shard_map/ppermute | solution.py:40
  108.1 3.1 %collective-permute-start.16 = (bf16[2,384,512]{2,1,0:T(8,128)(2,1)S(1)}, bf16[2,384,512]{2,1,0:T(8,128)(2,1)S(1)}, u32[]{:S(2)}, u32[]{:S(2)}) collective-permute-start(bf16[2,384,512]{2,1,0:T(8,128)(2,1)S(1)} %get-tuple-element.38), channel_id=1, source_target_pairs={{0,1},{1,0},{2,3},{3,2},{4,5},{5,4},{6,7},{7,6},{8,9},{9,8},{10,11... | collective-permute-start | bytes 2359304 | tf_op jit(solution)/shard_map/ppermute | solution.py:40
  109.3 108.1 %collective-permute-start.23 = (bf16[192,2048]{1,0:T(8,128)(2,1)}, bf16[192,2048]{1,0:T(8,128)(2,1)S(1)}, u32[]{:S(2)}, u32[]{:S(2)}) collective-permute-start(bf16[192,2048]{1,0:T(8,128)(2,1)} %get-tuple-element.40), channel_id=1, source_target_pairs={{0,2},{1,3},{2,0},{3,1},{4,6},{5,7},{6,4},{7,5},{8,10},{9,11},{10,... | collective-permute-start | bytes 2359304 | tf_op jit(solution)/shard_map/ppermute | solution.py:40
  111.4 55.8 %collective-permute-start.17 = (bf16[2,3,64,512]{3,2,1,0:T(8,128)(2,1)S(1)}, bf16[2,3,64,512]{3,2,1,0:T(8,128)(2,1)S(1)}, u32[]{:S(2)}, u32[]{:S(2)}) collective-permute-start(bf16[2,3,64,512]{3,2,1,0:T(8,128)(2,1)S(1)} %bitcast.64), channel_id=1, source_target_pairs={{0,2},{1,3},{2,0},{3,1},{4,6},{5,7},{6,4},{7,5},{8,10},{9,11},{10,... | collective-permute-start | bytes 1179656 | tf_op jit(solution)/shard_map/ppermute | solution.py:40
  112.1 62.3 %collective-permute-start.20 = (bf16[2,3,64,512]{3,2,1,0:T(8,128)(2,1)S(1)}, bf16[2,3,64,512]{3,2,1,0:T(8,128)(2,1)S(1)}, u32[]{:S(2)}, u32[]{:S(2)}) collective-permute-start(bf16[2,3,64,512]{3,2,1,0:T(8,128)(2,1)S(1)} %pad_maximum_fusion.3), channel_id=1, source_target_pairs={{24,0},{28,4},{0,8},{4,12},{8,16},{12,20},{16,24},{20,28},{25,1},{... | collective-permute-start | bytes 1179656 | tf_op jit(solution)/shard_map/ppermute | solution.py:27
  167.2 11.7 %collective-permute-start.21 = (bf16[2,3,64,512]{3,2,1,0:T(8,128)(2,1)S(1)}, bf16[2,3,64,512]{3,2,1,0:T(8,128)(2,1)S(1)}, u32[]{:S(2)}, u32[]{:S(2)}) collective-permute-start(bf16[2,3,64,512]{3,2,1,0:T(8,128)(2,1)S(1)} %pad_maximum_fusion.4), channel_id=1, source_target_pairs={{20,0},{24,4},{28,8},{0,12},{4,16},{8,20},{12,24},{16,28},{21,1},{... | collective-permute-start | bytes 1179656 | tf_op jit(solution)/shard_map/ppermute | solution.py:27
  167.3 20.2 %collective-permute-start.18 = (bf16[2,3,64,512]{3,2,1,0:T(8,128)(2,1)S(1)}, bf16[2,3,64,512]{3,2,1,0:T(8,128)(2,1)S(1)}, u32[]{:S(2)}, u32[]{:S(2)}) collective-permute-start(bf16[2,3,64,512]{3,2,1,0:T(8,128)(2,1)S(1)} %pad_maximum_fusion.2), channel_id=1, source_target_pairs={{28,0},{0,4},{4,8},{8,12},{12,16},{16,20},{20,24},{24,28},{29,1},{... | collective-permute-start | bytes 1179656 | tf_op jit(solution)/shard_map/ppermute | solution.py:27
  172.2 41.7 %collective-permute-start.22 = (bf16[2,3,64,512]{3,2,1,0:T(8,128)(2,1)S(1)}, bf16[2,3,64,512]{3,2,1,0:T(8,128)(2,1)}, u32[]{:S(2)}, u32[]{:S(2)}) collective-permute-start(bf16[2,3,64,512]{3,2,1,0:T(8,128)(2,1)S(1)} %pad_maximum_fusion.5), channel_id=1, source_target_pairs={{16,0},{20,4},{24,8},{28,12},{0,16},{4,20},{8,24},{12,28},{17,1},{... | collective-permute-start | bytes 1179656 | tf_op jit(solution)/shard_map/ppermute | solution.py:27
  (10 other events, 123.4 us)

commit v6 on v4

--- a/solution.py
+++ b/solution.py
@@ -316,9 +316,10 @@
     def quarter(first, end):
         return jnp.concatenate([pick(x_rows, first, end), pick(grad_rows, first, end)], axis=1)
 
-    my_wide = quarter(MOST, nblk)
-    wide = ahead(my_wide, 2)
-    my_wide, counts, x_rows, grad_rows = lax.optimization_barrier((my_wide, counts, x_rows, grad_rows))
+    my_x, my_c = pick(x_rows, MOST, nblk), pick(grad_rows, MOST, nblk)
+    wide_x = ahead(my_x, 2)
+    wide_c = ahead(my_c, 2)
+    my_x, my_c, counts, x_rows, grad_rows = lax.optimization_barrier((my_x, my_c, counts, x_rows, grad_rows))
     my_two, my_one = quarter(2, MOST), quarter(1, 2)
     two = ahead(my_two, 2)
     one = ahead_even(my_one, 2)
@@ -332,11 +333,13 @@
     o_in = swap_dp(w_in, 2)
     o_out = swap_dp(w_out, 2)
 
-    third = cut(wide, table[WIN + SPAN + 3] - MOST)
-    fourth = wide[nblk - 2 * MOST :]
+    begin = table[WIN + SPAN + 3] - MOST
+    third_x, fourth_x = cut(wide_x, begin), wide_x[nblk - 2 * MOST :]
+    third = jnp.concatenate([third_x, cut(wide_c, begin)], axis=1)
+    fourth = jnp.concatenate([fourth_x, wide_c[nblk - 2 * MOST :]], axis=1)
     third = ahead(third, 1)
     fourth = ahead(fourth, 2)
-    there = jnp.concatenate([one, two, wide])
+    there = jnp.concatenate([one, two, jnp.concatenate([wide_x, wide_c], axis=1)])
     first = jnp.where(table[ODD] == 1, mine, cut(there, table[WIN + SPAN + 1] - 1))
     second = cut(there, table[WIN + SPAN + 2] - 1)
     first = swap_pair(first)

time: 217 us -> 215 us (level)
  the two profiles are of different devices: /device:TPU:2 before, /device:TPU:6 now
where the time goes in v6:
time: 215 us; the launch traced here: 214 us
  waiting for transfers between devices  131 us (61%)
  Pallas kernels  31.6 us (15%)
  starting transfers between devices  23.6 us (11%)
  local copies, waits for them, and re-layouts  12.1 us (6%)
  other arithmetic  9.74 us (5%)
  between operations  6.45 us (3%)
    ppermute x9, waiting for transfers between devices, ahead(): lax.ppermute(array, 'blk', [((i + by) % size if moves(i) else i, i) for i...  69.6 us
    ppermute x13, waiting for transfers between devices, swap_dp(): lax.ppermute(array, 'dp', [(i, i ^ bit) for i in range(size_of('dp'))])  59.1 us
    pallas_call x2, Pallas kernels, expert(): pl.pallas_call(functools.partial(expert_kernel, tuple(offsets), len(home)...  26.8 us
    ppermute x9, starting transfers between devices, ahead(): lax.ppermute(array, 'blk', [((i + by) % size if moves(i) else i, i) for i...  16.2 us
    dynamic_slice x4, local copies, waits for them, and re-layouts, pick(): lax.dynamic_slice(array, (first, own, 0, 0), (end - first, 1, part, depth))  6.68 us
    ppermute x13, starting transfers between devices, swap_dp(): lax.ppermute(array, 'dp', [(i, i ^ bit) for i in range(size_of('dp'))])  6.01 us
  transfers between devices with their start and end apart: 24, of which 10 were waited for; matrix products, arithmetic and copies ran while one was open for 9% of the time, Pallas kernels for 15%

profile of v6, /device:TPU:6, one launch (start us, length us, event | category | flops | bytes accessed | tf_op | source)
XLA Modules:
  0.0 214.5 jit_solution(13160449393046829329)
XLA Ops:
  0.6 2.0 constant_dynamic-slice_fusion.12
  2.6 3.6 %collective-permute-start.2 = (bf16[5,1,32,2048]{3,2,1,0:T(8,128)(2,1)}, bf16[5,1,32,2048]{3,2,1,0:T(8,128)(2,1)S(1)}, u32[]{:S(2)}, u32[]{:S(2)}) collective-permute-start(bf16[5,1,32,2048]{3,2,1,0:T(8,128)(2,1)} %constant_dynamic-slice_fusion.12), channel_id=1, source_target_pairs={{8,0},{12,4},{16,8},{20,12},{24,16},{28,20},{0,24},{4,28},{9,1},{1... | collective-permute-start | bytes 1966088 | tf_op jit(solution)/shard_map/ppermute | solution.py:27
  6.2 2.0 constant_dynamic-slice_fusion.11
  11.9 1.4 collective-permute-start
  15.9 1.5 fusion.6
  23.0 12.7 %collective-permute-done.3 = bf16[5,1,32,2048]{3,2,1,0:T(8,128)(2,1)} collective-permute-done((bf16[5,1,32,2048]{3,2,1,0:T(8,128)(2,1)}, bf16[5,1,32,2048]{3,2,1,0:T(8,128)(2,1)}, u32[]{:S(2)}, u32[]{:S(2)}) %collective-permute-start.3) | collective-permute-done | bytes 655392 | tf_op jit(solution)/shard_map/ppermute | solution.py:27
  38.9 1.6 constant_dynamic-slice_fusion.9
  40.5 1.4 maximum_maximum_fusion
  42.9 18.6 %collective-permute-done.11.refs_4_ = bf16[3,2,32,2048]{3,2,1,0:T(8,128)(2,1)} collective-permute-done((bf16[3,2,32,2048]{3,2,1,0:T(8,128)(2,1)S(1)}, bf16[3,2,32,2048]{3,2,1,0:T(8,128)(2,1)}, u32[]{:S(2)}, u32[]{:S(2)}) %collective-permute-start.11) | collective-permute-done | bytes 786464 | tf_op jit(solution)/shard_map/ppermute | solution.py:27
  61.5 1.6 constant_dynamic-slice_fusion.3
  63.3 5.5 %collective-permute-start.6 = (bf16[3,2,32,2048]{3,2,1,0:T(8,128)(2,1)S(1)}, bf16[3,2,32,2048]{3,2,1,0:T(8,128)(2,1)S(1)}, u32[]{:S(2)}, u32[]{:S(2)}) collective-permute-start(bf16[3,2,32,2048]{3,2,1,0:T(8,128)(2,1)S(1)} %pad_maximum_fusion), channel_id=1, source_target_pairs={{8,0},{12,4},{16,8},{20,12},{24,16},{28,20},{0,24},{4,28},{9,1},{1... | collective-permute-start | bytes 2359304 | tf_op jit(solution)/shard_map/ppermute | solution.py:27
  70.0 15.1 %shard_map.77 = (f32[768,2048]{1,0:T(8,128)S(1)}, f32[384,2048]{1,0:T(8,128)S(1)}, bf16[2,576,512]{2,1,0:T(8,128)(2,1)S(1)}, bf16[2,576,512]{2,1,0:T(8,128)(2,1)S(1)}) custom-call(s32[32]{0:T(128)S(1)} %copy-done, bf16[3,1,64,2048]{3,2,1,0:T(8,128)(2,1)S(1)} %get-tuple-element.75.refs_0_, bf16[3,1,64,2048]{3,2,1,0:T(8,128)(2,1)S(1)} %get-tuple-element.74.refs_1_, ...), custom_call_target="tpu_custom_call" | custom-call | flops 7247757312 | bytes 21233664 | tf_op jit(solution)/shard_map/pallas_call | solution.py:232
  86.2 2.2 %collective-permute-done.4.refs_0_ = bf16[3,2,32,2048]{3,2,1,0:T(8,128)(2,1)S(1)} collective-permute-done((bf16[3,2,32,2048]{3,2,1,0:T(8,128)(2,1)S(1)}, bf16[3,2,32,2048]{3,2,1,0:T(8,128)(2,1)S(1)}, u32[]{:S(2)}, u32[]{:S(2)}) %collective-permute-start.4) | collective-permute-done | bytes 786464 | tf_op jit(solution)/shard_map/ppermute | solution.py:36
  90.7 11.7 %shard_map.78 = (f32[2,192,2048]{2,1,0:T(8,128)S(1)}, f32[192,2048]{1,0:T(8,128)S(1)}, bf16[192,2048]{1,0:T(8,128)(2,1)S(1)}, bf16[192,2048]{1,0:T(8,128)(2,1)S(...) custom-call(s32[32]{0:T(128)S(1)} %copy-done, ...), custom_call_target="tpu_custom_call" | custom-call | flops 4831838208 | bytes 28311552 | tf_op jit(solution)/shard_map/pallas_call | solution.py:232
  103.1 1.5 collective-permute-start.15
  105.6 1.6 collective-permute-start.18
  108.0 56.5 %collective-permute-done.18 = bf16[2,3,64,512]{3,2,1,0:T(8,128)(2,1)S(1)} collective-permute-done((bf16[2,3,64,512]{3,2,1,0:T(8,128)(2,1)S(1)}, bf16[2,3,64,512]{3,2,1,0:T(8,128)(2,1)S(1)}, u32[]{:S(2)}, u32[]{:S(2)}) %collective-permute-start.18) | collective-permute-done | bytes 393248 | tf_op jit(solution)/shard_map/ppermute | solution.py:40
  165.7 1.5 collective-permute-start.19
  167.3 2.8 %collective-permute-start.22 = (bf16[2,3,64,512]{3,2,1,0:T(8,128)(2,1)S(1)}, bf16[2,3,64,512]{3,2,1,0:T(8,128)(2,1)}, u32[]{:S(2)}, u32[]{:S(2)}) collective-permute-start(bf16[2,3,64,512]{3,2,1,0:T(8,128)(2,1)S(1)} %pad_maximum_fusion.6), channel_id=1, source_target_pairs={{16,0},{20,4},{24,8},{28,12},{0,16},{4,20},{8,24},{12,28},{17,1},{... | collective-permute-start | bytes 1179656 | tf_op jit(solution)/shard_map/ppermute | solution.py:27
  170.0 2.3 %convert_add_fusion = f32[2,192,2048]{2,1,0:T(8,128)} fusion(f32[2,192,2048]{2,1,0:T(8,128)S(1)} %get-tuple-element.30, bf16[1,192,2048]{2,1,0:T(8,128)(2,1)S(1)} %bitcast.54, bf16[1,192,2048]{2,1,0:T(8,128)(2,1)S(1)} %bitcast.53), kind=kLoop, calls=%fused_computation | loop fusion | flops 2359296 | bytes 7864320 | tf_op jit(solution)/shard_map/add | solution.py:368
  172.3 7.0 %collective-permute-done.21.refs_3_ = bf16[2,3,64,512]{3,2,1,0:T(8,128)(2,1)S(1)} collective-permute-done((bf16[2,3,64,512]{3,2,1,0:T(8,128)(2,1)S(1)}, bf16[2,3,64,512]{3,2,1,0:T(8,128)(2,1)S(1)}, u32[]{:S(2)}, u32[]{:S(2)}) %collective-permute-start.21) | collective-permute-done | bytes 393248 | tf_op jit(solution)/shard_map/ppermute | solution.py:27
  179.3 5.9 %collective-permute-done.19.refs_1_ = bf16[2,3,64,512]{3,2,1,0:T(8,128)(2,1)S(1)} collective-permute-done((bf16[2,3,64,512]{3,2,1,0:T(8,128)(2,1)S(1)}, bf16[2,3,64,512]{3,2,1,0:T(8,128)(2,1)S(1)}, u32[]{:S(2)}, u32[]{:S(2)}) %collective-permute-start.19) | collective-permute-done | bytes 393248 | tf_op jit(solution)/shard_map/ppermute | solution.py:27
  185.2 24.4 %collective-permute-done.22.refs_4_ = bf16[2,3,64,512]{3,2,1,0:T(8,128)(2,1)} collective-permute-done((bf16[2,3,64,512]{3,2,1,0:T(8,128)(2,1)S(1)}, bf16[2,3,64,512]{3,2,1,0:T(8,128)(2,1)}, u32[]{:S(2)}, u32[]{:S(2)}) %collective-permute-start.22) | collective-permute-done | bytes 393248 | tf_op jit(solution)/shard_map/ppermute | solution.py:27
  209.7 3.5 %shard_map.79 = bf16[8,128,512]{2,1,0:T(8,128)(2,1)} custom-call(s32[32]{0:T(128)} %shard_map.76.s_ref, bf16[2,3,64,512]{3,2,1,0:T(8,128)(2,1)} %pad_maximum_fusion.2.refs_0_, bf16[2,3,64,512]{3,2,1,0:T(8,128)(2,1)} %copy-done.8, bf16[2,3,64,512]{3,2,1,0:T(8,128)(2,1)} %copy-done.6, bf16[2,3,64,512]{3,2,1,0:T(8,128)(2,1)} %copy-done.7, ...), custom_call_target="tpu_custom_call" | custom-call | tf_op jit(solution)/shard_map/pallas_call | solution.py:290
  (77 shorter events, 20.1 us)
Async XLA Ops:
  2.6 34.8 %collective-permute-start.2 = (bf16[5,1,32,2048]{3,2,1,0:T(8,128)(2,1)}, bf16[5,1,32,2048]{3,2,1,0:T(8,128)(2,1)S(1)}, u32[]{:S(2)}, u32[]{:S(2)}) collective-permute-start(bf16[5,1,32,2048]{3,2,1,0:T(8,128)(2,1)} %constant_dynamic-slice_fusion.12), channel_id=1, source_target_pairs={{8,0},{12,4},{16,8},{20,12},{24,16},{28,20},{0,24},{4,28},{9,1},{1... | collective-permute-start | bytes 1966088 | tf_op jit(solution)/shard_map/ppermute | solution.py:27
  8.2 27.5 %collective-permute-start.3 = (bf16[5,1,32,2048]{3,2,1,0:T(8,128)(2,1)}, bf16[5,1,32,2048]{3,2,1,0:T(8,128)(2,1)}, u32[]{:S(2)}, u32[]{:S(2)}) collective-permute-start(bf16[5,1,32,2048]{3,2,1,0:T(8,128)(2,1)} %constant_dynamic-slice_fusion.11), channel_id=1, source_target_pairs={{8,0},{12,4},{16,8},{20,12},{24,16},{28,20},{0,24},{4,28},{9,1},{1... | collective-permute-start | bytes 1966088 | tf_op jit(solution)/shard_map/ppermute | solution.py:27
  10.8 29.7 %collective-permute-start.1 = (bf16[1,2,32,2048]{3,2,1,0:T(8,128)(2,1)}, bf16[1,2,32,2048]{3,2,1,0:T(8,128)(2,1)}, u32[]{:S(2)}, u32[]{:S(2)}) collective-permute-start(bf16[1,2,32,2048]{3,2,1,0:T(8,128)(2,1)} %pad_maximum_fusion.8), channel_id=1, source_target_pairs={{8,0},{12,4},{16,8},{20,12},{24,16},{28,20},{0,24},{4,28},{9,1},{1... | collective-permute-start | bytes 786440 | tf_op jit(solution)/shard_map/ppermute | solution.py:27
  11.9 28.5 %collective-permute-start = (bf16[1,2,32,2048]{3,2,1,0:T(8,128)(2,1)}, bf16[1,2,32,2048]{3,2,1,0:T(8,128)(2,1)}, u32[]{:S(2)}, u32[]{:S(2)}) collective-permute-start(bf16[1,2,32,2048]{3,2,1,0:T(8,128)(2,1)} %pad_maximum_fusion.7), channel_id=1, source_target_pairs={{8,0},{16,8},{24,16},{0,24},{9,1},{17,9},{25,17},{1,25},{10,2},{18... | collective-permute-start | bytes 786440 | tf_op jit(solution)/shard_map/ppermute | solution.py:32
  13.3 55.4 %collective-permute-start.9 = (bf16[192,2048]{1,0:T(8,128)(2,1)S(1)}, bf16[192,2048]{1,0:T(8,128)(2,1)}, u32[]{:S(2)}, u32[]{:S(2)}) collective-permute-start(bf16[192,2048]{1,0:T(8,128)(2,1)S(1)} %bitcast.35), channel_id=1, source_target_pairs={{0,2},{1,3},{2,0},{3,1},{4,6},{5,7},{6,4},{7,5},{8,10},{9,11},{10,... | collective-permute-start | bytes 2359304 | tf_op jit(solution)/shard_map/ppermute | solution.py:40
  35.7 34.3 %collective-permute-start.8 = (bf16[2,192,2048]{2,1,0:T(8,128)(2,1)S(1)}, bf16[2,192,2048]{2,1,0:T(8,128)(2,1)}, u32[]{:S(2)}, u32[]{:S(2)}) collective-permute-start(bf16[2,192,2048]{2,1,0:T(8,128)(2,1)S(1)} %bitcast.32), channel_id=1, source_target_pairs={{0,2},{1,3},{2,0},{3,1},{4,6},{5,7},{6,4},{7,5},{8,10},{9,11},{10,... | collective-permute-start | bytes 4718600 | tf_op jit(solution)/shard_map/ppermute | solution.py:40
  38.3 23.2 %collective-permute-start.11 = (bf16[3,2,32,2048]{3,2,1,0:T(8,128)(2,1)S(1)}, bf16[3,2,32,2048]{3,2,1,0:T(8,128)(2,1)}, u32[]{:S(2)}, u32[]{:S(2)}) collective-permute-start(bf16[3,2,32,2048]{3,2,1,0:T(8,128)(2,1)S(1)} %pad_maximum_fusion.1), channel_id=1, source_target_pairs={{4,0},{8,4},{12,8},{16,12},{20,16},{24,20},{28,24},{0,28},{5,1},{9... | collective-permute-start | bytes 2359304 | tf_op jit(solution)/shard_map/ppermute | solution.py:27
  42.9 25.8 %collective-permute-start.10 = (bf16[3,2,32,2048]{3,2,1,0:T(8,128)(2,1)S(1)}, bf16[3,2,32,2048]{3,2,1,0:T(8,128)(2,1)}, u32[]{:S(2)}, u32[]{:S(2)}) collective-permute-start(bf16[3,2,32,2048]{3,2,1,0:T(8,128)(2,1)S(1)} %get-tuple-element.47.refs_2_), channel_id=1, source_target_pairs={{0,1},{1,0},{2,3},{3,2},{4,5},{5,4},{6,7},{7,6},{8,9},{9,8},{10,11... | collective-permute-start | bytes 2359304 | tf_op jit(solution)/shard_map/ppermute | solution.py:40
  61.5 8.5 %collective-permute-start.12 = (bf16[3,2,32,2048]{3,2,1,0:T(8,128)(2,1)}, bf16[3,2,32,2048]{3,2,1,0:T(8,128)(2,1)}, u32[]{:S(2)}, u32[]{:S(2)}) collective-permute-start(bf16[3,2,32,2048]{3,2,1,0:T(8,128)(2,1)} %collective-permute-done.11.refs_4_), channel_id=1, source_target_pairs={{0,1},{1,0},{2,3},{3,2},{4,5},{5,4},{6,7},{7,6},{8,9},{9,8},{10,11... | collective-permute-start | bytes 2359304 | tf_op jit(solution)/shard_map/ppermute | solution.py:40
  63.3 22.9 %collective-permute-start.6 = (bf16[3,2,32,2048]{3,2,1,0:T(8,128)(2,1)S(1)}, bf16[3,2,32,2048]{3,2,1,0:T(8,128)(2,1)S(1)}, u32[]{:S(2)}, u32[]{:S(2)}) collective-permute-start(bf16[3,2,32,2048]{3,2,1,0:T(8,128)(2,1)S(1)} %pad_maximum_fusion), channel_id=1, source_target_pairs={{8,0},{12,4},{16,8},{20,12},{24,16},{28,20},{0,24},{4,28},{9,1},{1... | collective-permute-start | bytes 2359304 | tf_op jit(solution)/shard_map/ppermute | solution.py:27
  68.7 19.7 %collective-permute-start.4 = (bf16[3,2,32,2048]{3,2,1,0:T(8,128)(2,1)S(1)}, bf16[3,2,32,2048]{3,2,1,0:T(8,128)(2,1)S(1)}, u32[]{:S(2)}, u32[]{:S(2)}) collective-permute-start(bf16[3,2,32,2048]{3,2,1,0:T(8,128)(2,1)S(1)} %copy-done.5), channel_id=1, source_target_pairs={{0,4},{4,0},{8,12},{12,8},{16,20},{20,16},{24,28},{28,24},{1,5},{5... | collective-permute-start | bytes 2359304 | tf_op jit(solution)/shard_map/ppermute | solution.py:36
  85.1 3.3 %collective-permute-start.13 = (bf16[2,576,512]{2,1,0:T(8,128)(2,1)S(1)}, bf16[2,576,512]{2,1,0:T(8,128)(2,1)S(1)}, u32[]{:S(2)}, u32[]{:S(2)}) collective-permute-start(bf16[2,576,512]{2,1,0:T(8,128)(2,1)S(1)} %get-tuple-element.27), channel_id=1, source_target_pairs={{0,1},{1,0},{2,3},{3,2},{4,5},{5,4},{6,7},{7,6},{8,9},{9,8},{10,11... | collective-permute-start | bytes 3538952 | tf_op jit(solution)/shard_map/ppermute | solution.py:40
  86.2 3.1 %collective-permute-start.7 = (bf16[3,2,32,2048]{3,2,1,0:T(8,128)(2,1)S(1)}, bf16[3,2,32,2048]{3,2,1,0:T(8,128)(2,1)S(1)}, u32[]{:S(2)}, u32[]{:S(2)}) collective-permute-start(bf16[3,2,32,2048]{3,2,1,0:T(8,128)(2,1)S(1)} %collective-permute-done.6.refs_2_), channel_id=1, source_target_pairs={{0,1},{1,0},{2,3},{3,2},{4,5},{5,4},{6,7},{7,6},{8,9},{9,8},{10,11... | collective-permute-start | bytes 2359304 | tf_op jit(solution)/shard_map/ppermute | solution.py:40
  88.4 2.3 %collective-permute-start.5 = (bf16[3,2,32,2048]{3,2,1,0:T(8,128)(2,1)S(1)}, bf16[3,2,32,2048]{3,2,1,0:T(8,128)(2,1)S(1)}, u32[]{:S(2)}, u32[]{:S(2)}) collective-permute-start(bf16[3,2,32,2048]{3,2,1,0:T(8,128)(2,1)S(1)} %collective-permute-done.4.refs_0_), channel_id=1, source_target_pairs={{0,1},{1,0},{2,3},{3,2},{4,5},{5,4},{6,7},{7,6},{8,9},{9,8},{10,11... | collective-permute-start | bytes 2359304 | tf_op jit(solution)/shard_map/ppermute | solution.py:40
  88.7 16.4 %collective-permute-start.16 = (bf16[3,3,64,512]{3,2,1,0:T(8,128)(2,1)S(1)}, bf16[3,3,64,512]{3,2,1,0:T(8,128)(2,1)S(1)}, u32[]{:S(2)}, u32[]{:S(2)}) collective-permute-start(bf16[3,3,64,512]{3,2,1,0:T(8,128)(2,1)S(1)} %bitcast.55), channel_id=1, source_target_pairs={{0,2},{1,3},{2,0},{3,1},{4,6},{5,7},{6,4},{7,5},{8,10},{9,11},{10,... | collective-permute-start | bytes 1769480 | tf_op jit(solution)/shard_map/ppermute | solution.py:40
  102.4 3.0 %collective-permute-start.17 = (bf16[2,384,512]{2,1,0:T(8,128)(2,1)S(1)}, bf16[2,384,512]{2,1,0:T(8,128)(2,1)S(1)}, u32[]{:S(2)}, u32[]{:S(2)}) collective-permute-start(bf16[2,384,512]{2,1,0:T(8,128)(2,1)S(1)} %get-tuple-element.35), channel_id=1, source_target_pairs={{0,1},{1,0},{2,3},{3,2},{4,5},{5,4},{6,7},{7,6},{8,9},{9,8},{10,11... | collective-permute-start | bytes 2359304 | tf_op jit(solution)/shard_map/ppermute | solution.py:40
  102.6 63.1 %collective-permute-start.14 = (bf16[192,2048]{1,0:T(8,128)(2,1)S(1)}, bf16[192,2048]{1,0:T(8,128)(2,1)S(1)}, u32[]{:S(2)}, u32[]{:S(2)}) collective-permute-start(bf16[192,2048]{1,0:T(8,128)(2,1)S(1)} %get-tuple-element.31), channel_id=1, source_target_pairs={{0,2},{1,3},{2,0},{3,1},{4,6},{5,7},{6,4},{7,5},{8,10},{9,11},{10,... | collective-permute-start | bytes 2359304 | tf_op jit(solution)/shard_map/ppermute | solution.py:40
  103.1 64.1 %collective-permute-start.15 = (bf16[192,2048]{1,0:T(8,128)(2,1)S(1)}, bf16[192,2048]{1,0:T(8,128)(2,1)S(1)}, u32[]{:S(2)}, u32[]{:S(2)}) collective-permute-start(bf16[192,2048]{1,0:T(8,128)(2,1)S(1)} %get-tuple-element.32), channel_id=1, source_target_pairs={{0,2},{1,3},{2,0},{3,1},{4,6},{5,7},{6,4},{7,5},{8,10},{9,11},{10,... | collective-permute-start | bytes 2359304 | tf_op jit(solution)/shard_map/ppermute | solution.py:40
  104.6 108.5 %collective-permute-start.23 = (bf16[192,2048]{1,0:T(8,128)(2,1)}, bf16[192,2048]{1,0:T(8,128)(2,1)S(1)}, u32[]{:S(2)}, u32[]{:S(2)}) collective-permute-start(bf16[192,2048]{1,0:T(8,128)(2,1)} %get-tuple-element.36), channel_id=1, source_target_pairs={{0,2},{1,3},{2,0},{3,1},{4,6},{5,7},{6,4},{7,5},{8,10},{9,11},{10,... | collective-permute-start | bytes 2359304 | tf_op jit(solution)/shard_map/ppermute | solution.py:40
  105.3 67.0 %collective-permute-start.20 = (bf16[2,3,64,512]{3,2,1,0:T(8,128)(2,1)S(1)}, bf16[2,3,64,512]{3,2,1,0:T(8,128)(2,1)S(1)}, u32[]{:S(2)}, u32[]{:S(2)}) collective-permute-start(bf16[2,3,64,512]{3,2,1,0:T(8,128)(2,1)S(1)} %pad_maximum_fusion.4), channel_id=1, source_target_pairs={{24,0},{28,4},{0,8},{4,12},{8,16},{12,20},{16,24},{20,28},{25,1},{... | collective-permute-start | bytes 1179656 | tf_op jit(solution)/shard_map/ppermute | solution.py:27
  105.6 59.0 %collective-permute-start.18 = (bf16[2,3,64,512]{3,2,1,0:T(8,128)(2,1)S(1)}, bf16[2,3,64,512]{3,2,1,0:T(8,128)(2,1)S(1)}, u32[]{:S(2)}, u32[]{:S(2)}) collective-permute-start(bf16[2,3,64,512]{3,2,1,0:T(8,128)(2,1)S(1)} %bitcast.56), channel_id=1, source_target_pairs={{0,2},{1,3},{2,0},{3,1},{4,6},{5,7},{6,4},{7,5},{8,10},{9,11},{10,... | collective-permute-start | bytes 1179656 | tf_op jit(solution)/shard_map/ppermute | solution.py:40
  164.5 14.8 %collective-permute-start.21 = (bf16[2,3,64,512]{3,2,1,0:T(8,128)(2,1)S(1)}, bf16[2,3,64,512]{3,2,1,0:T(8,128)(2,1)S(1)}, u32[]{:S(2)}, u32[]{:S(2)}) collective-permute-start(bf16[2,3,64,512]{3,2,1,0:T(8,128)(2,1)S(1)} %pad_maximum_fusion.5), channel_id=1, source_target_pairs={{20,0},{24,4},{28,8},{0,12},{4,16},{8,20},{12,24},{16,28},{21,1},{... | collective-permute-start | bytes 1179656 | tf_op jit(solution)/shard_map/ppermute | solution.py:27
  165.7 19.5 %collective-permute-start.19 = (bf16[2,3,64,512]{3,2,1,0:T(8,128)(2,1)S(1)}, bf16[2,3,64,512]{3,2,1,0:T(8,128)(2,1)S(1)}, u32[]{:S(2)}, u32[]{:S(2)}) collective-permute-start(bf16[2,3,64,512]{3,2,1,0:T(8,128)(2,1)S(1)} %pad_maximum_fusion.3), channel_id=1, source_target_pairs={{28,0},{0,4},{4,8},{8,12},{12,16},{16,20},{20,24},{24,28},{29,1},{... | collective-permute-start | bytes 1179656 | tf_op jit(solution)/shard_map/ppermute | solution.py:27
  167.3 42.4 %collective-permute-start.22 = (bf16[2,3,64,512]{3,2,1,0:T(8,128)(2,1)S(1)}, bf16[2,3,64,512]{3,2,1,0:T(8,128)(2,1)}, u32[]{:S(2)}, u32[]{:S(2)}) collective-permute-start(bf16[2,3,64,512]{3,2,1,0:T(8,128)(2,1)S(1)} %pad_maximum_fusion.6), channel_id=1, source_target_pairs={{16,0},{20,4},{24,8},{28,12},{0,16},{4,20},{8,24},{12,28},{17,1},{... | collective-permute-start | bytes 1179656 | tf_op jit(solution)/shard_map/ppermute | solution.py:27
  (10 other events, 170.0 us)
